TPU v7x, 512 devices: a whole 4x4x16 slice. The times are simulated.
512 devices in a mesh: tex: 64 (over x, z_lo, core), view: 8 (over y, z_hi).
Axes of the slice: x: 4, y: 4, z: 16 (z_hi: 2, z_lo: 8; z = z_hi * 8 + z_lo), core: 2. Of those that a mesh axis runs over, the one named last changes fastest.
Arguments:
- measured: bfloat16 [1536, 160, 151], P('tex', 'view'), may hold values from -6 to 6
- view_mask: int32 [160], P('view'), may hold values from 0 to 1, as said below
- tex_factor: float32 [1536, 256], P('tex'), may hold values from -6 to 6
- view_factor: float32 [160, 64], P('view'), as said below
- light_factor: bfloat16 [151, 64], replicated, as said below
- core_tensor: float32 [256, 64, 64], P('tex', 'view'), may hold values from -6 to 6
Outputs:
- tex_updated: float32 [1536, 256], P('tex')
- view_updated: float32 [160, 64], P('view')
- core_updated: float32 [256, 64, 64], P('tex', 'view')
Inputs may be any that keep to these rules, and one draw needn't show every extreme that they name: `view_mask`: exactly 151 of the 160 entries are 1. `view_factor`: entries of order one. `light_factor`: entries of order one.
All inputs are finite; a program needn't handle non-finite values.
Results may differ from a plain program's by a relative error of at most 0.014.
Values may be sent and summed in bfloat16 or wider, within the bound.
No kernel may reach another device: no remote copies, remote signals or barrier semaphores. Data moves between devices by JAX's collectives and lax.ppermute only.
A program may use at most 64 MiB of HBM per device.

v0:
```python
import jax
import jax.numpy as jnp
from jax import lax
from jax.sharding import PartitionSpec as P

RT = 256
RV = 64
RL = 64
VALID = 151
L = 151


def per_device(measured, view_mask, tex_factor, view_factor, light_factor, core_tensor):
    tex_count = lax.axis_size("tex")
    view_count = lax.axis_size("view")
    tex_rows = measured.shape[0]
    texels_all = tex_rows * tex_count
    band_width = RV // view_count
    band_start = lax.axis_index("view") * band_width
    scaling = (RT * RV * RL) ** (-0.5)
    rate_tex = RT / (VALID * L)
    rate_view = RV / (texels_all * L)
    rate_core = RT * RV * RL / (texels_all * VALID * L)
    weights = view_mask.astype(jnp.float32)[None, :, None]
    tex_now = tex_factor
    view_now = view_factor
    core_now = core_tensor
    tex_bf = tex_now.astype(jnp.bfloat16)
    view_bf = view_now.astype(jnp.bfloat16)
    core_bf = core_now.astype(jnp.bfloat16)
    core_band = lax.all_gather(core_bf, "view", axis=1, tiled=True)
    core_whole = lax.all_gather(core_band, "tex", axis=0, tiled=True)
    core_flat = core_whole.reshape(RT, RV * RL)
    projected = jnp.dot(tex_bf, core_flat, preferred_element_type=jnp.float32).astype(jnp.bfloat16)
    projected = projected.reshape(tex_rows, RV, RL)
    mixed = jnp.einsum(
        "vb,tbc->tvc", view_bf, projected, preferred_element_type=jnp.float32
    ).astype(jnp.bfloat16)
    approx = jnp.einsum("tvc,lc->tvl", mixed, light_factor, preferred_element_type=jnp.float32)
    resid = (weights * (scaling * approx - measured.astype(jnp.float32))).astype(jnp.bfloat16)
    back = jnp.einsum(
        "tvl,lc->tvc", resid, light_factor, preferred_element_type=jnp.float32
    ).astype(jnp.bfloat16)
    view_part = scaling * jnp.einsum(
        "tvc,tbc->vb", back, projected, preferred_element_type=jnp.float32
    )
    grad_view = lax.psum(view_part, "tex")
    partial_y = jnp.einsum("vb,tvc->tbc", view_bf, back, preferred_element_type=jnp.float32)
    summed = lax.psum(partial_y.astype(jnp.bfloat16), "view")
    grad_tex = scaling * lax.dot_general(
        summed.reshape(tex_rows, RV * RL),
        core_flat,
        (((1,), (1,)), ((), ())),
        preferred_element_type=jnp.float32,
    )
    summed_bf = lax.dynamic_slice_in_dim(summed, band_start, band_width, 1)
    flat_y = summed_bf.reshape(tex_rows, band_width * RL)
    grad_core = lax.psum_scatter(
        scaling
        * lax.dot_general(
            tex_bf, flat_y, (((0,), (0,)), ((), ())), preferred_element_type=jnp.float32
        ),
        "tex",
        scatter_dimension=0,
        tiled=True,
    )
    tex_now = tex_now - rate_tex * grad_tex
    view_now = view_now - rate_view * grad_view
    core_now = core_now - rate_core * grad_core.reshape(core_now.shape)
    return (tex_now, view_now, core_now)


def solution(mesh):
    return jax.shard_map(
        per_device,
        mesh=mesh,
        in_specs=(
            P("tex", "view", None),
            P("view"),
            P("tex", None),
            P("view", None),
            P(),
            P("tex", "view", None),
        ),
        out_specs=(P("tex", None), P("view", None), P("tex", "view", None)),
        check_vma=False,
    )
```

profile of v0, /device:TPU:1, one launch (start us, length us, event | category | flops | bytes accessed | tf_op | source)
XLA Modules:
  0.0 1214.5 jit_solution(1821549432471933966)
XLA Ops:
  7.2 0.0 all-gather.2.cloned.1.call-start
  7.2 0.7 copy.41
  8.0 61.5 %all_gather.6 = bf16[4,64,64]{2,0,1:T(4,128)(2,1)S(1)} all-gather(bf16[4,8,64]{2,0,1:T(4,128)(2,1)S(1)} %copy.41), channel_id=1, replica_groups=mesh['tex'=64,'view'=8] {'view'}, dimensions={1}, use_global_device_ids=true | all-gather | bytes 36864 | tf_op jit(solution)/shard_map/all_gather | solution.py:31
  69.5 0.6 copy.22
  70.1 0.0 all-gather.2.cloned.1.call-update
  70.1 0.0 all-reduce.4.cloned.1.call-start
  70.2 0.7 convert_element_type.36
  70.9 129.2 %all-gather.2.cloned.1.call-done = bf16[256,64,64]{2,1,0:T(8,128)(2,1)} async-done(((bf16[4,64,64]{2,1,0:T(8,128)(2,1)}), bf16[256,64,64]{2,1,0:T(8,128)(2,1)}) %all-gather.2.cloned.1.call-update) | async-done | bytes 2097168 | tf_op jit(solution)/shard_map/all_gather | solution.py:32
  200.0 4.9 copy.23
  205.0 0.6 convolution_convert_fusion
  205.6 0.4 reshape.21
  206.1 0.2 fusion.7
  206.3 0.4 fusion.6
  206.6 1.1 fusion.3
  207.7 0.0 all-reduce.4.cloned.1.call-update
  207.7 0.0 all-reduce.6.cloned.1.call-start
  207.8 1.3 dynamic-slice
  209.7 162.2 %all-reduce.4.cloned.1.call-done = bf16[24,64,64]{1,2,0:T(8,128)(2,1)} async-done(((bf16[24,64,64]{1,2,0:T(8,128)(2,1)}), bf16[24,64,64]{1,2,0:T(8,128)(2,1)}) %all-reduce.4.cloned.1.call-update) | async-done | bytes 196624 | tf_op jit(solution)/shard_map/psum | solution.py:49
  371.9 1.2 constant_dynamic-slice_fusion
  373.2 0.2 copy.29
  373.3 0.1 reshape.22
  373.4 1.1 fusion
  374.5 0.0 all-reduce.6.cloned.1.call-update
  374.5 0.2 fusion.10
  374.7 417.5 %psum.15 = f32[20,64]{1,0:T(8,128)S(1)} all-reduce(f32[20,64]{1,0:T(8,128)S(1)} %fusion.10), channel_id=1, replica_groups=mesh['tex'=64,'view'=8] {'tex'}, use_global_device_ids=true, to_apply=%region_1.0 | all-reduce | flops 1280 | bytes 10240 | tf_op jit(solution)/shard_map/psum | solution.py:47
  792.3 0.6 multiply_subtract_fusion
  792.9 0.2 copy.26
  793.1 1.1 fusion.9
  794.2 411.9 %all-reduce.6.cloned.1.call-done = f32[256,512]{0,1:T(8,128)} async-done(((f32[256,512]{0,1:T(8,128)}), f32[256,512]{0,1:T(8,128)}) %all-reduce.6.cloned.1.call-update) | async-done | bytes 524304
  1206.2 1.1 dynamic-slice_multiply_fusion
  1207.2 0.1 copy.30
  1207.4 0.6 sub.15
  (12 shorter events, 0.0 us)
Async XLA Ops:
  7.2 199.1 %copy-start = (bf16[151,64]{0,1:T(8,128)(2,1)S(1)}, bf16[151,64]{0,1:T(8,128)(2,1)}, u32[]{:S(2)}) copy-start(bf16[151,64]{0,1:T(8,128)(2,1)} %param.10) | copy-start | bytes 57988
  7.2 192.9 %all-gather.2.cloned.1.call-start = ((), (), s32[]{:S(2)}) async-start(), calls=%async_computation | async-start | bytes 4259840 | tf_op jit(solution)/shard_map/all_gather | solution.py:32
  70.1 301.8 %all-reduce.4.cloned.1.call-start = ((), (), s32[]{:S(2)}) async-start(), calls=%async_computation.1 | async-start | bytes 786432 | tf_op jit(solution)/shard_map/psum | solution.py:49
  70.9 134.1 %copy-start.2 = (f32[24,256]{1,0:T(8,128)S(1)}, f32[24,256]{1,0:T(8,128)}, u32[]{:S(2)}) copy-start(f32[24,256]{1,0:T(8,128)} %param.8) | copy-start | bytes 73732
  205.0 1.1 copy-start.3
  205.0 1.3 copy-start.5
  207.7 998.4 %all-reduce.6.cloned.1.call-start = ((), (), s32[]{:S(2)}) async-start(), calls=%async_computation.2 | async-start | bytes 1048576
  371.9 421.0 %copy-start.1 = (bf16[24,64,64]{1,2,0:T(8,128)(2,1)S(1)}, bf16[24,64,64]{1,2,0:T(8,128)(2,1)}, u32[]{:S(2)}) copy-start(bf16[24,64,64]{1,2,0:T(8,128)(2,1)} %all-reduce.4.cloned.1.call-done) | copy-start | bytes 589828
  374.7 832.6 %copy-start.4 = (f32[4,8,64]{2,1,0:T(8,128)S(1)}, f32[4,8,64]{2,1,0:T(8,128)}, u32[]{:S(2)}) copy-start(f32[4,8,64]{2,1,0:T(8,128)} %param.11) | copy-start | bytes 24580
Sparse Core Ops, SparseCore 0:
  70.3 129.7 all-gather.1
  207.8 164.0 all-reduce.3
  374.8 831.2 all-reduce.5
where the time goes:
time: 1210 us
  waiting for transfers between devices  703 us (58%)
  blocking collectives  479 us (40%)
  between operations  14.5 us (1%)
    psum x1, blocking collectives, per_device(): grad_view = lax.psum(view_part, 'tex')  418 us
    unnamed x4, waiting for transfers between devices  412 us
    psum x1, waiting for transfers between devices, per_device(): summed = lax.psum(partial_y.astype(jnp.bfloat16), 'view')  162 us
    all_gather x1, waiting for transfers between devices, per_device(): core_whole = lax.all_gather(core_band, 'tex', axis=0, tiled=True)  129 us
    all_gather x1, blocking collectives, per_device(): core_band = lax.all_gather(core_bf, 'view', axis=1, tiled=True)  61.5 us
  transfers between devices with their start and end apart: 3, of which 3 were waited for; matrix products, arithmetic and copies ran while one was open for 0% of the time, Pallas kernels for 0%

commit v1 on v0

v1 whole, which is shorter than its diff:
```python
import jax
import jax.numpy as jnp
from jax import lax
from jax.sharding import PartitionSpec as P

RT = 256
RV = 64
RL = 64
VALID = 151
L = 151

F32 = jnp.float32
BF16 = jnp.bfloat16


def gather_blocks(x, axis):
    count = lax.axis_size(axis)
    return lax.all_to_all(
        jnp.broadcast_to(x[None], (count,) + x.shape), axis, 0, 0, tiled=True
    )


def sum_blocks(x):
    return jnp.sum(x.astype(F32), axis=0)


def per_device(measured, view_mask, tex_factor, view_factor, light_factor, core_tensor):
    tex_count = lax.axis_size("tex")
    view_count = lax.axis_size("view")
    tex_rows, views = measured.shape[:2]
    core_rows, band = core_tensor.shape[:2]
    width = band * RL
    texels_all = tex_rows * tex_count
    scaling = (RT * RV * RL) ** (-0.5)
    rate_tex = RT / (VALID * L)
    rate_view = RV / (texels_all * L)
    rate_core = RT * RV * RL / (texels_all * VALID * L)
    weights = view_mask.astype(F32)[:, None, None]
    tex_bf = tex_factor.astype(BF16)
    view_bf = view_factor.astype(BF16)
    core_bf = core_tensor.astype(BF16).reshape(core_rows, width)

    core_band = gather_blocks(core_bf, "tex").reshape(RT, width)
    proj_band = jnp.dot(tex_bf, core_band, preferred_element_type=F32).astype(BF16)
    projected = gather_blocks(proj_band, "view")
    projected = projected.reshape(view_count, tex_rows, band, RL)
    view_bands = view_bf.reshape(views, view_count, band)

    mixed = jnp.einsum(
        "vgb,gtbc->vtc", view_bands, projected, preferred_element_type=F32
    ).astype(BF16)
    approx = jnp.einsum("vtc,lc->vtl", mixed, light_factor, preferred_element_type=F32)
    target = jnp.transpose(measured, (1, 0, 2)).astype(F32)
    resid = (weights * (scaling * approx - target)).astype(BF16)
    back = jnp.einsum("vtl,lc->vtc", resid, light_factor, preferred_element_type=F32).astype(BF16)

    partial_y = jnp.einsum("vgb,vtc->gtbc", view_bands, back, preferred_element_type=F32)
    partial_y = partial_y.astype(BF16).reshape(view_count, tex_rows, width)
    summed = sum_blocks(lax.all_to_all(partial_y, "view", 0, 0, tiled=True)).astype(BF16)

    tex_part = lax.dot_general(
        summed, core_band, (((1,), (1,)), ((), ())), preferred_element_type=F32
    )
    grad_tex = scaling * sum_blocks(gather_blocks(tex_part.astype(BF16), "view"))

    view_part = jnp.einsum("vtc,gtbc->vgb", back, projected, preferred_element_type=F32)
    core_part = lax.dot_general(
        tex_bf, summed, (((0,), (0,)), ((), ())), preferred_element_type=F32
    )
    core_part = core_part.astype(BF16).reshape(tex_count, core_rows * width)
    view_part = view_part.astype(BF16).reshape(1, views * RV)
    view_part = jnp.broadcast_to(view_part, (tex_count, views * RV))
    both = jnp.concatenate([core_part, view_part], axis=1)
    both = sum_blocks(lax.all_to_all(both, "tex", 0, 0, tiled=True))
    grad_core = scaling * both[: core_rows * width].reshape(core_tensor.shape)
    grad_view = scaling * both[core_rows * width :].reshape(view_factor.shape)

    return (
        tex_factor - rate_tex * grad_tex,
        view_factor - rate_view * grad_view,
        core_tensor - rate_core * grad_core,
    )


def solution(mesh):
    return jax.shard_map(
        per_device,
        mesh=mesh,
        in_specs=(
            P("tex", "view", None),
            P("view"),
            P("tex", None),
            P("view", None),
            P(),
            P("tex", "view", None),
        ),
        out_specs=(P("tex", None), P("view", None), P("tex", "view", None)),
        check_vma=False,
    )
```

time: 1210 us -> 150 us (0.12)
  waiting for transfers between devices: 703 us -> 64.9 us
  blocking collectives: 479 us -> 36 us
  starting transfers between devices: 0.12 us -> 34.4 us
  between operations: 14.5 us -> 0.83 us
    psum x1 -> x0, blocking collectives: 418 us -> none  [per_device(): grad_view = lax.psum(view_part, 'tex')]
    unnamed x4 -> x0, waiting for transfers between devices: 412 us -> none
    psum x1 -> x0, waiting for transfers between devices: 162 us -> none  [per_device(): summed = lax.psum(partial_y.astype(jnp.bfloat16), 'view')]
    all_gather x1 -> x0, waiting for transfers between devices: 129 us -> none  [per_device(): core_whole = lax.all_gather(core_band, 'tex', axis=0, tiled=True)]
    all_to_all x0 -> x4, waiting for transfers between devices: none -> 64.9 us  [the longest x2 25.9 us: gather_blocks(): lax.all_to_all(jnp.broadcast_to(x[None], (count,) + x.shape), axis, 0, 0,...]
    all_gather x1 -> x0, blocking collectives: 61.5 us -> none  [per_device(): core_band = lax.all_gather(core_bf, 'view', axis=1, tiled=True)]
    all_to_all x0 -> x1, blocking collectives: none -> 36 us  [gather_blocks(): lax.all_to_all(jnp.broadcast_to(x[None], (count,) + x.shape), axis, 0, 0,...]
    all_to_all x0 -> x4, starting transfers between devices: none -> 34.4 us  [the longest x1 17.6 us: per_device(): both = sum_blocks(lax.all_to_all(both, 'tex', 0, 0, tiled=True))]
  transfers between devices with their start and end apart: 3 -> 4, of which waited for: 3 -> 4; matrix products, arithmetic and copies ran while one was open for 0% -> 3% of each run, Pallas kernels for 0% -> 0%
where the time goes in v1:
time: 150 us; the launch traced here: 149 us
  waiting for transfers between devices  64.9 us (43%)
  blocking collectives  36 us (24%)
  starting transfers between devices  34.4 us (23%)
  local copies, waits for them, and re-layouts  7.32 us (5%)
  other arithmetic  4.38 us (3%)
  matrix products  1.69 us (1%)
    all_to_all x1, blocking collectives, gather_blocks(): lax.all_to_all(jnp.broadcast_to(x[None], (count,) + x.shape), axis, 0, 0,...  36 us
    all_to_all x2, waiting for transfers between devices, gather_blocks(): lax.all_to_all(jnp.broadcast_to(x[None], (count,) + x.shape), axis, 0, 0,...  25.9 us
    all_to_all x1, waiting for transfers between devices, per_device(): both = sum_blocks(lax.all_to_all(both, 'tex', 0, 0, tiled=True))  25 us
    all_to_all x1, starting transfers between devices, per_device(): both = sum_blocks(lax.all_to_all(both, 'tex', 0, 0, tiled=True))  17.6 us
    all_to_all x1, waiting for transfers between devices, per_device(): lax.all_to_all(partial_y, 'view', 0, 0, tiled=True)  14 us
    all_to_all x2, starting transfers between devices, gather_blocks(): lax.all_to_all(jnp.broadcast_to(x[None], (count,) + x.shape), axis, 0, 0,...  13.4 us
    all_to_all x1, starting transfers between devices, per_device(): lax.all_to_all(partial_y, 'view', 0, 0, tiled=True)  3.39 us
    unnamed x15, local copies, waits for them, and re-layouts  3.32 us
  transfers between devices with their start and end apart: 4, of which 4 were waited for; matrix products, arithmetic and copies ran while one was open for 3% of the time, Pallas kernels for 0%

profile of v1, /device:TPU:1, one launch (start us, length us, event | category | flops | bytes accessed | tf_op | source)
XLA Modules:
  0.0 149.5 jit_solution(8895970560929331329)
XLA Ops:
  0.6 0.7 convert_element_type.62
  1.5 36.0 %all_to_all.29 = bf16[64,4,512]{2,1,0:T(4,128)(2,1)S(1)} all-to-all(bf16[64,4,512]{2,1,0:T(4,128)(2,1)S(1)} %broadcast_in_dim.13), channel_id=1, replica_groups=mesh['tex'=64,'view'=8] {'tex'}, dimensions={0} | all-to-all | bytes 524288 | tf_op jit(solution)/shard_map/all_to_all | solution.py:18
  37.6 0.7 copy-done.1
  38.4 0.7 broadcast_in_dim.14
  39.1 10.1 %all-to-all-start.1 = ((bf16[8,24,512]{2,1,0:T(8,128)(2,1)}), bf16[8,24,512]{2,1,0:T(8,128)(2,1)S(1)}, u32[]{:S(2)}, u32[]{:S(2)}) async-start(bf16[8,24,512]{2,1,0:T(8,128)(2,1)} %broadcast_in_dim.14), calls=%async_computation.1 | async-start | bytes 393216 | tf_op jit(solution)/shard_map/all_to_all | solution.py:18
  49.3 14.5 %all-to-all-done.1 = bf16[8,24,512]{2,1,0:T(8,128)(2,1)S(1)} async-done(((bf16[8,24,512]{2,1,0:T(8,128)(2,1)}), bf16[8,24,512]{2,1,0:T(8,128)(2,1)S(1)}, u32[]{:S(2)}, u32[]{:S(2)}) %all-to-all-start.1) | async-done | bytes 196640 | tf_op jit(solution)/shard_map/all_to_all | solution.py:18
  63.8 0.2 reshape.45
  64.1 0.2 fusion.8
  64.3 0.7 copy-done.4
  65.0 0.4 fusion.7
  65.4 0.2 fusion.2
  65.6 0.3 reshape.47
  65.9 0.7 copy.28
  66.6 3.4 %all-to-all-start.2 = ((bf16[8,24,512]{2,1,0:T(8,128)(2,1)}), bf16[8,24,512]{2,1,0:T(8,128)(2,1)S(1)}, u32[]{:S(2)}, u32[]{:S(2)}) async-start(bf16[8,24,512]{2,1,0:T(8,128)(2,1)} %copy.28), calls=%async_computation.2 | async-start | bytes 393216 | tf_op jit(solution)/shard_map/all_to_all | solution.py:59
  70.0 0.3 fusion.9
  70.5 14.0 %all-to-all-done.2 = bf16[8,24,512]{2,1,0:T(8,128)(2,1)S(1)} async-done(((bf16[8,24,512]{2,1,0:T(8,128)(2,1)}), bf16[8,24,512]{2,1,0:T(8,128)(2,1)S(1)}, u32[]{:S(2)}, u32[]{:S(2)}) %all-to-all-start.2) | async-done | bytes 196640 | tf_op jit(solution)/shard_map/all_to_all | solution.py:59
  84.7 0.3 fusion.4
  85.0 0.7 broadcast_in_dim.30
  85.7 3.4 %all-to-all-start.3 = ((bf16[8,24,256]{2,1,0:T(8,128)(2,1)}), bf16[8,24,256]{2,1,0:T(8,128)(2,1)S(1)}, u32[]{:S(2)}, u32[]{:S(2)}) async-start(bf16[8,24,256]{2,1,0:T(8,128)(2,1)} %broadcast_in_dim.30), calls=%async_computation.3 | async-start | bytes 196608 | tf_op jit(solution)/shard_map/all_to_all | solution.py:18
  89.2 0.2 reshape.48
  89.5 0.5 broadcast.12
  90.0 0.9 reduce.2
  90.9 0.9 reshape.56
  91.7 11.4 %all-to-all-done.3 = bf16[8,24,256]{2,1,0:T(8,128)(2,1)S(1)} async-done(((bf16[8,24,256]{2,1,0:T(8,128)(2,1)}), bf16[8,24,256]{2,1,0:T(8,128)(2,1)S(1)}, u32[]{:S(2)}, u32[]{:S(2)}) %all-to-all-start.3) | async-done | bytes 98336 | tf_op jit(solution)/shard_map/all_to_all | solution.py:18
  103.1 17.6 %all-to-all-start.4 = ((bf16[64,2,1664]{2,1,0:T(2,128)(2,1)}), bf16[64,2,1664]{2,1,0:T(2,128)(2,1)S(1)}, u32[]{:S(2)}, u32[]{:S(2)}) async-start(bf16[64,2,1664]{2,1,0:T(2,128)(2,1)} %reshape.56), calls=%async_computation.4 | async-start | bytes 851968 | tf_op jit(solution)/shard_map/all_to_all | solution.py:74
  120.7 0.6 multiply_subtract_fusion
  121.3 25.0 %all-to-all-done.4 = bf16[64,2,1664]{2,1,0:T(2,128)(2,1)S(1)} async-done(((bf16[64,2,1664]{2,1,0:T(2,128)(2,1)}), bf16[64,2,1664]{2,1,0:T(2,128)(2,1)S(1)}, u32[]{:S(2)}, u32[]{:S(2)}) %all-to-all-start.4) | async-done | bytes 426016 | tf_op jit(solution)/shard_map/all_to_all | solution.py:74
  146.3 0.3 reshape.57
  146.7 0.8 convert_reduce_fusion
  147.6 0.6 sub.14
  148.2 0.6 copy-done.2
  148.9 0.6 sub.15
  (27 shorter events, 1.3 us)
Async XLA Ops:
  0.6 63.7 %copy-start = (bf16[151,64]{0,1:T(8,128)(2,1)S(1)}, bf16[151,64]{0,1:T(8,128)(2,1)}, u32[]{:S(2)}) copy-start(bf16[151,64]{0,1:T(8,128)(2,1)} %param.10) | copy-start | bytes 57988
  37.5 0.7 copy-start.1
  39.1 10.1 %copy-start.5 = (s32[20]{0:T(128)S(1)}, s32[20]{0:T(128)}, u32[]{:S(2)}) copy-start(s32[20]{0:T(128)} %param.7) | copy-start | bytes 244
  39.1 10.1 %copy-start.3 = (f32[20,64]{1,0:T(8,128)S(1)}, f32[20,64]{1,0:T(8,128)}, u32[]{:S(2)}) copy-start(f32[20,64]{1,0:T(8,128)} %param.9) | copy-start | bytes 15364
  39.1 24.7 %all-to-all-start.1 = ((bf16[8,24,512]{2,1,0:T(8,128)(2,1)}), bf16[8,24,512]{2,1,0:T(8,128)(2,1)S(1)}, u32[]{:S(2)}, u32[]{:S(2)}) async-start(bf16[8,24,512]{2,1,0:T(8,128)(2,1)} %broadcast_in_dim.14), calls=%async_computation.1 | async-start | bytes 393216 | tf_op jit(solution)/shard_map/all_to_all | solution.py:18
  64.0 0.9 copy-start.4
  66.6 17.9 %all-to-all-start.2 = ((bf16[8,24,512]{2,1,0:T(8,128)(2,1)}), bf16[8,24,512]{2,1,0:T(8,128)(2,1)S(1)}, u32[]{:S(2)}, u32[]{:S(2)}) async-start(bf16[8,24,512]{2,1,0:T(8,128)(2,1)} %copy.28), calls=%async_computation.2 | async-start | bytes 393216 | tf_op jit(solution)/shard_map/all_to_all | solution.py:59
  85.7 17.4 %all-to-all-start.3 = ((bf16[8,24,256]{2,1,0:T(8,128)(2,1)}), bf16[8,24,256]{2,1,0:T(8,128)(2,1)S(1)}, u32[]{:S(2)}, u32[]{:S(2)}) async-start(bf16[8,24,256]{2,1,0:T(8,128)(2,1)} %broadcast_in_dim.30), calls=%async_computation.3 | async-start | bytes 196608 | tf_op jit(solution)/shard_map/all_to_all | solution.py:18
  103.1 43.2 %all-to-all-start.4 = ((bf16[64,2,1664]{2,1,0:T(2,128)(2,1)}), bf16[64,2,1664]{2,1,0:T(2,128)(2,1)S(1)}, u32[]{:S(2)}, u32[]{:S(2)}) async-start(bf16[64,2,1664]{2,1,0:T(2,128)(2,1)} %reshape.56), calls=%async_computation.4 | async-start | bytes 851968 | tf_op jit(solution)/shard_map/all_to_all | solution.py:74
  148.2 0.7 copy-start.2

commit v2 on v1

v2 whole, which is shorter than its diff:
```python
import jax
import jax.numpy as jnp
from jax import lax
from jax.sharding import Mesh, PartitionSpec as P

RT = 256
RV = 64
RL = 64
VALID = 151
L = 151

F32 = jnp.float32
BF16 = jnp.bfloat16

SIZES = (4, 8, 2, 4, 2)
NAMES = ("x", "zl", "c", "y", "zh")
TEX = ("x", "zl", "c")
VIEW = ("y", "zh")


def exchange(x, axes):
    return lax.all_to_all(x, axes, 0, 0, tiled=True)


def gather_blocks(x, axes):
    count = lax.axis_size(axes)
    return exchange(jnp.broadcast_to(x[None], (count,) + x.shape), axes)


def sum_blocks(x):
    return jnp.sum(x.astype(F32), axis=0)


def column_order():
    i = lax.broadcasted_iota(jnp.int32, (RT, RT), 0)
    j = lax.broadcasted_iota(jnp.int32, (RT, RT), 1)
    target = (i // 64) * 64 + ((i // 4) % 2) * 32 + ((i // 8) % 8) * 4 + i % 4
    return (target == j).astype(BF16)


def per_device(measured, view_mask, tex_factor, view_factor, light_factor, core_tensor):
    tex_count = lax.axis_size(TEX)
    tex_rows, views = measured.shape[:2]
    core_rows, band = core_tensor.shape[:2]
    width = band * RL
    texels_all = tex_rows * tex_count
    scaling = (RT * RV * RL) ** (-0.5)
    rate_tex = RT / (VALID * L)
    rate_view = RV / (texels_all * L)
    rate_core = RT * RV * RL / (texels_all * VALID * L)
    nx, nzl, nc, ny, nzh = SIZES
    bands = ny * nzh
    near = nzl * core_rows
    weights = view_mask.astype(F32)[:, None, None]
    order = column_order()
    tex_bf = jnp.dot(tex_factor.astype(BF16), order, preferred_element_type=F32).astype(BF16)
    view_bands = view_factor.astype(BF16).reshape(views, bands, band)
    core_bf = core_tensor.astype(BF16).reshape(core_rows, width)

    core_z = gather_blocks(core_bf, ("zh", "zl")).reshape(nzh, near, width)
    core_xc = gather_blocks(core_z, ("x", "c"))
    core_pair = jnp.transpose(core_xc, (1, 0, 2, 3)).reshape(nzh, RT, width)
    proj_pair = jnp.einsum("ta,zan->ztn", tex_bf, core_pair, preferred_element_type=F32)
    projected = gather_blocks(proj_pair.astype(BF16), ("y",))
    projected = projected.reshape(bands, tex_rows, band, RL)

    mixed = jnp.einsum(
        "vgb,gtbc->vtc", view_bands, projected, preferred_element_type=F32
    ).astype(BF16)
    approx = jnp.einsum("vtc,lc->vtl", mixed, light_factor, preferred_element_type=F32)
    target = jnp.transpose(measured, (1, 0, 2)).astype(F32)
    resid = (weights * (scaling * approx - target)).astype(BF16)
    back = jnp.einsum("vtl,lc->vtc", resid, light_factor, preferred_element_type=F32).astype(BF16)

    partial_y = jnp.einsum("vgb,vtc->gtbc", view_bands, back, preferred_element_type=F32)
    partial_y = partial_y.astype(BF16).reshape(ny, 1, nzh, tex_rows, width)
    partial_y = jnp.broadcast_to(partial_y, (ny, nzh, nzh, tex_rows, width))
    partial_y = partial_y.reshape(bands, nzh, tex_rows, width)
    summed = sum_blocks(exchange(partial_y, VIEW)).astype(BF16)
    view_part = jnp.einsum("vtc,gtbc->vgb", back, projected, preferred_element_type=F32)

    tex_part = jnp.einsum("ztn,zan->ta", summed, core_pair, preferred_element_type=F32)
    tex_part = lax.dot_general(
        tex_part.astype(BF16), order, (((1,), (1,)), ((), ())), preferred_element_type=F32
    )
    tex_blocks = gather_blocks(tex_part.astype(BF16), ("y",))
    grad_tex = scaling * sum_blocks(tex_blocks)

    own = jnp.where(lax.axis_index("zh") == 0, summed[0], summed[1])
    core_part = jnp.einsum("ta,tn->an", tex_bf, own, preferred_element_type=F32)
    core_part = core_part.astype(BF16).reshape(nx * nc, near, width)
    spare = core_rows * width - views * RV
    view_part = jnp.pad(view_part.astype(BF16).reshape(views * RV), (0, spare))
    view_part = view_part.reshape(core_rows, width)
    view_block = jnp.broadcast_to(view_part[None], (nx * nc, core_rows, width))
    both = exchange(jnp.concatenate([core_part, view_block], axis=1), ("x", "c"))
    both = sum_blocks(both).astype(BF16)
    core_part = both[:near].reshape(nzl, core_rows, width)
    view_block = jnp.broadcast_to(both[None, near:], (nzl, core_rows, width))
    both = exchange(jnp.concatenate([core_part, view_block], axis=1), ("zl",))
    both = scaling * sum_blocks(both)
    grad_core = both[:core_rows].reshape(core_tensor.shape)
    grad_view = both[core_rows:].reshape(core_rows * width)[: views * RV]

    return (
        tex_factor - rate_tex * grad_tex,
        view_factor - rate_view * grad_view.reshape(view_factor.shape),
        core_tensor - rate_core * grad_core,
    )


def solution(mesh):
    parts = Mesh(mesh.devices.reshape(SIZES), NAMES)
    return jax.shard_map(
        per_device,
        mesh=parts,
        in_specs=(
            P(TEX, VIEW, None),
            P(VIEW),
            P(TEX, None),
            P(VIEW, None),
            P(),
            P(TEX, VIEW, None),
        ),
        out_specs=(P(TEX, None), P(VIEW, None), P(TEX, VIEW, None)),
        check_vma=False,
    )
```

time: 150 us -> 135 us (0.900)
  blocking collectives: 36 us -> 0 us
  starting transfers between devices: 34.4 us -> 59.5 us
  waiting for transfers between devices: 64.9 us -> 59.1 us
    all_to_all x1 -> x0, blocking collectives: 36 us -> none  [gather_blocks(): lax.all_to_all(jnp.broadcast_to(x[None], (count,) + x.shape), axis, 0, 0,...]
    all_to_all x4 -> x7, starting transfers between devices: 34.4 us -> 59.5 us  [exchange(): return lax.all_to_all(x, axes, 0, 0, tiled=True)]
    all_to_all x4 -> x7, waiting for transfers between devices: 64.9 us -> 59.1 us  [exchange(): return lax.all_to_all(x, axes, 0, 0, tiled=True)]
    broadcast_in_dim x5 -> x12, local copies, waits for them, and re-layouts: 1.63 us -> 4.03 us  [the longest x6 2.93 us: gather_blocks(): return exchange(jnp.broadcast_to(x[None], (count,) + x.shape), axes)]
    unnamed x15 -> x13, local copies, waits for them, and re-layouts: 3.32 us -> 2.15 us
  transfers between devices with their start and end apart: 4 -> 7, of which waited for: 4 -> 7; matrix products, arithmetic and copies ran while one was open for 3% -> 2% of each run, Pallas kernels for 0% -> 0%
where the time goes in v2:
time: 135 us; the launch traced here: 133 us
  starting transfers between devices  59.5 us (44%)
  waiting for transfers between devices  59.1 us (44%)
  local copies, waits for them, and re-layouts  6.89 us (5%)
  other arithmetic  4.13 us (3%)
  matrix products  2.7 us (2%)
    all_to_all x7, starting transfers between devices, exchange(): return lax.all_to_all(x, axes, 0, 0, tiled=True)  59.5 us
    all_to_all x7, waiting for transfers between devices, exchange(): return lax.all_to_all(x, axes, 0, 0, tiled=True)  59.1 us
    broadcast_in_dim x6, local copies, waits for them, and re-layouts, gather_blocks(): return exchange(jnp.broadcast_to(x[None], (count,) + x.shape), axes)  2.93 us
  transfers between devices with their start and end apart: 7, of which 7 were waited for; matrix products, arithmetic and copies ran while one was open for 2% of the time, Pallas kernels for 0%

profile of v2, /device:TPU:1, one launch (start us, length us, event | category | flops | bytes accessed | tf_op | source)
XLA Modules:
  0.0 133.2 jit_solution(4071513372938943642)
XLA Ops:
  0.6 0.7 convert_element_type.74
  1.5 0.6 broadcast_in_dim.23
  2.1 15.7 %all-to-all-start = ((bf16[16,4,512]{2,1,0:T(4,128)(2,1)}), bf16[16,4,512]{2,1,0:T(4,128)(2,1)S(1)}, u32[]{:S(2)}, u32[]{:S(2)}) async-start(bf16[16,4,512]{2,1,0:T(4,128)(2,1)} %broadcast_in_dim.23), calls=%async_computation | async-start | bytes 131072 | tf_op jit(solution)/shard_map/all_to_all | solution.py:22
  17.9 11.5 %all-to-all-done = bf16[16,4,512]{2,1,0:T(4,128)(2,1)S(1)} async-done(((bf16[16,4,512]{2,1,0:T(4,128)(2,1)}), bf16[16,4,512]{2,1,0:T(4,128)(2,1)S(1)}, u32[]{:S(2)}, u32[]{:S(2)}) %all-to-all-start) | async-done | bytes 65568 | tf_op jit(solution)/shard_map/all_to_all | solution.py:22
  29.4 0.8 broadcast_in_dim.50
  30.3 6.4 %all-to-all-start.1 = ((bf16[8,2,32,512]{3,2,1,0:T(8,128)(2,1)}), bf16[8,2,32,512]{3,2,1,0:T(8,128)(2,1)S(1)}, u32[]{:S(2)}, u32[]{:S(2)}) async-start(bf16[8,2,32,512]{3,2,1,0:T(8,128)(2,1)} %broadcast_in_dim.50), calls=%async_computation.1 | async-start | bytes 1048576 | tf_op jit(solution)/shard_map/all_to_all | solution.py:22
  36.7 0.7 copy-done.3
  37.4 0.6 convolution_convert_fusion.4
  38.0 8.0 %all-to-all-done.1 = bf16[8,2,32,512]{3,2,1,0:T(8,128)(2,1)S(1)} async-done(((bf16[8,2,32,512]{3,2,1,0:T(8,128)(2,1)}), bf16[8,2,32,512]{3,2,1,0:T(8,128)(2,1)S(1)}, u32[]{:S(2)}, u32[]{:S(2)}) %all-to-all-start.1) | async-done | bytes 524320 | tf_op jit(solution)/shard_map/all_to_all | solution.py:22
  46.3 0.7 broadcast_in_dim.51
  47.0 4.3 %all-to-all-start.2 = ((bf16[4,2,24,512]{3,2,1,0:T(8,128)(2,1)}), bf16[4,2,24,512]{3,2,1,0:T(8,128)(2,1)S(1)}, u32[]{:S(2)}, u32[]{:S(2)}) async-start(bf16[4,2,24,512]{3,2,1,0:T(8,128)(2,1)} %broadcast_in_dim.51), calls=%async_computation.2 | async-start | bytes 393216 | tf_op jit(solution)/shard_map/all_to_all | solution.py:22
  51.4 5.1 %all-to-all-done.2 = bf16[4,2,24,512]{3,2,1,0:T(8,128)(2,1)S(1)} async-done(((bf16[4,2,24,512]{3,2,1,0:T(8,128)(2,1)}), bf16[4,2,24,512]{3,2,1,0:T(8,128)(2,1)S(1)}, u32[]{:S(2)}, u32[]{:S(2)}) %all-to-all-start.2) | async-done | bytes 196640 | tf_op jit(solution)/shard_map/all_to_all | solution.py:22
  57.0 0.7 copy-done.4
  57.6 0.4 fusion.6
  58.6 0.8 broadcast_in_dim.53
  59.3 3.5 %all-to-all-start.3 = ((bf16[8,2,24,512]{3,2,1,0:T(8,128)(2,1)}), bf16[8,2,24,512]{3,2,1,0:T(8,128)(2,1)S(1)}, u32[]{:S(2)}, u32[]{:S(2)}) async-start(bf16[8,2,24,512]{3,2,1,0:T(8,128)(2,1)} %bitcast.13), calls=%async_computation.3 | async-start | bytes 786432 | tf_op jit(solution)/shard_map/all_to_all | solution.py:22
  62.8 0.3 fusion.9
  63.4 15.2 %all-to-all-done.3 = bf16[8,2,24,512]{3,2,1,0:T(8,128)(2,1)S(1)} async-done(((bf16[8,2,24,512]{3,2,1,0:T(8,128)(2,1)}), bf16[8,2,24,512]{3,2,1,0:T(8,128)(2,1)S(1)}, u32[]{:S(2)}, u32[]{:S(2)}) %all-to-all-start.3) | async-done | bytes 393248 | tf_op jit(solution)/shard_map/all_to_all | solution.py:22
  78.9 0.7 pad_maximum_fusion
  79.7 7.1 %all-to-all-start.5 = ((bf16[8,36,512]{2,1,0:T(8,128)(2,1)}), bf16[8,36,512]{2,1,0:T(8,128)(2,1)S(1)}, u32[]{:S(2)}, u32[]{:S(2)}) async-start(bf16[8,36,512]{2,1,0:T(8,128)(2,1)} %pad_maximum_fusion), calls=%async_computation.5 | async-start | bytes 655360 | tf_op jit(solution)/shard_map/all_to_all | solution.py:22
  86.8 0.6 convolution_convert_fusion.3
  87.4 6.5 %all-to-all-done.5 = bf16[8,36,512]{2,1,0:T(8,128)(2,1)S(1)} async-done(((bf16[8,36,512]{2,1,0:T(8,128)(2,1)}), bf16[8,36,512]{2,1,0:T(8,128)(2,1)S(1)}, u32[]{:S(2)}, u32[]{:S(2)}) %all-to-all-start.5) | async-done | bytes 294944 | tf_op jit(solution)/shard_map/all_to_all | solution.py:22
  93.9 0.6 broadcast_in_dim.54
  94.5 11.4 %all-to-all-start.4 = ((bf16[4,24,256]{2,1,0:T(8,128)(2,1)}), bf16[4,24,256]{2,1,0:T(8,128)(2,1)S(1)}, u32[]{:S(2)}, u32[]{:S(2)}) async-start(bf16[4,24,256]{2,1,0:T(8,128)(2,1)} %broadcast_in_dim.54), calls=%async_computation.4 | async-start | bytes 98304 | tf_op jit(solution)/shard_map/all_to_all | solution.py:22
  106.1 0.7 pad_maximum_fusion.1
  106.7 3.6 %all-to-all-done.4 = bf16[4,24,256]{2,1,0:T(8,128)(2,1)S(1)} async-done(((bf16[4,24,256]{2,1,0:T(8,128)(2,1)}), bf16[4,24,256]{2,1,0:T(8,128)(2,1)S(1)}, u32[]{:S(2)}, u32[]{:S(2)}) %all-to-all-start.4) | async-done | bytes 49184 | tf_op jit(solution)/shard_map/all_to_all | solution.py:22
  110.4 11.0 %all-to-all-start.6 = ((bf16[8,8,512]{2,1,0:T(8,128)(2,1)}), bf16[8,8,512]{2,1,0:T(8,128)(2,1)S(1)}, u32[]{:S(2)}, u32[]{:S(2)}) async-start(bf16[8,8,512]{2,1,0:T(8,128)(2,1)} %pad_maximum_fusion.1), calls=%async_computation.6 | async-start | bytes 131072 | tf_op jit(solution)/shard_map/all_to_all | solution.py:22
  121.4 0.6 multiply_subtract_fusion
  122.0 9.1 %all-to-all-done.6 = bf16[8,8,512]{2,1,0:T(8,128)(2,1)S(1)} async-done(((bf16[8,8,512]{2,1,0:T(8,128)(2,1)}), bf16[8,8,512]{2,1,0:T(8,128)(2,1)S(1)}, u32[]{:S(2)}, u32[]{:S(2)}) %all-to-all-start.6) | async-done | bytes 65568 | tf_op jit(solution)/shard_map/all_to_all | solution.py:22
  131.3 0.6 copy-done.1
  131.9 0.6 sub.41
  132.6 0.6 fusion.36
  (44 shorter events, 2.3 us)
Async XLA Ops:
  0.6 56.3 %copy-start = (bf16[151,64]{0,1:T(8,128)(2,1)S(1)}, bf16[151,64]{0,1:T(8,128)(2,1)}, u32[]{:S(2)}) copy-start(bf16[151,64]{0,1:T(8,128)(2,1)} %param.10) | copy-start | bytes 57988
  2.1 27.3 %all-to-all-start = ((bf16[16,4,512]{2,1,0:T(4,128)(2,1)}), bf16[16,4,512]{2,1,0:T(4,128)(2,1)S(1)}, u32[]{:S(2)}, u32[]{:S(2)}) async-start(bf16[16,4,512]{2,1,0:T(4,128)(2,1)} %broadcast_in_dim.23), calls=%async_computation | async-start | bytes 131072 | tf_op jit(solution)/shard_map/all_to_all | solution.py:22
  30.3 15.8 %all-to-all-start.1 = ((bf16[8,2,32,512]{3,2,1,0:T(8,128)(2,1)}), bf16[8,2,32,512]{3,2,1,0:T(8,128)(2,1)S(1)}, u32[]{:S(2)}, u32[]{:S(2)}) async-start(bf16[8,2,32,512]{3,2,1,0:T(8,128)(2,1)} %broadcast_in_dim.50), calls=%async_computation.1 | async-start | bytes 1048576 | tf_op jit(solution)/shard_map/all_to_all | solution.py:22
  36.7 0.7 copy-start.3
  47.0 4.3 %copy-start.5 = (s32[20]{0:T(128)S(1)}, s32[20]{0:T(128)}, u32[]{:S(2)}) copy-start(s32[20]{0:T(128)} %param.7) | copy-start | bytes 244
  47.0 4.3 %copy-start.2 = (f32[20,64]{1,0:T(8,128)S(1)}, f32[20,64]{1,0:T(8,128)}, u32[]{:S(2)}) copy-start(f32[20,64]{1,0:T(8,128)} %param.9) | copy-start | bytes 15364
  47.0 9.5 %all-to-all-start.2 = ((bf16[4,2,24,512]{3,2,1,0:T(8,128)(2,1)}), bf16[4,2,24,512]{3,2,1,0:T(8,128)(2,1)S(1)}, u32[]{:S(2)}, u32[]{:S(2)}) async-start(bf16[4,2,24,512]{3,2,1,0:T(8,128)(2,1)} %broadcast_in_dim.51), calls=%async_computation.2 | async-start | bytes 393216 | tf_op jit(solution)/shard_map/all_to_all | solution.py:22
  56.7 0.9 copy-start.4
  59.3 19.2 %all-to-all-start.3 = ((bf16[8,2,24,512]{3,2,1,0:T(8,128)(2,1)}), bf16[8,2,24,512]{3,2,1,0:T(8,128)(2,1)S(1)}, u32[]{:S(2)}, u32[]{:S(2)}) async-start(bf16[8,2,24,512]{3,2,1,0:T(8,128)(2,1)} %bitcast.13), calls=%async_computation.3 | async-start | bytes 786432 | tf_op jit(solution)/shard_map/all_to_all | solution.py:22
  79.7 14.3 %all-to-all-start.5 = ((bf16[8,36,512]{2,1,0:T(8,128)(2,1)}), bf16[8,36,512]{2,1,0:T(8,128)(2,1)S(1)}, u32[]{:S(2)}, u32[]{:S(2)}) async-start(bf16[8,36,512]{2,1,0:T(8,128)(2,1)} %pad_maximum_fusion), calls=%async_computation.5 | async-start | bytes 655360 | tf_op jit(solution)/shard_map/all_to_all | solution.py:22
  94.5 15.8 %all-to-all-start.4 = ((bf16[4,24,256]{2,1,0:T(8,128)(2,1)}), bf16[4,24,256]{2,1,0:T(8,128)(2,1)S(1)}, u32[]{:S(2)}, u32[]{:S(2)}) async-start(bf16[4,24,256]{2,1,0:T(8,128)(2,1)} %broadcast_in_dim.54), calls=%async_computation.4 | async-start | bytes 98304 | tf_op jit(solution)/shard_map/all_to_all | solution.py:22
  110.4 20.8 %all-to-all-start.6 = ((bf16[8,8,512]{2,1,0:T(8,128)(2,1)}), bf16[8,8,512]{2,1,0:T(8,128)(2,1)S(1)}, u32[]{:S(2)}, u32[]{:S(2)}) async-start(bf16[8,8,512]{2,1,0:T(8,128)(2,1)} %pad_maximum_fusion.1), calls=%async_computation.6 | async-start | bytes 131072 | tf_op jit(solution)/shard_map/all_to_all | solution.py:22
  131.2 0.7 copy-start.1

commit v3 on v2

--- a/solution.py
+++ b/solution.py
@@ -31,10 +31,15 @@
     return jnp.sum(x.astype(F32), axis=0)
 
 
-def column_order():
+def column_order(flip):
     i = lax.broadcasted_iota(jnp.int32, (RT, RT), 0)
     j = lax.broadcasted_iota(jnp.int32, (RT, RT), 1)
-    target = (i // 64) * 64 + ((i // 4) % 2) * 32 + ((i // 8) % 8) * 4 + i % 4
+    x, zl, c, r = i // 64, (i // 8) % 8, (i // 4) % 2, i % 4
+    low = zl * 4 + r
+    if flip is None:
+        target = x * 64 + c * 32 + low
+    else:
+        target = (c ^ flip) * 128 + x * 32 + low
     return (target == j).astype(BF16)
 
 
@@ -52,17 +57,25 @@
     bands = ny * nzh
     near = nzl * core_rows
     weights = view_mask.astype(F32)[:, None, None]
-    order = column_order()
-    tex_bf = jnp.dot(tex_factor.astype(BF16), order, preferred_element_type=F32).astype(BF16)
-    view_bands = view_factor.astype(BF16).reshape(views, bands, band)
+    view_bf = view_factor.astype(BF16)
+    view_bands = view_bf.reshape(views, bands, band)
     core_bf = core_tensor.astype(BF16).reshape(core_rows, width)
 
     core_z = gather_blocks(core_bf, ("zh", "zl")).reshape(nzh, near, width)
-    core_xc = gather_blocks(core_z, ("x", "c"))
-    core_pair = jnp.transpose(core_xc, (1, 0, 2, 3)).reshape(nzh, RT, width)
-    proj_pair = jnp.einsum("ta,zan->ztn", tex_bf, core_pair, preferred_element_type=F32)
-    projected = gather_blocks(proj_pair.astype(BF16), ("y",))
-    projected = projected.reshape(bands, tex_rows, band, RL)
+    core_own = gather_blocks(core_z, ("x", "y")).reshape(nx, ny, nzh, near, width)
+    core_other = lax.ppermute(core_own, "c", [(0, 1), (1, 0)])
+
+    tex_raw = tex_factor.astype(BF16)
+    order = lax.optimization_barrier(column_order(lax.axis_index("c")))
+    tex_rel = jnp.dot(tex_raw, order, preferred_element_type=F32).astype(BF16)
+    tex_rel = tex_rel.reshape(tex_rows, nc, nx, near)
+    tex_abs = jnp.dot(tex_raw, column_order(None), preferred_element_type=F32).astype(BF16)
+    tex_rel, tex_abs = lax.optimization_barrier((tex_rel, tex_abs))
+
+    projected = jnp.einsum(
+        "txk,xyzkn->yztn", tex_rel[:, 0], core_own, preferred_element_type=F32
+    ) + jnp.einsum("txk,xyzkn->yztn", tex_rel[:, 1], core_other, preferred_element_type=F32)
+    projected = projected.astype(BF16).reshape(bands, tex_rows, band, RL)
 
     mixed = jnp.einsum(
         "vgb,gtbc->vtc", view_bands, projected, preferred_element_type=F32
@@ -73,21 +86,27 @@
     back = jnp.einsum("vtl,lc->vtc", resid, light_factor, preferred_element_type=F32).astype(BF16)
 
     partial_y = jnp.einsum("vgb,vtc->gtbc", view_bands, back, preferred_element_type=F32)
-    partial_y = partial_y.astype(BF16).reshape(ny, 1, nzh, tex_rows, width)
-    partial_y = jnp.broadcast_to(partial_y, (ny, nzh, nzh, tex_rows, width))
-    partial_y = partial_y.reshape(bands, nzh, tex_rows, width)
-    summed = sum_blocks(exchange(partial_y, VIEW)).astype(BF16)
+    partial_y = partial_y.astype(BF16).reshape(ny, nzh, tex_rows, width)
+    tex_part = jnp.concatenate(
+        [
+            jnp.einsum("yztn,xyzkn->txk", partial_y, half, preferred_element_type=F32)
+            .astype(BF16)
+            .reshape(tex_rows, nx * near)
+            for half in (core_own, core_other)
+        ],
+        axis=1,
+    )
+    tex_part = lax.dot_general(
+        tex_part, order, (((1,), (1,)), ((), ())), preferred_element_type=F32
+    ).astype(BF16)
+    tex_block = jnp.broadcast_to(tex_part[None], (bands, tex_rows, RT))
+    blocks = jnp.concatenate([partial_y.reshape(bands, tex_rows, width), tex_block], axis=2)
+    blocks = sum_blocks(exchange(blocks, VIEW))
+    summed = blocks[:, :width].astype(BF16)
+    grad_tex = scaling * blocks[:, width:]
     view_part = jnp.einsum("vtc,gtbc->vgb", back, projected, preferred_element_type=F32)
 
-    tex_part = jnp.einsum("ztn,zan->ta", summed, core_pair, preferred_element_type=F32)
-    tex_part = lax.dot_general(
-        tex_part.astype(BF16), order, (((1,), (1,)), ((), ())), preferred_element_type=F32
-    )
-    tex_blocks = gather_blocks(tex_part.astype(BF16), ("y",))
-    grad_tex = scaling * sum_blocks(tex_blocks)
-
-    own = jnp.where(lax.axis_index("zh") == 0, summed[0], summed[1])
-    core_part = jnp.einsum("ta,tn->an", tex_bf, own, preferred_element_type=F32)
+    core_part = jnp.einsum("ta,tn->an", tex_abs, summed, preferred_element_type=F32)
     core_part = core_part.astype(BF16).reshape(nx * nc, near, width)
     spare = core_rows * width - views * RV
     view_part = jnp.pad(view_part.astype(BF16).reshape(views * RV), (0, spare))

time: 135 us -> 128 us (0.948); the launches traced: 133 us -> 128 us
  blocking collectives: 0 us -> 38.6 us
  starting transfers between devices: 59.5 us -> 32.3 us
  waiting for transfers between devices: 59.1 us -> 39.6 us
  matrix products: 2.7 us -> 4.65 us
    all_to_all x0 -> x2, blocking collectives: none -> 38.6 us  [exchange(): return lax.all_to_all(x, axes, 0, 0, tiled=True)]
    all_to_all x7 -> x3, starting transfers between devices: 59.5 us -> 27 us  [exchange(): return lax.all_to_all(x, axes, 0, 0, tiled=True)]
    all_to_all x7 -> x3, waiting for transfers between devices: 59.1 us -> 39.6 us  [exchange(): return lax.all_to_all(x, axes, 0, 0, tiled=True)]
    ppermute x0 -> x1, starting transfers between devices: none -> 5.3 us  [per_device(): core_other = lax.ppermute(core_own, 'c', [(0, 1), (1, 0)])]
    dot_general x4 -> x8, matrix products: 1.6 us -> 3.55 us  [the longest x2 1.62 us: per_device(): jnp.einsum('yztn,xyzkn->txk', partial_y, half, preferred_element_type=F32)]
    broadcast_in_dim x6 -> x4, local copies, waits for them, and re-layouts: 2.93 us -> 1.23 us  [gather_blocks(): return exchange(jnp.broadcast_to(x[None], (count,) + x.shape), axes)]
    reshape x1 -> x6, local copies, waits for them, and re-layouts: 0.22 us -> 1.78 us  [the longest x1 1.05 us: per_device(): gather_blocks(core_z, ('x', 'y')).reshape(nx, ny, nzh, near, width)]
    unnamed x13 -> x17, local copies, waits for them, and re-layouts: 2.15 us -> 2.85 us
  transfers between devices with their start and end apart: 7 -> 4, of which waited for: 7 -> 3; matrix products, arithmetic and copies ran while one was open for 2% -> 2% of each run, Pallas kernels for 0% -> 0%
where the time goes in v3:
time: 128 us
  waiting for transfers between devices  39.6 us (31%)
  blocking collectives  38.6 us (30%)
  starting transfers between devices  32.3 us (25%)
  local copies, waits for them, and re-layouts  6.75 us (5%)
  other arithmetic  4.78 us (4%)
  matrix products  4.65 us (4%)
    all_to_all x3, waiting for transfers between devices, exchange(): return lax.all_to_all(x, axes, 0, 0, tiled=True)  39.6 us
    all_to_all x2, blocking collectives, exchange(): return lax.all_to_all(x, axes, 0, 0, tiled=True)  38.6 us
    all_to_all x3, starting transfers between devices, exchange(): return lax.all_to_all(x, axes, 0, 0, tiled=True)  27 us
    ppermute x1, starting transfers between devices, per_device(): core_other = lax.ppermute(core_own, 'c', [(0, 1), (1, 0)])  5.3 us
    unnamed x17, local copies, waits for them, and re-layouts  2.85 us
  transfers between devices with their start and end apart: 4, of which 3 were waited for; matrix products, arithmetic and copies ran while one was open for 2% of the time, Pallas kernels for 0%

profile of v3, /device:TPU:1, one launch (start us, length us, event | category | flops | bytes accessed | tf_op | source)
XLA Modules:
  0.0 127.7 jit_solution(35128546762780447)
XLA Ops:
  0.6 0.7 convert_element_type.91
  1.5 27.1 %all_to_all.25 = bf16[16,4,512]{2,1,0:T(4,128)(2,1)S(1)} all-to-all(bf16[16,4,512]{2,1,0:T(4,128)(2,1)S(1)} %broadcast_in_dim.17), channel_id=1, replica_groups=mesh['x'=4,'zl'=8,'c'=2,'y'=4,'zh'=2] {'zh','zl'}, dimensions={0} | all-to-all | bytes 131072 | tf_op jit(solution)/shard_map/all_to_all | solution.py:22
  28.6 1.1 broadcast_in_dim.37
  29.7 6.8 %all-to-all-start.1 = ((bf16[16,2,32,512]{3,2,1,0:T(8,128)(2,1)}), bf16[16,2,32,512]{3,2,1,0:T(8,128)(2,1)S(1)}, u32[]{:S(2)}, u32[]{:S(2)}) async-start(bf16[16,2,32,512]{3,2,1,0:T(8,128)(2,1)} %broadcast_in_dim.37), calls=%async_computation.1 | async-start | bytes 2097152 | tf_op jit(solution)/shard_map/all_to_all | solution.py:22
  36.5 14.6 %all-to-all-done.1 = bf16[16,2,32,512]{3,2,1,0:T(8,128)(2,1)S(1)} async-done(((bf16[16,2,32,512]{3,2,1,0:T(8,128)(2,1)}), bf16[16,2,32,512]{3,2,1,0:T(8,128)(2,1)S(1)}, u32[]{:S(2)}, u32[]{:S(2)}) %all-to-all-start.1) | async-done | bytes 1048608 | tf_op jit(solution)/shard_map/all_to_all | solution.py:22
  51.1 1.0 copy.47
  52.2 5.3 %collective-permute-start = (bf16[4,4,2,32,512]{4,3,0,2,1:T(8,128)(2,1)}, bf16[4,4,2,32,512]{4,3,0,2,1:T(8,128)(2,1)S(1)}, u32[]{:S(2)}, u32[]{:S(2)}) collective-permute-start(bf16[4,4,2,32,512]{4,3,0,2,1:T(8,128)(2,1)} %copy.47), channel_id=1, source_target_pairs={{0,8},{8,0},{1,9},{9,1},{2,10},{10,2},{3,11},{11,3},{4,12},{12,4},... | collective-permute-start | bytes 3145736 | tf_op jit(solution)/shard_map/ppermute | solution.py:66
  57.5 0.6 fusion.28
  58.5 0.6 fusion.15
  59.1 0.7 copy-done.5
  59.9 0.3 convolution_bitcast_fusion
  60.3 0.5 fusion.8
  61.2 0.7 copy-done.6
  61.9 0.4 fusion.9
  62.3 0.6 copy-done.1
  62.9 0.2 fusion.2
  63.4 0.3 reshape_reshape.3
  63.7 0.8 fusion.11
  64.5 0.8 fusion.12
  65.8 0.7 pad_maximum_fusion.1
  66.5 3.6 %all-to-all-start.2 = ((bf16[8,24,768]{2,1,0:T(8,128)(2,1)}), bf16[8,24,768]{2,1,0:T(8,128)(2,1)S(1)}, u32[]{:S(2)}, u32[]{:S(2)}) async-start(bf16[8,24,768]{2,1,0:T(8,128)(2,1)} %pad_maximum_fusion.1), calls=%async_computation.2 | async-start | bytes 589824 | tf_op jit(solution)/shard_map/all_to_all | solution.py:22
  70.2 0.3 fusion.13
  70.7 15.9 %all-to-all-done.2 = bf16[8,24,768]{2,1,0:T(8,128)(2,1)S(1)} async-done(((bf16[8,24,768]{2,1,0:T(8,128)(2,1)}), bf16[8,24,768]{2,1,0:T(8,128)(2,1)S(1)}, u32[]{:S(2)}, u32[]{:S(2)}) %all-to-all-start.2) | async-done | bytes 294944 | tf_op jit(solution)/shard_map/all_to_all | solution.py:22
  86.6 0.2 convolution_convert_fusion.1
  86.9 11.5 %all_to_all.26 = bf16[8,36,512]{2,1,0:T(8,128)(2,1)S(1)} all-to-all(bf16[8,36,512]{2,1,0:T(8,128)(2,1)S(1)} %pad_maximum_fusion), channel_id=1, replica_groups=mesh['x'=4,'zl'=8,'c'=2,'y'=4,'zh'=2] {'x','c'}, dimensions={0} | all-to-all | bytes 589824 | tf_op jit(solution)/shard_map/all_to_all | solution.py:22
  98.6 0.7 pad_maximum_fusion.2
  99.2 16.6 %all-to-all-start.4 = ((bf16[8,8,512]{2,1,0:T(8,128)(2,1)}), bf16[8,8,512]{2,1,0:T(8,128)(2,1)S(1)}, u32[]{:S(2)}, u32[]{:S(2)}) async-start(bf16[8,8,512]{2,1,0:T(8,128)(2,1)} %pad_maximum_fusion.2), calls=%async_computation.4 | async-start | bytes 131072 | tf_op jit(solution)/shard_map/all_to_all | solution.py:22
  115.9 0.6 fusion.55
  116.5 9.1 %all-to-all-done.4 = bf16[8,8,512]{2,1,0:T(8,128)(2,1)S(1)} async-done(((bf16[8,8,512]{2,1,0:T(8,128)(2,1)}), bf16[8,8,512]{2,1,0:T(8,128)(2,1)S(1)}, u32[]{:S(2)}, u32[]{:S(2)}) %all-to-all-start.4) | async-done | bytes 65568 | tf_op jit(solution)/shard_map/all_to_all | solution.py:22
  125.7 0.6 fusion.58
  126.4 0.6 copy-done.4
  127.1 0.6 sub.47
  (54 shorter events, 2.4 us)
Async XLA Ops:
  0.6 60.6 %copy-start = (bf16[151,64]{0,1:T(8,128)(2,1)S(1)}, bf16[151,64]{0,1:T(8,128)(2,1)}, u32[]{:S(2)}) copy-start(bf16[151,64]{0,1:T(8,128)(2,1)} %param.10) | copy-start | bytes 57988
  29.7 21.4 %all-to-all-start.1 = ((bf16[16,2,32,512]{3,2,1,0:T(8,128)(2,1)}), bf16[16,2,32,512]{3,2,1,0:T(8,128)(2,1)S(1)}, u32[]{:S(2)}, u32[]{:S(2)}) async-start(bf16[16,2,32,512]{3,2,1,0:T(8,128)(2,1)} %broadcast_in_dim.37), calls=%async_computation.1 | async-start | bytes 2097152 | tf_op jit(solution)/shard_map/all_to_all | solution.py:22
  52.2 8.1 %collective-permute-start = (bf16[4,4,2,32,512]{4,3,0,2,1:T(8,128)(2,1)}, bf16[4,4,2,32,512]{4,3,0,2,1:T(8,128)(2,1)S(1)}, u32[]{:S(2)}, u32[]{:S(2)}) collective-permute-start(bf16[4,4,2,32,512]{4,3,0,2,1:T(8,128)(2,1)} %copy.47), channel_id=1, source_target_pairs={{0,8},{8,0},{1,9},{9,1},{2,10},{10,2},{3,11},{11,3},{4,12},{12,4},... | collective-permute-start | bytes 3145736 | tf_op jit(solution)/shard_map/ppermute | solution.py:66
  57.5 0.7 copy-start.7
  57.5 0.7 copy-start.3
  59.1 0.7 copy-start.5
  61.0 0.9 copy-start.6
  62.3 0.7 copy-start.1
  66.5 3.6 %copy-start.2 = (bf16[20,24,64]{2,1,0:T(8,128)(2,1)S(1)}, bf16[20,24,64]{2,1,0:T(8,128)(2,1)}, u32[]{:S(2)}) copy-start(bf16[20,24,64]{2,1,0:T(8,128)(2,1)} %copy-done.1) | copy-start | bytes 184324
  66.5 20.0 %all-to-all-start.2 = ((bf16[8,24,768]{2,1,0:T(8,128)(2,1)}), bf16[8,24,768]{2,1,0:T(8,128)(2,1)S(1)}, u32[]{:S(2)}, u32[]{:S(2)}) async-start(bf16[8,24,768]{2,1,0:T(8,128)(2,1)} %pad_maximum_fusion.1), calls=%async_computation.2 | async-start | bytes 589824 | tf_op jit(solution)/shard_map/all_to_all | solution.py:22
  99.2 26.4 %all-to-all-start.4 = ((bf16[8,8,512]{2,1,0:T(8,128)(2,1)}), bf16[8,8,512]{2,1,0:T(8,128)(2,1)S(1)}, u32[]{:S(2)}, u32[]{:S(2)}) async-start(bf16[8,8,512]{2,1,0:T(8,128)(2,1)} %pad_maximum_fusion.2), calls=%async_computation.4 | async-start | bytes 131072 | tf_op jit(solution)/shard_map/all_to_all | solution.py:22
  126.3 0.7 copy-start.4

commit v4 on v3

--- a/solution.py
+++ b/solution.py
@@ -56,9 +56,32 @@
     nx, nzl, nc, ny, nzh = SIZES
     bands = ny * nzh
     near = nzl * core_rows
-    weights = view_mask.astype(F32)[:, None, None]
-    view_bf = view_factor.astype(BF16)
-    view_bands = view_bf.reshape(views, bands, band)
+    zh = lax.axis_index("zh")
+    weights = view_mask.astype(F32)
+
+    seen = jnp.einsum(
+        "vtl,lc->vtc", jnp.transpose(measured, (1, 0, 2)), light_factor, preferred_element_type=F32
+    )
+    seen = (weights[:, None, None] * seen).astype(BF16)
+    masked_bf = (weights[:, None] * view_factor).astype(BF16)
+    sent = jnp.concatenate([seen, masked_bf[:, None, :]], axis=1)
+    sent = jnp.concatenate([sent[: views // 2], sent[views // 2 :]], axis=2)
+    came = lax.ppermute(sent, "zh", [(0, 1), (1, 0)])
+    both_halves = jnp.where(
+        zh == 0, jnp.stack([sent, came]), jnp.stack([came, sent])
+    )
+    both_halves = jnp.concatenate([both_halves[..., :RL], both_halves[..., RL:]], axis=1)
+    both_halves = both_halves.reshape(nzh * views, tex_rows + 1, RL)
+    seen_all = both_halves[:, :tex_rows].astype(F32)
+    masked_all = both_halves[:, tex_rows].reshape(nzh * views, bands, band)
+
+    gram = scaling * lax.dot_general(
+        light_factor, light_factor, (((0,), (0,)), ((), ())), preferred_element_type=F32
+    )
+    gram_high = lax.reduce_precision(gram, 8, 7)
+    gram_low = (gram - gram_high).astype(BF16)
+    gram_high = gram_high.astype(BF16)
+
     core_bf = core_tensor.astype(BF16).reshape(core_rows, width)
 
     core_z = gather_blocks(core_bf, ("zh", "zl")).reshape(nzh, near, width)
@@ -78,14 +101,13 @@
     projected = projected.astype(BF16).reshape(bands, tex_rows, band, RL)
 
     mixed = jnp.einsum(
-        "vgb,gtbc->vtc", view_bands, projected, preferred_element_type=F32
+        "vgb,gtbc->vtc", masked_all, projected, preferred_element_type=F32
     ).astype(BF16)
-    approx = jnp.einsum("vtc,lc->vtl", mixed, light_factor, preferred_element_type=F32)
-    target = jnp.transpose(measured, (1, 0, 2)).astype(F32)
-    resid = (weights * (scaling * approx - target)).astype(BF16)
-    back = jnp.einsum("vtl,lc->vtc", resid, light_factor, preferred_element_type=F32).astype(BF16)
+    fitted = jnp.einsum("vtc,cd->vtd", mixed, gram_high, preferred_element_type=F32)
+    fitted += jnp.einsum("vtc,cd->vtd", mixed, gram_low, preferred_element_type=F32)
+    back = (fitted - seen_all).astype(BF16)
 
-    partial_y = jnp.einsum("vgb,vtc->gtbc", view_bands, back, preferred_element_type=F32)
+    partial_y = jnp.einsum("vgb,vtc->gtbc", masked_all, back, preferred_element_type=F32)
     partial_y = partial_y.astype(BF16).reshape(ny, nzh, tex_rows, width)
     tex_part = jnp.concatenate(
         [
@@ -99,12 +121,14 @@
     tex_part = lax.dot_general(
         tex_part, order, (((1,), (1,)), ((), ())), preferred_element_type=F32
     ).astype(BF16)
-    tex_block = jnp.broadcast_to(tex_part[None], (bands, tex_rows, RT))
-    blocks = jnp.concatenate([partial_y.reshape(bands, tex_rows, width), tex_block], axis=2)
-    blocks = sum_blocks(exchange(blocks, VIEW))
+    tex_block = jnp.broadcast_to(tex_part[None], (ny, tex_rows, RT))
+    own_y = jnp.where(zh == 0, partial_y[:, 0], partial_y[:, 1])
+    blocks = jnp.concatenate([own_y, tex_block], axis=2)
+    blocks = sum_blocks(exchange(blocks, ("y",)))
     summed = blocks[:, :width].astype(BF16)
     grad_tex = scaling * blocks[:, width:]
-    view_part = jnp.einsum("vtc,gtbc->vgb", back, projected, preferred_element_type=F32)
+    own_back = jnp.where(zh == 0, back[:views], back[views:])
+    view_part = jnp.einsum("vtc,gtbc->vgb", own_back, projected, preferred_element_type=F32)
 
     core_part = jnp.einsum("ta,tn->an", tex_abs, summed, preferred_element_type=F32)
     core_part = core_part.astype(BF16).reshape(nx * nc, near, width)

time: 128 us -> 106 us (0.83)
  blocking collectives: 38.6 us -> 11.3 us
  starting transfers between devices: 32.3 us -> 46.2 us
  waiting for transfers between devices: 39.6 us -> 28.6 us
  local copies, waits for them, and re-layouts: 6.75 us -> 8.1 us
    all_to_all x2 -> x1, blocking collectives: 38.6 us -> 11.3 us  [exchange(): return lax.all_to_all(x, axes, 0, 0, tiled=True)]
    ppermute x0 -> x1, starting transfers between devices: none -> 12 us  [per_device(): came = lax.ppermute(sent, 'zh', [(0, 1), (1, 0)])]
    all_to_all x3 -> x4, waiting for transfers between devices: 39.6 us -> 27.7 us  [exchange(): return lax.all_to_all(x, axes, 0, 0, tiled=True)]
    all_to_all x3 -> x4, starting transfers between devices: 27 us -> 29.3 us  [exchange(): return lax.all_to_all(x, axes, 0, 0, tiled=True)]
    unnamed x17 -> x19, local copies, waits for them, and re-layouts: 2.85 us -> 2.77 us
  transfers between devices with their start and end apart: 4 -> 6, of which waited for: 3 -> 4; matrix products, arithmetic and copies ran while one was open for 2% -> 6% of each run, Pallas kernels for 0% -> 0%
where the time goes in v4:
time: 106 us
  starting transfers between devices  46.2 us (44%)
  waiting for transfers between devices  28.6 us (27%)
  blocking collectives  11.3 us (11%)
  local copies, waits for them, and re-layouts  8.1 us (8%)
  matrix products  5.18 us (5%)
  other arithmetic  5.14 us (5%)
  between operations  1.09 us (1%)
    all_to_all x4, starting transfers between devices, exchange(): return lax.all_to_all(x, axes, 0, 0, tiled=True)  29.3 us
    all_to_all x4, waiting for transfers between devices, exchange(): return lax.all_to_all(x, axes, 0, 0, tiled=True)  27.7 us
    ppermute x1, starting transfers between devices, per_device(): came = lax.ppermute(sent, 'zh', [(0, 1), (1, 0)])  12 us
    all_to_all x1, blocking collectives, exchange(): return lax.all_to_all(x, axes, 0, 0, tiled=True)  11.3 us
    ppermute x1, starting transfers between devices, per_device(): core_other = lax.ppermute(core_own, 'c', [(0, 1), (1, 0)])  4.91 us
    unnamed x19, local copies, waits for them, and re-layouts  2.77 us
  transfers between devices with their start and end apart: 6, of which 4 were waited for; matrix products, arithmetic and copies ran while one was open for 6% of the time, Pallas kernels for 0%

profile of v4, /device:TPU:1, one launch (start us, length us, event | category | flops | bytes accessed | tf_op | source)
XLA Modules:
  0.0 105.7 jit_solution(16541574011717028048)
XLA Ops:
  0.6 0.8 convert_element_type.93
  1.5 0.6 broadcast_in_dim.40
  2.1 15.9 %all-to-all-start = ((bf16[16,4,512]{2,1,0:T(4,128)(2,1)}), bf16[16,4,512]{2,1,0:T(4,128)(2,1)S(1)}, u32[]{:S(2)}, u32[]{:S(2)}) async-start(bf16[16,4,512]{2,1,0:T(4,128)(2,1)} %broadcast_in_dim.40), calls=%async_computation | async-start | bytes 131072 | tf_op jit(solution)/shard_map/all_to_all | solution.py:22
  18.2 0.6 copy-done.3
  19.1 12.0 %collective-permute-start = (bf16[10,25,128]{2,1,0:T(8,128)(2,1)S(1)}, bf16[10,25,128]{2,1,0:T(8,128)(2,1)S(1)}, u32[]{:S(2)}, u32[]{:S(2)}) collective-permute-start(bf16[10,25,128]{2,1,0:T(8,128)(2,1)S(1)} %fusion.49), channel_id=1, source_target_pairs={{0,1},{1,0},{2,3},{3,2},{4,5},{5,4},{6,7},{7,6},{8,9},{9,8},{10,11... | collective-permute-start | bytes 192008 | tf_op jit(solution)/shard_map/ppermute | solution.py:69
  31.2 1.1 %broadcast_in_dim.42 = bf16[16,2,32,512]{3,2,1,0:T(8,128)(2,1)} broadcast(bf16[2,32,512]{2,1,0:T(8,128)(2,1)S(1)} %broadcast_in_dim.41), dimensions={1,2,3} | broadcast | bytes 1114112 | tf_op jit(solution)/shard_map/broadcast_in_dim | solution.py:27
  32.3 6.8 %all-to-all-start.1 = ((bf16[16,2,32,512]{3,2,1,0:T(8,128)(2,1)}), bf16[16,2,32,512]{3,2,1,0:T(8,128)(2,1)S(1)}, u32[]{:S(2)}, u32[]{:S(2)}) async-start(bf16[16,2,32,512]{3,2,1,0:T(8,128)(2,1)} %broadcast_in_dim.42), calls=%async_computation.1 | async-start | bytes 2097152 | tf_op jit(solution)/shard_map/all_to_all | solution.py:22
  39.1 0.6 fusion.23
  40.0 14.3 %all-to-all-done.1 = bf16[16,2,32,512]{3,2,1,0:T(8,128)(2,1)S(1)} async-done(((bf16[16,2,32,512]{3,2,1,0:T(8,128)(2,1)}), bf16[16,2,32,512]{3,2,1,0:T(8,128)(2,1)S(1)}, u32[]{:S(2)}, u32[]{:S(2)}) %all-to-all-start.1) | async-done | bytes 1048608 | tf_op jit(solution)/shard_map/all_to_all | solution.py:22
  54.3 1.1 %copy.38 = bf16[4,4,2,32,512]{4,3,0,2,1:T(8,128)(2,1)} copy(bf16[4,4,2,32,512]{4,3,2,1,0:T(8,128)(2,1)S(1)} %bitcast.129) | data formatting | bytes 2097152 | tf_op jit(solution)/shard_map/reshape | solution.py:88
  55.4 4.9 %collective-permute-start.1 = (bf16[4,4,2,32,512]{4,3,0,2,1:T(8,128)(2,1)}, bf16[4,4,2,32,512]{4,3,0,2,1:T(8,128)(2,1)S(1)}, u32[]{:S(2)}, u32[]{:S(2)}) collective-permute-start(bf16[4,4,2,32,512]{4,3,0,2,1:T(8,128)(2,1)} %copy.38), channel_id=1, source_target_pairs={{0,8},{8,0},{1,9},{9,1},{2,10},{10,2},{3,11},{11,3},{4,12},{12,4},... | collective-permute-start | bytes 3145736 | tf_op jit(solution)/shard_map/ppermute | solution.py:89
  60.4 0.6 fusion.12
  61.6 0.3 convolution_bitcast_fusion.1
  61.9 0.9 collective-permute-done.1
  62.8 0.5 fusion.6
  64.0 0.3 fusion.2
  64.3 0.7 copy-done.1
  65.7 0.8 fusion.8
  66.7 0.8 fusion.9
  67.9 0.7 pad_maximum_fusion.2
  68.6 3.3 %all-to-all-start.2 = ((bf16[4,24,768]{2,1,0:T(8,128)(2,1)}), bf16[4,24,768]{2,1,0:T(8,128)(2,1)S(1)}, u32[]{:S(2)}, u32[]{:S(2)}) async-start(bf16[4,24,768]{2,1,0:T(8,128)(2,1)} %pad_maximum_fusion.2), calls=%async_computation.2 | async-start | bytes 294912 | tf_op jit(solution)/shard_map/all_to_all | solution.py:22
  72.5 4.3 %all-to-all-done.2 = bf16[4,24,768]{2,1,0:T(8,128)(2,1)S(1)} async-done(((bf16[4,24,768]{2,1,0:T(8,128)(2,1)}), bf16[4,24,768]{2,1,0:T(8,128)(2,1)S(1)}, u32[]{:S(2)}, u32[]{:S(2)}) %all-to-all-start.2) | async-done | bytes 147488 | tf_op jit(solution)/shard_map/all_to_all | solution.py:22
  77.2 11.3 %all_to_all.25 = bf16[8,36,512]{2,1,0:T(8,128)(2,1)S(1)} all-to-all(bf16[8,36,512]{2,1,0:T(8,128)(2,1)S(1)} %pad_maximum_fusion.1), channel_id=1, replica_groups=mesh['x'=4,'zl'=8,'c'=2,'y'=4,'zh'=2] {'x','c'}, dimensions={0} | all-to-all | bytes 589824 | tf_op jit(solution)/shard_map/all_to_all | solution.py:22
  88.6 0.6 copy-done.4
  89.2 0.7 slice-done
  89.9 0.7 pad_maximum_fusion.4
  90.5 3.3 %all-to-all-start.4 = ((bf16[8,8,512]{2,1,0:T(8,128)(2,1)}), bf16[8,8,512]{2,1,0:T(8,128)(2,1)S(1)}, u32[]{:S(2)}, u32[]{:S(2)}) async-start(bf16[8,8,512]{2,1,0:T(8,128)(2,1)} %pad_maximum_fusion.4), calls=%async_computation.4 | async-start | bytes 131072 | tf_op jit(solution)/shard_map/all_to_all | solution.py:22
  93.9 0.6 fusion.52
  94.5 9.1 %all-to-all-done.4 = bf16[8,8,512]{2,1,0:T(8,128)(2,1)S(1)} async-done(((bf16[8,8,512]{2,1,0:T(8,128)(2,1)}), bf16[8,8,512]{2,1,0:T(8,128)(2,1)S(1)}, u32[]{:S(2)}, u32[]{:S(2)}) %all-to-all-start.4) | async-done | bytes 65568 | tf_op jit(solution)/shard_map/all_to_all | solution.py:22
  103.7 0.6 copy-done.6
  104.4 0.6 sub.51
  105.0 0.6 fusion.60
  (72 shorter events, 4.6 us)
Async XLA Ops:
  0.6 17.5 %copy-start = (bf16[24,20,151]{2,0,1:T(8,128)(2,1)S(1)}, bf16[24,20,151]{2,0,1:T(8,128)(2,1)}, u32[]{:S(2)}) copy-start(bf16[24,20,151]{2,0,1:T(8,128)(2,1)} %param.6) | copy-start | bytes 434884
  2.1 15.9 %copy-start.8 = (s32[20]{0:T(128)S(1)}, s32[20]{0:T(128)}, u32[]{:S(2)}) copy-start(s32[20]{0:T(128)} %param.7) | copy-start | bytes 244
  2.1 15.9 %copy-start.7 = (f32[20,64]{1,0:T(8,128)S(1)}, f32[20,64]{1,0:T(8,128)}, u32[]{:S(2)}) copy-start(f32[20,64]{1,0:T(8,128)} %param.9) | copy-start | bytes 15364
  2.1 29.0 %all-to-all-start = ((bf16[16,4,512]{2,1,0:T(4,128)(2,1)}), bf16[16,4,512]{2,1,0:T(4,128)(2,1)S(1)}, u32[]{:S(2)}, u32[]{:S(2)}) async-start(bf16[16,4,512]{2,1,0:T(4,128)(2,1)} %broadcast_in_dim.40), calls=%async_computation | async-start | bytes 131072 | tf_op jit(solution)/shard_map/all_to_all | solution.py:22
  18.0 0.8 copy-start.3
  19.1 42.0 %collective-permute-start = (bf16[10,25,128]{2,1,0:T(8,128)(2,1)S(1)}, bf16[10,25,128]{2,1,0:T(8,128)(2,1)S(1)}, u32[]{:S(2)}, u32[]{:S(2)}) collective-permute-start(bf16[10,25,128]{2,1,0:T(8,128)(2,1)S(1)} %fusion.49), channel_id=1, source_target_pairs={{0,1},{1,0},{2,3},{3,2},{4,5},{5,4},{6,7},{7,6},{8,9},{9,8},{10,11... | collective-permute-start | bytes 192008 | tf_op jit(solution)/shard_map/ppermute | solution.py:69
  32.3 22.0 %all-to-all-start.1 = ((bf16[16,2,32,512]{3,2,1,0:T(8,128)(2,1)}), bf16[16,2,32,512]{3,2,1,0:T(8,128)(2,1)S(1)}, u32[]{:S(2)}, u32[]{:S(2)}) async-start(bf16[16,2,32,512]{3,2,1,0:T(8,128)(2,1)} %broadcast_in_dim.42), calls=%async_computation.1 | async-start | bytes 2097152 | tf_op jit(solution)/shard_map/all_to_all | solution.py:22
  39.1 0.7 copy-start.5
  55.4 7.4 %collective-permute-start.1 = (bf16[4,4,2,32,512]{4,3,0,2,1:T(8,128)(2,1)}, bf16[4,4,2,32,512]{4,3,0,2,1:T(8,128)(2,1)S(1)}, u32[]{:S(2)}, u32[]{:S(2)}) collective-permute-start(bf16[4,4,2,32,512]{4,3,0,2,1:T(8,128)(2,1)} %copy.38), channel_id=1, source_target_pairs={{0,8},{8,0},{1,9},{9,1},{2,10},{10,2},{3,11},{11,3},{4,12},{12,4},... | collective-permute-start | bytes 3145736 | tf_op jit(solution)/shard_map/ppermute | solution.py:89
  64.3 0.7 copy-start.1
  67.9 4.0 %copy-start.2 = (bf16[40,24,64]{2,0,1:T(8,128)(2,1)S(1)}, bf16[40,24,64]{2,0,1:T(8,128)(2,1)}, u32[]{:S(2)}) copy-start(bf16[40,24,64]{2,0,1:T(8,128)(2,1)} %copy-done.1) | copy-start | bytes 368644
  68.6 8.2 %all-to-all-start.2 = ((bf16[4,24,768]{2,1,0:T(8,128)(2,1)}), bf16[4,24,768]{2,1,0:T(8,128)(2,1)S(1)}, u32[]{:S(2)}, u32[]{:S(2)}) async-start(bf16[4,24,768]{2,1,0:T(8,128)(2,1)} %pad_maximum_fusion.2), calls=%async_computation.2 | async-start | bytes 294912 | tf_op jit(solution)/shard_map/all_to_all | solution.py:22
  88.6 0.6 copy-start.4
  89.2 0.7 slice-start
  90.5 13.1 %all-to-all-start.4 = ((bf16[8,8,512]{2,1,0:T(8,128)(2,1)}), bf16[8,8,512]{2,1,0:T(8,128)(2,1)S(1)}, u32[]{:S(2)}, u32[]{:S(2)}) async-start(bf16[8,8,512]{2,1,0:T(8,128)(2,1)} %pad_maximum_fusion.4), calls=%async_computation.4 | async-start | bytes 131072 | tf_op jit(solution)/shard_map/all_to_all | solution.py:22
  103.6 0.7 copy-start.6

commit v5 on v4

--- a/solution.py
+++ b/solution.py
@@ -1,6 +1,8 @@
 import jax
 import jax.numpy as jnp
 from jax import lax
+from jax.experimental import pallas as pl
+from jax.experimental.pallas import tpu as pltpu
 from jax.sharding import Mesh, PartitionSpec as P
 
 RT = 256
@@ -41,6 +43,129 @@
     else:
         target = (c ^ flip) * 128 + x * 32 + low
     return (target == j).astype(BF16)
+
+
+def dot(a, b):
+    return jnp.dot(a, b, preferred_element_type=F32)
+
+
+def dot_t(a, b):
+    return lax.dot_general(a, b, (((1,), (1,)), ((), ())), preferred_element_type=F32)
+
+
+def same(shape, left, right):
+    return lax.broadcasted_iota(jnp.int32, shape, 0) // left == (
+        lax.broadcasted_iota(jnp.int32, shape, 1) // right
+    )
+
+
+def middle_kernel(
+    zh_ref, own_ref, other_ref, tex_ref, order_ref, seen_ref, factor_ref, high_ref, low_ref,
+    blocks_ref, view_ref,
+):
+    sub = 8
+    nx, ny, nzh = SIZES[0], SIZES[3], SIZES[4]
+    pairs, both, width = own_ref.shape
+    near = both // nzh
+    rows = tex_ref.shape[0]
+    band = width // RL
+    groups = rows // sub
+    views = factor_ref.shape[0]
+    factor = factor_ref[...].astype(F32)
+
+    spread_v = jnp.where(same((views * sub, views), sub, 1), 1.0, 0.0).astype(BF16)
+    spread_b = jnp.where(same((RV * sub, RV), sub, 1), 1.0, 0.0).astype(BF16)
+    tall = dot_t(dot(spread_v, factor.astype(BF16)).astype(BF16), spread_b)
+    r = lax.broadcasted_iota(jnp.int32, tall.shape, 0) % sub
+    c = lax.broadcasted_iota(jnp.int32, tall.shape, 1) % sub
+    eye = r == c
+    tall = jnp.where(eye, tall, 0.0).astype(BF16)
+    wide = dot_t(dot_t(spread_b, factor.astype(BF16)).astype(BF16), spread_v)
+    r = lax.broadcasted_iota(jnp.int32, wide.shape, 0) % sub
+    c = lax.broadcasted_iota(jnp.int32, wide.shape, 1) % sub
+    wide = jnp.where(r == c, wide, 0.0).astype(BF16)
+
+    def core_of(g):
+        y, z = g // nzh, g % nzh
+        return jnp.concatenate(
+            [
+                ref[x * ny + y, z * near : (z + 1) * near, :]
+                for ref in (own_ref, other_ref)
+                for x in range(nx)
+            ],
+            axis=0,
+        )
+
+    tex = tex_ref[...]
+    projected = [dot(tex, core_of(g)) for g in range(ny * nzh)]
+    backs, ys, stacks = [], [], []
+    for k in range(groups):
+        stack = jnp.concatenate(
+            [
+                p[k * sub : (k + 1) * sub, b * RL : (b + 1) * RL]
+                for p in projected
+                for b in range(band)
+            ],
+            axis=0,
+        ).astype(BF16)
+        mixed = dot(tall, stack).astype(BF16)
+        fitted = dot(mixed, high_ref[...]) + dot(mixed, low_ref[...])
+        seen = seen_ref[:, k * sub : (k + 1) * sub, :].reshape(views * sub, RL)
+        back = (fitted - seen).astype(BF16)
+        stacks.append(stack)
+        backs.append(back)
+        ys.append(dot(wide, back))
+
+    tex_part = None
+    for g in range(ny * nzh):
+        y_g = jnp.concatenate(
+            [
+                jnp.concatenate(
+                    [y[(g * band + b) * sub : (g * band + b + 1) * sub, :] for b in range(band)],
+                    axis=1,
+                )
+                for y in ys
+            ],
+            axis=0,
+        ).astype(BF16)
+        part = dot_t(y_g, core_of(g))
+        tex_part = part if tex_part is None else tex_part + part
+
+        @pl.when(zh_ref[0] == g % nzh)
+        def _():
+            blocks_ref[g // nzh, :, :width] = y_g
+
+    tex_part = dot_t(tex_part.astype(BF16), order_ref[...]).astype(BF16)
+    for y in range(ny):
+        blocks_ref[y, :, width:] = tex_part
+
+    cross = None
+    for back, stack in zip(backs, stacks):
+        part = dot_t(back, stack)
+        cross = part if cross is None else cross + part
+    cross = jnp.where(eye, cross, 0.0).astype(BF16)
+    cross = lax.dot_general(
+        spread_v, cross, (((0,), (0,)), ((), ())), preferred_element_type=F32
+    )
+    view_ref[...] = dot(cross.astype(BF16), spread_b)
+
+
+def middle(zh, core_own, core_other, tex_rel, order, seen, factor, high, low):
+    rows, views = tex_rel.shape[0], factor.shape[0]
+    ny, width = SIZES[3], core_own.shape[-1]
+    vmem = pl.BlockSpec(memory_space=pltpu.VMEM)
+    return pl.pallas_call(
+        middle_kernel,
+        out_shape=(
+            jax.ShapeDtypeStruct((ny, rows, width + RT), BF16),
+            jax.ShapeDtypeStruct((views, RV), F32),
+        ),
+        in_specs=[pl.BlockSpec(memory_space=pltpu.SMEM)] + [vmem] * 8,
+        out_specs=(vmem, vmem),
+        compiler_params=pltpu.CompilerParams(vmem_limit_bytes=24 << 20),
+        cost_estimate=pl.CostEstimate(flops=10**9, bytes_accessed=3 * 10**6, transcendentals=0),
+        name="middle",
+    )(zh.reshape(1), core_own, core_other, tex_rel, order, seen, factor, high, low)
 
 
 def per_device(measured, view_mask, tex_factor, view_factor, light_factor, core_tensor):
@@ -73,7 +198,7 @@
     both_halves = jnp.concatenate([both_halves[..., :RL], both_halves[..., RL:]], axis=1)
     both_halves = both_halves.reshape(nzh * views, tex_rows + 1, RL)
     seen_all = both_halves[:, :tex_rows].astype(F32)
-    masked_all = both_halves[:, tex_rows].reshape(nzh * views, bands, band)
+    masked_all = both_halves[:, tex_rows]
 
     gram = scaling * lax.dot_general(
         light_factor, light_factor, (((0,), (0,)), ((), ())), preferred_element_type=F32
@@ -85,50 +210,22 @@
     core_bf = core_tensor.astype(BF16).reshape(core_rows, width)
 
     core_z = gather_blocks(core_bf, ("zh", "zl")).reshape(nzh, near, width)
-    core_own = gather_blocks(core_z, ("x", "y")).reshape(nx, ny, nzh, near, width)
+    core_own = gather_blocks(core_z, ("x", "y")).reshape(nx * ny, nzh * near, width)
     core_other = lax.ppermute(core_own, "c", [(0, 1), (1, 0)])
 
     tex_raw = tex_factor.astype(BF16)
     order = lax.optimization_barrier(column_order(lax.axis_index("c")))
     tex_rel = jnp.dot(tex_raw, order, preferred_element_type=F32).astype(BF16)
-    tex_rel = tex_rel.reshape(tex_rows, nc, nx, near)
     tex_abs = jnp.dot(tex_raw, column_order(None), preferred_element_type=F32).astype(BF16)
     tex_rel, tex_abs = lax.optimization_barrier((tex_rel, tex_abs))
 
-    projected = jnp.einsum(
-        "txk,xyzkn->yztn", tex_rel[:, 0], core_own, preferred_element_type=F32
-    ) + jnp.einsum("txk,xyzkn->yztn", tex_rel[:, 1], core_other, preferred_element_type=F32)
-    projected = projected.astype(BF16).reshape(bands, tex_rows, band, RL)
-
-    mixed = jnp.einsum(
-        "vgb,gtbc->vtc", masked_all, projected, preferred_element_type=F32
-    ).astype(BF16)
-    fitted = jnp.einsum("vtc,cd->vtd", mixed, gram_high, preferred_element_type=F32)
-    fitted += jnp.einsum("vtc,cd->vtd", mixed, gram_low, preferred_element_type=F32)
-    back = (fitted - seen_all).astype(BF16)
-
-    partial_y = jnp.einsum("vgb,vtc->gtbc", masked_all, back, preferred_element_type=F32)
-    partial_y = partial_y.astype(BF16).reshape(ny, nzh, tex_rows, width)
-    tex_part = jnp.concatenate(
-        [
-            jnp.einsum("yztn,xyzkn->txk", partial_y, half, preferred_element_type=F32)
-            .astype(BF16)
-            .reshape(tex_rows, nx * near)
-            for half in (core_own, core_other)
-        ],
-        axis=1,
-    )
-    tex_part = lax.dot_general(
-        tex_part, order, (((1,), (1,)), ((), ())), preferred_element_type=F32
-    ).astype(BF16)
-    tex_block = jnp.broadcast_to(tex_part[None], (ny, tex_rows, RT))
-    own_y = jnp.where(zh == 0, partial_y[:, 0], partial_y[:, 1])
-    blocks = jnp.concatenate([own_y, tex_block], axis=2)
+    blocks, view_part = middle(
+        zh, core_own, core_other, tex_rel, order, seen_all, masked_all, gram_high, gram_low
+    )
     blocks = sum_blocks(exchange(blocks, ("y",)))
     summed = blocks[:, :width].astype(BF16)
     grad_tex = scaling * blocks[:, width:]
-    own_back = jnp.where(zh == 0, back[:views], back[views:])
-    view_part = jnp.einsum("vtc,gtbc->vgb", own_back, projected, preferred_element_type=F32)
+    view_part = jnp.where(zh == 0, view_part[:views], view_part[views:])
 
     core_part = jnp.einsum("ta,tn->an", tex_abs, summed, preferred_element_type=F32)
     core_part = core_part.astype(BF16).reshape(nx * nc, near, width)
@@ -137,9 +234,9 @@
     view_part = view_part.reshape(core_rows, width)
     view_block = jnp.broadcast_to(view_part[None], (nx * nc, core_rows, width))
     both = exchange(jnp.concatenate([core_part, view_block], axis=1), ("x", "c"))
-    both = sum_blocks(both).astype(BF16)
-    core_part = both[:near].reshape(nzl, core_rows, width)
-    view_block = jnp.broadcast_to(both[None, near:], (nzl, core_rows, width))
+    core_part = sum_blocks(both[:, :near]).astype(BF16).reshape(nzl, core_rows, width)
+    view_block = sum_blocks(both[:, near:]).astype(BF16)
+    view_block = jnp.broadcast_to(view_block[None], (nzl, core_rows, width))
     both = exchange(jnp.concatenate([core_part, view_block], axis=1), ("zl",))
     both = scaling * sum_blocks(both)
     grad_core = both[:core_rows].reshape(core_tensor.shape)

time: 106 us -> 103 us (0.972)
  Pallas kernels: 0 us -> 5.06 us
  local copies, waits for them, and re-layouts: 8.1 us -> 3.67 us
  matrix products: 5.18 us -> 1.32 us
    pallas_call x0 -> x1, Pallas kernels: none -> 5.06 us  [middle(): pl.pallas_call(middle_kernel, out_shape=(jax.ShapeDtypeStruct((ny, rows,...]
    dot_general x10 -> x0, matrix products: 3.85 us -> none  [the longest x2 1.6 us: per_device(): jnp.einsum('yztn,xyzkn->txk', partial_y, half, preferred_element_type=F32)]
    reshape x7 -> x1, local copies, waits for them, and re-layouts: 1.84 us -> 0.02 us  [per_device(): sum_blocks(both[:, :near]).astype(BF16).reshape(nzl, core_rows, width)]
    unnamed x19 -> x13, local copies, waits for them, and re-layouts: 2.77 us -> 1.38 us
  transfers between devices with their start and end apart: 6 -> 6, of which waited for: 4 -> 4; matrix products, arithmetic and copies ran while one was open for 6% -> 4% of each run, Pallas kernels for 0% -> 0%
where the time goes in v5:
time: 103 us; the launch traced here: 102 us
  starting transfers between devices  46.2 us (45%)
  waiting for transfers between devices  29.4 us (29%)
  blocking collectives  11.3 us (11%)
  Pallas kernels  5.06 us (5%)
  other arithmetic  4.42 us (4%)
  local copies, waits for them, and re-layouts  3.67 us (4%)
  matrix products  1.32 us (1%)
    all_to_all x4, starting transfers between devices, exchange(): return lax.all_to_all(x, axes, 0, 0, tiled=True)  29.3 us
    all_to_all x4, waiting for transfers between devices, exchange(): return lax.all_to_all(x, axes, 0, 0, tiled=True)  28.2 us
    ppermute x1, starting transfers between devices, per_device(): came = lax.ppermute(sent, 'zh', [(0, 1), (1, 0)])  12 us
    all_to_all x1, blocking collectives, exchange(): return lax.all_to_all(x, axes, 0, 0, tiled=True)  11.3 us
    pallas_call x1, Pallas kernels, middle(): pl.pallas_call(middle_kernel, out_shape=(jax.ShapeDtypeStruct((ny, rows,...  5.06 us
    ppermute x1, starting transfers between devices, per_device(): core_other = lax.ppermute(core_own, 'c', [(0, 1), (1, 0)])  4.91 us
  transfers between devices with their start and end apart: 6, of which 4 were waited for; matrix products, arithmetic and copies ran while one was open for 4% of the time, Pallas kernels for 0%

profile of v5, /device:TPU:1, one launch (start us, length us, event | category | flops | bytes accessed | tf_op | source)
XLA Modules:
  0.0 102.3 jit_solution(4764882444349451945)
XLA Ops:
  0.6 0.8 convert_element_type.59
  1.4 0.1 broadcast_in_dim.32
  1.5 0.6 broadcast_in_dim.33
  2.1 15.9 %all-to-all-start = ((bf16[16,4,512]{2,1,0:T(4,128)(2,1)}), bf16[16,4,512]{2,1,0:T(4,128)(2,1)S(1)}, u32[]{:S(2)}, u32[]{:S(2)}) async-start(bf16[16,4,512]{2,1,0:T(4,128)(2,1)} %broadcast_in_dim.33), calls=%async_computation | async-start | bytes 131072 | tf_op jit(solution)/shard_map/all_to_all | solution.py:24
  18.2 0.6 copy-done.1
  18.8 0.2 fusion
  19.0 0.1 fusion.29
  19.1 12.0 %collective-permute-start.1 = (bf16[10,25,128]{2,1,0:T(8,128)(2,1)S(1)}, bf16[10,25,128]{2,1,0:T(8,128)(2,1)S(1)}, u32[]{:S(2)}, u32[]{:S(2)}) collective-permute-start(bf16[10,25,128]{2,1,0:T(8,128)(2,1)S(1)} %fusion.29), channel_id=1, source_target_pairs={{0,1},{1,0},{2,3},{3,2},{4,5},{5,4},{6,7},{7,6},{8,9},{9,8},{10,11... | collective-permute-start | bytes 192008 | tf_op jit(solution)/shard_map/ppermute | solution.py:194
  31.2 1.1 %broadcast_in_dim.35 = bf16[16,2,32,512]{3,2,1,0:T(8,128)(2,1)} broadcast(bf16[2,32,512]{2,1,0:T(8,128)(2,1)S(1)} %broadcast_in_dim.34), dimensions={1,2,3} | broadcast | bytes 1114112 | tf_op jit(solution)/shard_map/broadcast_in_dim | solution.py:29
  32.3 6.8 %all-to-all-start.1 = ((bf16[16,2,32,512]{3,2,1,0:T(8,128)(2,1)}), bf16[16,2,32,512]{3,2,1,0:T(8,128)(2,1)S(1)}, u32[]{:S(2)}, u32[]{:S(2)}) async-start(bf16[16,2,32,512]{3,2,1,0:T(8,128)(2,1)} %broadcast_in_dim.35), calls=%async_computation.1 | async-start | bytes 2097152 | tf_op jit(solution)/shard_map/all_to_all | solution.py:24
  39.1 0.6 fusion.13.order_ref
  39.8 0.1 copy-done.2
  39.8 0.1 fusion.1.tex_ref
  40.0 14.3 %all-to-all-done.1 = bf16[16,2,32,512]{3,2,1,0:T(8,128)(2,1)S(1)} async-done(((bf16[16,2,32,512]{3,2,1,0:T(8,128)(2,1)}), bf16[16,2,32,512]{3,2,1,0:T(8,128)(2,1)S(1)}, u32[]{:S(2)}, u32[]{:S(2)}) %all-to-all-start.1) | async-done | bytes 1048608 | tf_op jit(solution)/shard_map/all_to_all | solution.py:24
  54.3 4.9 %collective-permute-start = (bf16[16,64,512]{2,1,0:T(8,128)(2,1)S(1)}, bf16[16,64,512]{2,1,0:T(8,128)(2,1)S(1)}, u32[]{:S(2)}, u32[]{:S(2)}) collective-permute-start(bf16[16,64,512]{2,1,0:T(8,128)(2,1)S(1)} %bitcast.25), channel_id=1, source_target_pairs={{0,8},{8,0},{1,9},{9,1},{2,10},{10,2},{3,11},{11,3},{4,12},{12,4},... | collective-permute-start | bytes 3145736 | tf_op jit(solution)/shard_map/ppermute | solution.py:214
  59.2 0.1 fusion.30
  59.3 0.6 fusion.2
  60.0 0.1 fusion.49
  60.3 1.2 %collective-permute-done.other_ref = bf16[16,64,512]{2,1,0:T(8,128)(2,1)S(1)} collective-permute-done((bf16[16,64,512]{2,1,0:T(8,128)(2,1)S(1)}, bf16[16,64,512]{2,1,0:T(8,128)(2,1)S(1)}, u32[]{:S(2)}, u32[]{:S(2)}) %collective-permute-start) | collective-permute-done | bytes 1048608 | tf_op jit(solution)/shard_map/ppermute | solution.py:214
  61.5 5.1 %middle.1 = (bf16[4,24,768]{2,1,0:T(8,128)(2,1)}, f32[40,64]{1,0:T(8,128)S(1)}) custom-call(s32[1]{0:T(128)} %bitcast.zh_ref, bf16[16,64,512]{2,1,0:T(8,128)(2,1)S(1)} %bitcast.26, bf16[16,64,512]{2,1,0:T(8,128)(2,1)S(1)} %collective-permute-done.other_ref, bf16[24,256]{1,0:T(8,128)(2,1)S(1)} %fusion.1.tex_ref, bf16[256,256]{1,0:T(8,128)(2,1)S(1)} %fusion.13.order_ref, ...), custom_call_target="tpu_custom_call" | custom-call | flops 1000000000 | bytes 3000000 | tf_op jit(solution)/shard_map/middle/pallas_call | solution.py:157
  66.5 3.3 %all-to-all-start.2 = ((bf16[4,24,768]{2,1,0:T(8,128)(2,1)}), bf16[4,24,768]{2,1,0:T(8,128)(2,1)S(1)}, u32[]{:S(2)}, u32[]{:S(2)}) async-start(bf16[4,24,768]{2,1,0:T(8,128)(2,1)} %get-tuple-element.8), calls=%async_computation.2 | async-start | bytes 294912 | tf_op jit(solution)/shard_map/all_to_all | solution.py:24
  69.9 0.1 reshape.41
  70.0 4.8 %all-to-all-done.2 = bf16[4,24,768]{2,1,0:T(8,128)(2,1)S(1)} async-done(((bf16[4,24,768]{2,1,0:T(8,128)(2,1)}), bf16[4,24,768]{2,1,0:T(8,128)(2,1)S(1)}, u32[]{:S(2)}, u32[]{:S(2)}) %all-to-all-start.2) | async-done | bytes 147488 | tf_op jit(solution)/shard_map/all_to_all | solution.py:24
  74.8 0.2 convolution_convert_fusion
  75.1 11.3 %all_to_all.25 = bf16[8,36,512]{2,1,0:T(8,128)(2,1)S(1)} all-to-all(bf16[8,36,512]{2,1,0:T(8,128)(2,1)S(1)} %pad_maximum_fusion.1), channel_id=1, replica_groups=mesh['x'=4,'zl'=8,'c'=2,'y'=4,'zh'=2] {'x','c'}, dimensions={0} | all-to-all | bytes 589824 | tf_op jit(solution)/shard_map/all_to_all | solution.py:24
  86.6 0.7 pad_maximum_fusion.3
  87.2 3.3 %all-to-all-start.4 = ((bf16[8,8,512]{2,1,0:T(8,128)(2,1)}), bf16[8,8,512]{2,1,0:T(8,128)(2,1)S(1)}, u32[]{:S(2)}, u32[]{:S(2)}) async-start(bf16[8,8,512]{2,1,0:T(8,128)(2,1)} %pad_maximum_fusion.3), calls=%async_computation.4 | async-start | bytes 131072 | tf_op jit(solution)/shard_map/all_to_all | solution.py:24
  90.6 0.6 fusion.32
  91.2 9.1 %all-to-all-done.4 = bf16[8,8,512]{2,1,0:T(8,128)(2,1)S(1)} async-done(((bf16[8,8,512]{2,1,0:T(8,128)(2,1)}), bf16[8,8,512]{2,1,0:T(8,128)(2,1)S(1)}, u32[]{:S(2)}, u32[]{:S(2)}) %all-to-all-start.4) | async-done | bytes 65568 | tf_op jit(solution)/shard_map/all_to_all | solution.py:24
  100.4 0.6 copy-done.3
  101.1 0.6 sub.47
  101.7 0.6 fusion.33
  (42 shorter events, 0.7 us)
Async XLA Ops:
  0.6 17.5 %copy-start = (bf16[24,20,151]{2,0,1:T(8,128)(2,1)S(1)}, bf16[24,20,151]{2,0,1:T(8,128)(2,1)}, u32[]{:S(2)}) copy-start(bf16[24,20,151]{2,0,1:T(8,128)(2,1)} %param.6) | copy-start | bytes 434884
  2.1 15.9 %copy-start.5 = (s32[20]{0:T(128)S(1)}, s32[20]{0:T(128)}, u32[]{:S(2)}) copy-start(s32[20]{0:T(128)} %param.7) | copy-start | bytes 244
  2.1 15.9 %copy-start.4 = (f32[20,64]{1,0:T(8,128)S(1)}, f32[20,64]{1,0:T(8,128)}, u32[]{:S(2)}) copy-start(f32[20,64]{1,0:T(8,128)} %param.9) | copy-start | bytes 15364
  2.1 29.0 %all-to-all-start = ((bf16[16,4,512]{2,1,0:T(4,128)(2,1)}), bf16[16,4,512]{2,1,0:T(4,128)(2,1)S(1)}, u32[]{:S(2)}, u32[]{:S(2)}) async-start(bf16[16,4,512]{2,1,0:T(4,128)(2,1)} %broadcast_in_dim.33), calls=%async_computation | async-start | bytes 131072 | tf_op jit(solution)/shard_map/all_to_all | solution.py:24
  18.0 0.8 copy-start.1
  19.1 40.8 %collective-permute-start.1 = (bf16[10,25,128]{2,1,0:T(8,128)(2,1)S(1)}, bf16[10,25,128]{2,1,0:T(8,128)(2,1)S(1)}, u32[]{:S(2)}, u32[]{:S(2)}) collective-permute-start(bf16[10,25,128]{2,1,0:T(8,128)(2,1)S(1)} %fusion.29), channel_id=1, source_target_pairs={{0,1},{1,0},{2,3},{3,2},{4,5},{5,4},{6,7},{7,6},{8,9},{9,8},{10,11... | collective-permute-start | bytes 192008 | tf_op jit(solution)/shard_map/ppermute | solution.py:194
  32.3 22.0 %all-to-all-start.1 = ((bf16[16,2,32,512]{3,2,1,0:T(8,128)(2,1)}), bf16[16,2,32,512]{3,2,1,0:T(8,128)(2,1)S(1)}, u32[]{:S(2)}, u32[]{:S(2)}) async-start(bf16[16,2,32,512]{3,2,1,0:T(8,128)(2,1)} %broadcast_in_dim.35), calls=%async_computation.1 | async-start | bytes 2097152 | tf_op jit(solution)/shard_map/all_to_all | solution.py:24
  39.1 0.7 copy-start.2
  54.3 7.2 %collective-permute-start = (bf16[16,64,512]{2,1,0:T(8,128)(2,1)S(1)}, bf16[16,64,512]{2,1,0:T(8,128)(2,1)S(1)}, u32[]{:S(2)}, u32[]{:S(2)}) collective-permute-start(bf16[16,64,512]{2,1,0:T(8,128)(2,1)S(1)} %bitcast.25), channel_id=1, source_target_pairs={{0,8},{8,0},{1,9},{9,1},{2,10},{10,2},{3,11},{11,3},{4,12},{12,4},... | collective-permute-start | bytes 3145736 | tf_op jit(solution)/shard_map/ppermute | solution.py:214
  66.5 8.3 %all-to-all-start.2 = ((bf16[4,24,768]{2,1,0:T(8,128)(2,1)}), bf16[4,24,768]{2,1,0:T(8,128)(2,1)S(1)}, u32[]{:S(2)}, u32[]{:S(2)}) async-start(bf16[4,24,768]{2,1,0:T(8,128)(2,1)} %get-tuple-element.8), calls=%async_computation.2 | async-start | bytes 294912 | tf_op jit(solution)/shard_map/all_to_all | solution.py:24
  87.2 13.1 %all-to-all-start.4 = ((bf16[8,8,512]{2,1,0:T(8,128)(2,1)}), bf16[8,8,512]{2,1,0:T(8,128)(2,1)S(1)}, u32[]{:S(2)}, u32[]{:S(2)}) async-start(bf16[8,8,512]{2,1,0:T(8,128)(2,1)} %pad_maximum_fusion.3), calls=%async_computation.4 | async-start | bytes 131072 | tf_op jit(solution)/shard_map/all_to_all | solution.py:24
  100.3 0.7 copy-start.3

commit v6 on v5

v6 whole, which is shorter than its diff:
```python
import functools

import jax
import jax.numpy as jnp
from jax import lax
from jax.experimental import pallas as pl
from jax.experimental.pallas import tpu as pltpu
from jax.sharding import Mesh, PartitionSpec as P

RT = 256
RV = 64
RL = 64
VALID = 151
L = 151

F32 = jnp.float32
BF16 = jnp.bfloat16

SIZES = (4, 8, 2, 4, 2)
NAMES = ("x", "zl", "c", "y", "zh")
TEX = ("x", "zl", "c")
VIEW = ("y", "zh")


def exchange(x, axes):
    return lax.all_to_all(x, axes, 0, 0, tiled=True)


def gather_blocks(x, axes):
    count = lax.axis_size(axes)
    return exchange(jnp.broadcast_to(x[None], (count,) + x.shape), axes)


def sum_blocks(x):
    return jnp.sum(x.astype(F32), axis=0)


def column_order(flip):
    i = lax.broadcasted_iota(jnp.int32, (RT, RT), 0)
    j = lax.broadcasted_iota(jnp.int32, (RT, RT), 1)
    x, zl, c, r = i // 64, (i // 8) % 8, (i // 4) % 2, i % 4
    return ((c ^ flip) * 128 + x * 32 + zl * 4 + r == j).astype(BF16)


def dot(a, b):
    return jnp.dot(a, b, preferred_element_type=F32)


def dot_t(a, b):
    return lax.dot_general(a, b, (((1,), (1,)), ((), ())), preferred_element_type=F32)


def same(shape, left, right):
    return lax.broadcasted_iota(jnp.int32, shape, 0) // left == (
        lax.broadcasted_iota(jnp.int32, shape, 1) // right
    )


SUB = 8
PARAMS = pltpu.CompilerParams(vmem_limit_bytes=24 << 20)
IN_VMEM = pl.BlockSpec(memory_space=pltpu.VMEM)
IN_SMEM = pl.BlockSpec(memory_space=pltpu.SMEM)


def core_band(ref, g):
    nx, ny, nzh = SIZES[0], SIZES[3], SIZES[4]
    near = ref.shape[1] // nzh
    y, z = g // nzh, g % nzh
    return [ref[x * ny + y, z * near : (z + 1) * near, :] for x in range(nx)]


def spread(n):
    return jnp.where(same((n * SUB, n), SUB, 1), 1.0, 0.0).astype(BF16)


def first_kernel(own_ref, tex_ref, factor_ref, part_ref, tall_ref, wide_ref):
    factor = factor_ref[...]
    views = factor.shape[0]
    half = tex_ref.shape[1] // 2
    tex = tex_ref[:, :half]
    for g in range(part_ref.shape[0]):
        part_ref[g] = dot(tex, jnp.concatenate(core_band(own_ref, g), axis=0))
    spread_v, spread_b = spread(views), spread(RV)
    tall = dot_t(dot(spread_v, factor).astype(BF16), spread_b)
    wide = dot_t(dot_t(spread_b, factor).astype(BF16), spread_v)
    for full, ref in ((tall, tall_ref), (wide, wide_ref)):
        r = lax.broadcasted_iota(jnp.int32, full.shape, 0) % SUB
        c = lax.broadcasted_iota(jnp.int32, full.shape, 1) % SUB
        ref[...] = jnp.where(r == c, full, 0.0).astype(BF16)


def second_kernel(
    zh_ref, own_ref, other_ref, part_ref, tall_ref, wide_ref, tex_ref, order_ref, seen_ref,
    high_ref, low_ref, blocks_ref, view_ref,
):
    ny, nzh = SIZES[3], SIZES[4]
    bands, rows, width = part_ref.shape
    band = width // RL
    views = seen_ref.shape[0]
    half = tex_ref.shape[1] // 2
    tex = tex_ref[:, half:]
    tall, wide = tall_ref[...], wide_ref[...]

    projected = [
        part_ref[g] + dot(tex, jnp.concatenate(core_band(other_ref, g), axis=0))
        for g in range(bands)
    ]
    backs, ys, stacks = [], [], []
    for k in range(rows // SUB):
        stack = jnp.concatenate(
            [
                p[k * SUB : (k + 1) * SUB, b * RL : (b + 1) * RL]
                for p in projected
                for b in range(band)
            ],
            axis=0,
        ).astype(BF16)
        mixed = dot(tall, stack).astype(BF16)
        fitted = dot(mixed, high_ref[...]) + dot(mixed, low_ref[...])
        seen = seen_ref[:, k * SUB : (k + 1) * SUB, :].reshape(views * SUB, RL)
        back = (fitted - seen).astype(BF16)
        stacks.append(stack)
        backs.append(back)
        ys.append(dot(wide, back))

    tex_part = None
    for g in range(bands):
        y_g = jnp.concatenate(
            [
                jnp.concatenate(
                    [y[(g * band + b) * SUB : (g * band + b + 1) * SUB, :] for b in range(band)],
                    axis=1,
                )
                for y in ys
            ],
            axis=0,
        ).astype(BF16)
        core = jnp.concatenate(core_band(own_ref, g) + core_band(other_ref, g), axis=0)
        part = dot_t(y_g, core)
        tex_part = part if tex_part is None else tex_part + part

        @pl.when(zh_ref[0] == g % nzh)
        def _():
            blocks_ref[g // nzh, :, :width] = y_g

    tex_part = dot_t(tex_part.astype(BF16), order_ref[...]).astype(BF16)
    for y in range(ny):
        blocks_ref[y, :, width:] = tex_part

    cross = None
    for back, stack in zip(backs, stacks):
        part = dot_t(back, stack)
        cross = part if cross is None else cross + part
    r = lax.broadcasted_iota(jnp.int32, cross.shape, 0) % SUB
    c = lax.broadcasted_iota(jnp.int32, cross.shape, 1) % SUB
    cross = jnp.where(r == c, cross, 0.0).astype(BF16)
    cross = lax.dot_general(
        spread(views), cross, (((0,), (0,)), ((), ())), preferred_element_type=F32
    )
    view_part = dot(cross.astype(BF16), spread(RV))
    height = view_ref.shape[0]
    count = views // nzh
    for z in range(nzh):

        @pl.when(zh_ref[0] == z)
        def _():
            view_ref[...] = jnp.concatenate(
                [
                    view_part[z * count + v : z * count + v + height, :]
                    for v in range(0, count, height)
                ]
                + [jnp.zeros((height, width - count // height * RL), F32)],
                axis=1,
            ).astype(BF16)


def middle(zh, core_own, core_other, tex_rel, order, seen, factor, high, low, height):
    rows, views = tex_rel.shape[0], factor.shape[0]
    ny, nzh, width = SIZES[3], SIZES[4], core_own.shape[-1]
    part, tall, wide = pl.pallas_call(
        first_kernel,
        out_shape=(
            jax.ShapeDtypeStruct((ny * nzh, rows, width), F32),
            jax.ShapeDtypeStruct((views * SUB, RV * SUB), BF16),
            jax.ShapeDtypeStruct((RV * SUB, views * SUB), BF16),
        ),
        in_specs=[IN_VMEM] * 3,
        out_specs=(IN_VMEM,) * 3,
        compiler_params=PARAMS,
        cost_estimate=pl.CostEstimate(flops=10**9, bytes_accessed=2 * 10**6, transcendentals=0),
        name="first",
    )(core_own, tex_rel, factor)
    return pl.pallas_call(
        second_kernel,
        out_shape=(
            jax.ShapeDtypeStruct((ny, rows, width + RT), BF16),
            jax.ShapeDtypeStruct((height, width), BF16),
        ),
        in_specs=[IN_SMEM] + [IN_VMEM] * 10,
        out_specs=(IN_VMEM, IN_VMEM),
        compiler_params=PARAMS,
        cost_estimate=pl.CostEstimate(flops=10**9, bytes_accessed=3 * 10**6, transcendentals=0),
        name="second",
    )(zh.reshape(1), core_own, core_other, part, tall, wide, tex_rel, order, seen, high, low)


def last_kernel(
    rates, sums_ref, blocks_ref, tex_ref, view_ref, core_ref, tex_out, view_out, core_out
):
    rate_tex, rate_view, rate_core = rates
    width = sums_ref.shape[-1]
    height = core_ref.shape[0]
    total = jnp.sum(sums_ref[...].astype(F32), axis=0)
    core_grad, view_grad = rate_core * total[:height], rate_view * total[height:]
    for b in range(core_ref.shape[1]):
        core_out[:, b, :] = core_ref[:, b, :] - core_grad[:, b * RL : (b + 1) * RL]
    for b in range(view_ref.shape[0] // height):
        at = slice(b * height, (b + 1) * height)
        view_out[at, :] = view_ref[at, :] - view_grad[:, b * RV : (b + 1) * RV]
    tex_out[...] = tex_ref[...] - rate_tex * blocks_ref[:, width:]


def last(rates, sums, blocks, tex, view, core):
    return pl.pallas_call(
        functools.partial(last_kernel, rates),
        out_shape=tuple(jax.ShapeDtypeStruct(a.shape, F32) for a in (tex, view, core)),
        in_specs=[IN_VMEM] * 5,
        out_specs=(IN_VMEM,) * 3,
        compiler_params=PARAMS,
        cost_estimate=pl.CostEstimate(flops=10**5, bytes_accessed=10**5, transcendentals=0),
        name="last",
    )(sums, blocks, tex, view, core)


def per_device(measured, view_mask, tex_factor, view_factor, light_factor, core_tensor):
    tex_count = lax.axis_size(TEX)
    tex_rows, views = measured.shape[:2]
    core_rows, band = core_tensor.shape[:2]
    width = band * RL
    texels_all = tex_rows * tex_count
    scaling = (RT * RV * RL) ** (-0.5)
    rate_tex = RT / (VALID * L)
    rate_view = RV / (texels_all * L)
    rate_core = RT * RV * RL / (texels_all * VALID * L)
    nx, nzl, nc, ny, nzh = SIZES
    bands = ny * nzh
    near = nzl * core_rows
    zh = lax.axis_index("zh")
    weights = view_mask.astype(F32)

    seen = jnp.einsum(
        "vtl,lc->vtc", jnp.transpose(measured, (1, 0, 2)), light_factor, preferred_element_type=F32
    )
    seen = (weights[:, None, None] * seen).astype(BF16)
    masked_bf = (weights[:, None] * view_factor).astype(BF16)
    sent = jnp.concatenate([seen, masked_bf[:, None, :]], axis=1)
    sent = jnp.concatenate([sent[: views // 2], sent[views // 2 :]], axis=2)
    came = lax.ppermute(sent, "zh", [(0, 1), (1, 0)])
    both_halves = jnp.where(
        zh == 0, jnp.stack([sent, came]), jnp.stack([came, sent])
    )
    both_halves = jnp.concatenate([both_halves[..., :RL], both_halves[..., RL:]], axis=1)
    both_halves = both_halves.reshape(nzh * views, tex_rows + 1, RL)
    seen_all = both_halves[:, :tex_rows].astype(F32)
    masked_all = both_halves[:, tex_rows]

    gram = scaling * lax.dot_general(
        light_factor, light_factor, (((0,), (0,)), ((), ())), preferred_element_type=F32
    )
    gram_high = lax.reduce_precision(gram, 8, 7)
    gram_low = (gram - gram_high).astype(BF16)
    gram_high = gram_high.astype(BF16)

    core_bf = core_tensor.astype(BF16).reshape(core_rows, width)

    core_z = gather_blocks(core_bf, ("zh", "zl")).reshape(nzh, near, width)
    core_own = gather_blocks(core_z, ("x", "y")).reshape(nx * ny, nzh * near, width)
    core_other = lax.ppermute(core_own, "c", [(0, 1), (1, 0)])

    tex_raw = tex_factor.astype(BF16)
    order = lax.optimization_barrier(column_order(lax.axis_index("c")))
    tex_rel = lax.optimization_barrier(dot(tex_raw, order).astype(BF16))

    blocks, view_part = middle(
        zh, core_own, core_other, tex_rel, order, seen_all, masked_all, gram_high, gram_low,
        core_rows,
    )
    blocks = sum_blocks(exchange(blocks, ("y",)))
    summed = blocks[:, :width].astype(BF16)

    half = RT // nc
    tex_abs = jnp.where(
        lax.axis_index("c") == 0,
        tex_rel,
        jnp.concatenate([tex_rel[:, half:], tex_rel[:, :half]], axis=1),
    )
    core_part = jnp.einsum("ta,tn->an", tex_abs, summed, preferred_element_type=F32)
    core_part = core_part.astype(BF16).reshape(nx * nc, near, width)
    view_block = jnp.broadcast_to(view_part[None], (nx * nc, core_rows, width))
    both = exchange(jnp.concatenate([core_part, view_block], axis=1), ("c", "x"))
    core_part = sum_blocks(both[:, :near]).astype(BF16).reshape(nzl, core_rows, width)
    view_block = sum_blocks(both[:, near:]).astype(BF16)
    view_block = jnp.broadcast_to(view_block[None], (nzl, core_rows, width))
    both = exchange(jnp.concatenate([core_part, view_block], axis=1), ("zl",))
    rates = (scaling * rate_tex, scaling * rate_view, scaling * rate_core)
    return last(rates, both, blocks, tex_factor, view_factor, core_tensor)


def solution(mesh):
    parts = Mesh(mesh.devices.reshape(SIZES), NAMES)
    return jax.shard_map(
        per_device,
        mesh=parts,
        in_specs=(
            P(TEX, VIEW, None),
            P(VIEW),
            P(TEX, None),
            P(VIEW, None),
            P(),
            P(TEX, VIEW, None),
        ),
        out_specs=(P(TEX, None), P(VIEW, None), P(TEX, VIEW, None)),
        check_vma=False,
    )
```

time: 103 us -> 100 us (0.971)
  blocking collectives: 11.3 us -> 25.6 us
  starting transfers between devices: 46.2 us -> 34.9 us
  waiting for transfers between devices: 29.4 us -> 26.4 us
  other arithmetic: 4.42 us -> 1.94 us
  Pallas kernels: 5.06 us -> 6.55 us
    all_to_all x1 -> x2, blocking collectives: 11.3 us -> 25.6 us  [exchange(): return lax.all_to_all(x, axes, 0, 0, tiled=True)]
    ppermute x1, starting transfers between devices: 12 us -> 3.69 us  [per_device(): came = lax.ppermute(sent, 'zh', [(0, 1), (1, 0)])]
    all_to_all x4 -> x3, starting transfers between devices: 29.3 us -> 26 us  [exchange(): return lax.all_to_all(x, axes, 0, 0, tiled=True)]
    all_to_all x4 -> x3, waiting for transfers between devices: 28.2 us -> 25.6 us  [exchange(): return lax.all_to_all(x, axes, 0, 0, tiled=True)]
    sub x3 -> x0, other arithmetic: 1.83 us -> none  [the longest x1 0.61 us: per_device(): tex_factor - rate_tex * grad_tex]
    pallas_call x1 -> x3, Pallas kernels: 5.06 us -> 6.55 us  [the longest x1 5.01 us: middle(): pl.pallas_call(second_kernel, out_shape=(jax.ShapeDtypeStruct((ny, rows,...]
  transfers between devices with their start and end apart: 6 -> 5, of which waited for: 4 -> 4; matrix products, arithmetic and copies ran while one was open for 4% -> 2% of each run, Pallas kernels for 0% -> 1%
where the time goes in v6:
time: 100 us; the launch traced here: 99.8 us
  starting transfers between devices  34.9 us (35%)
  waiting for transfers between devices  26.4 us (26%)
  blocking collectives  25.6 us (26%)
  Pallas kernels  6.55 us (7%)
  local copies, waits for them, and re-layouts  2.7 us (3%)
  other arithmetic  1.94 us (2%)
    all_to_all x3, starting transfers between devices, exchange(): return lax.all_to_all(x, axes, 0, 0, tiled=True)  26 us
    all_to_all x2, blocking collectives, exchange(): return lax.all_to_all(x, axes, 0, 0, tiled=True)  25.6 us
    all_to_all x3, waiting for transfers between devices, exchange(): return lax.all_to_all(x, axes, 0, 0, tiled=True)  25.6 us
    ppermute x1, starting transfers between devices, per_device(): core_other = lax.ppermute(core_own, 'c', [(0, 1), (1, 0)])  5.3 us
    pallas_call x1, Pallas kernels, middle(): pl.pallas_call(second_kernel, out_shape=(jax.ShapeDtypeStruct((ny, rows,...  5.01 us
    ppermute x1, starting transfers between devices, per_device(): came = lax.ppermute(sent, 'zh', [(0, 1), (1, 0)])  3.69 us
  transfers between devices with their start and end apart: 5, of which 4 were waited for; matrix products, arithmetic and copies ran while one was open for 2% of the time, Pallas kernels for 1%

profile of v6, /device:TPU:1, one launch (start us, length us, event | category | flops | bytes accessed | tf_op | source)
XLA Modules:
  0.0 99.8 jit_solution(11820577188874312790)
XLA Ops:
  0.6 0.0 copy-start
  0.6 0.8 convert_element_type.48
  1.4 0.1 broadcast_in_dim.14
  1.5 0.6 broadcast_in_dim.15
  2.1 15.9 %all-to-all-start = ((bf16[16,4,512]{2,1,0:T(4,128)(2,1)}), bf16[16,4,512]{2,1,0:T(4,128)(2,1)S(1)}, u32[]{:S(2)}, u32[]{:S(2)}) async-start(bf16[16,4,512]{2,1,0:T(4,128)(2,1)} %broadcast_in_dim.15), calls=%async_computation | async-start | bytes 131072 | tf_op jit(solution)/shard_map/all_to_all | solution.py:26
  18.0 0.0 copy-start.4
  18.1 0.1 fusion.21
  18.2 0.6 copy-done.4
  18.8 0.2 fusion
  19.0 10.6 %all-to-all-done = bf16[16,4,512]{2,1,0:T(4,128)(2,1)S(1)} async-done(((bf16[16,4,512]{2,1,0:T(4,128)(2,1)}), bf16[16,4,512]{2,1,0:T(4,128)(2,1)S(1)}, u32[]{:S(2)}, u32[]{:S(2)}) %all-to-all-start) | async-done | bytes 65568 | tf_op jit(solution)/shard_map/all_to_all | solution.py:26
  29.6 1.1 %broadcast_in_dim.34 = bf16[16,2,32,512]{3,2,1,0:T(8,128)(2,1)} broadcast(bf16[2,32,512]{2,1,0:T(8,128)(2,1)S(1)} %broadcast_in_dim.16), dimensions={1,2,3} | broadcast | bytes 1114112 | tf_op jit(solution)/shard_map/broadcast_in_dim | solution.py:31
  30.7 6.8 %all-to-all-start.1 = ((bf16[16,2,32,512]{3,2,1,0:T(8,128)(2,1)}), bf16[16,2,32,512]{3,2,1,0:T(8,128)(2,1)S(1)}, u32[]{:S(2)}, u32[]{:S(2)}) async-start(bf16[16,2,32,512]{3,2,1,0:T(8,128)(2,1)} %broadcast_in_dim.34), calls=%async_computation.1 | async-start | bytes 2097152 | tf_op jit(solution)/shard_map/all_to_all | solution.py:26
  37.5 0.1 fusion.14
  37.6 3.7 %collective-permute-start.1 = (bf16[10,25,128]{2,1,0:T(8,128)(2,1)S(1)}, bf16[10,25,128]{2,1,0:T(8,128)(2,1)S(1)}, u32[]{:S(2)}, u32[]{:S(2)}) collective-permute-start(bf16[10,25,128]{2,1,0:T(8,128)(2,1)S(1)} %fusion.14), channel_id=1, source_target_pairs={{0,1},{1,0},{2,3},{3,2},{4,5},{5,4},{6,7},{7,6},{8,9},{9,8},{10,11... | collective-permute-start | bytes 192008 | tf_op jit(solution)/shard_map/ppermute | solution.py:258
  41.3 0.0 copy-start.1
  41.4 0.6 fusion.11.order_ref
  42.0 10.1 %all-to-all-done.1 = bf16[16,2,32,512]{3,2,1,0:T(8,128)(2,1)S(1)} async-done(((bf16[16,2,32,512]{3,2,1,0:T(8,128)(2,1)}), bf16[16,2,32,512]{3,2,1,0:T(8,128)(2,1)S(1)}, u32[]{:S(2)}, u32[]{:S(2)}) %all-to-all-start.1) | async-done | bytes 1048608 | tf_op jit(solution)/shard_map/all_to_all | solution.py:26
  52.1 5.3 %collective-permute-start = (bf16[16,64,512]{2,1,0:T(8,128)(2,1)S(1)}, bf16[16,64,512]{2,1,0:T(8,128)(2,1)S(1)}, u32[]{:S(2)}, u32[]{:S(2)}) collective-permute-start(bf16[16,64,512]{2,1,0:T(8,128)(2,1)S(1)} %bitcast.22), channel_id=1, source_target_pairs={{0,8},{8,0},{1,9},{9,1},{2,10},{10,2},{3,11},{11,3},{4,12},{12,4},... | collective-permute-start | bytes 3145736 | tf_op jit(solution)/shard_map/ppermute | solution.py:278
  57.4 0.1 fusion.1.tex_ref
  57.6 0.2 fusion.15
  57.8 0.1 fusion.27
  57.9 0.1 pad_maximum_fusion
  58.1 0.8 first.1
  58.9 0.8 collective-permute-done.other_ref
  59.7 5.0 %second.1 = (bf16[4,24,768]{2,1,0:T(8,128)(2,1)}, bf16[4,512]{1,0:T(4,128)(2,1)S(1)}) custom-call(s32[1]{0:T(128)} %bitcast.1.zh_ref, bf16[16,64,512]{2,1,0:T(8,128)(2,1)S(1)} %bitcast.24, bf16[16,64,512]{2,1,0:T(8,128)(2,1)S(1)} %collective-permute-done.other_ref, f32[8,24,512]{2,1,0:T(8,128)S(1)} %get-tuple-element.8.part_ref, ...), custom_call_target="tpu_custom_call" | custom-call | flops 1000000000 | bytes 3000000 | tf_op jit(solution)/shard_map/second/pallas_call | solution.py:193
  64.7 3.3 %all-to-all-start.2 = ((bf16[4,24,768]{2,1,0:T(8,128)(2,1)}), bf16[4,24,768]{2,1,0:T(8,128)(2,1)S(1)}, u32[]{:S(2)}, u32[]{:S(2)}) async-start(bf16[4,24,768]{2,1,0:T(8,128)(2,1)} %get-tuple-element.11), calls=%async_computation.2 | async-start | bytes 294912 | tf_op jit(solution)/shard_map/all_to_all | solution.py:26
  68.1 4.9 %all-to-all-done.2 = bf16[4,24,768]{2,1,0:T(8,128)(2,1)S(1)} async-done(((bf16[4,24,768]{2,1,0:T(8,128)(2,1)}), bf16[4,24,768]{2,1,0:T(8,128)(2,1)S(1)}, u32[]{:S(2)}, u32[]{:S(2)}) %all-to-all-start.2) | async-done | bytes 147488 | tf_op jit(solution)/shard_map/all_to_all | solution.py:26
  73.0 0.2 convolution_convert_fusion
  73.3 12.8 %all_to_all.25 = bf16[8,36,512]{2,1,0:T(8,128)(2,1)S(1)} all-to-all(bf16[8,36,512]{2,1,0:T(8,128)(2,1)S(1)} %pad_maximum_fusion.1), channel_id=1, replica_groups=mesh['x'=4,'zl'=8,'c'=2,'y'=4,'zh'=2] {'c','x'}, dimensions={0} | all-to-all | bytes 589824 | tf_op jit(solution)/shard_map/all_to_all | solution.py:26
  86.2 0.0 copy-start.2
  86.3 12.8 %all_to_all.26.sums_ref = bf16[8,8,512]{2,1,0:T(8,128)(2,1)S(1)} all-to-all(bf16[8,8,512]{2,1,0:T(8,128)(2,1)S(1)} %pad_maximum_fusion.3), channel_id=1, replica_groups=mesh['x'=4,'zl'=8,'c'=2,'y'=4,'zh'=2] {'zl'}, dimensions={0} | all-to-all | bytes 131072 | tf_op jit(solution)/shard_map/all_to_all | solution.py:26
  99.1 0.8 last.1
  (31 shorter events, 0.4 us)
Async XLA Ops:
  0.6 17.5 %copy-start = (bf16[24,20,151]{2,0,1:T(8,128)(2,1)S(1)}, bf16[24,20,151]{2,0,1:T(8,128)(2,1)}, u32[]{:S(2)}) copy-start(bf16[24,20,151]{2,0,1:T(8,128)(2,1)} %param.6) | copy-start | bytes 434884
  2.1 15.9 %copy-start.5 = (s32[20]{0:T(128)S(1)}, s32[20]{0:T(128)}, u32[]{:S(2)}) copy-start(s32[20]{0:T(128)} %param.7) | copy-start | bytes 244
  2.1 15.9 %copy-start.3 = (f32[20,64]{1,0:T(8,128)S(1)}, f32[20,64]{1,0:T(8,128)}, u32[]{:S(2)}) copy-start(f32[20,64]{1,0:T(8,128)} %view_ref.1) | copy-start | bytes 15364
  2.1 27.4 %all-to-all-start = ((bf16[16,4,512]{2,1,0:T(4,128)(2,1)}), bf16[16,4,512]{2,1,0:T(4,128)(2,1)S(1)}, u32[]{:S(2)}, u32[]{:S(2)}) async-start(bf16[16,4,512]{2,1,0:T(4,128)(2,1)} %broadcast_in_dim.15), calls=%async_computation | async-start | bytes 131072 | tf_op jit(solution)/shard_map/all_to_all | solution.py:26
  18.0 0.8 copy-start.4
  30.7 21.4 %all-to-all-start.1 = ((bf16[16,2,32,512]{3,2,1,0:T(8,128)(2,1)}), bf16[16,2,32,512]{3,2,1,0:T(8,128)(2,1)S(1)}, u32[]{:S(2)}, u32[]{:S(2)}) async-start(bf16[16,2,32,512]{3,2,1,0:T(8,128)(2,1)} %broadcast_in_dim.34), calls=%async_computation.1 | async-start | bytes 2097152 | tf_op jit(solution)/shard_map/all_to_all | solution.py:26
  37.6 20.2 %collective-permute-start.1 = (bf16[10,25,128]{2,1,0:T(8,128)(2,1)S(1)}, bf16[10,25,128]{2,1,0:T(8,128)(2,1)S(1)}, u32[]{:S(2)}, u32[]{:S(2)}) collective-permute-start(bf16[10,25,128]{2,1,0:T(8,128)(2,1)S(1)} %fusion.14), channel_id=1, source_target_pairs={{0,1},{1,0},{2,3},{3,2},{4,5},{5,4},{6,7},{7,6},{8,9},{9,8},{10,11... | collective-permute-start | bytes 192008 | tf_op jit(solution)/shard_map/ppermute | solution.py:258
  41.3 16.1 %copy-start.1 = (f32[24,256]{1,0:T(8,128)S(1)}, f32[24,256]{1,0:T(8,128)}, u32[]{:S(2)}) copy-start(f32[24,256]{1,0:T(8,128)} %tex_ref.1) | copy-start | bytes 73732
  52.1 7.6 %collective-permute-start = (bf16[16,64,512]{2,1,0:T(8,128)(2,1)S(1)}, bf16[16,64,512]{2,1,0:T(8,128)(2,1)S(1)}, u32[]{:S(2)}, u32[]{:S(2)}) collective-permute-start(bf16[16,64,512]{2,1,0:T(8,128)(2,1)S(1)} %bitcast.22), channel_id=1, source_target_pairs={{0,8},{8,0},{1,9},{9,1},{2,10},{10,2},{3,11},{11,3},{4,12},{12,4},... | collective-permute-start | bytes 3145736 | tf_op jit(solution)/shard_map/ppermute | solution.py:278
  64.7 8.2 %all-to-all-start.2 = ((bf16[4,24,768]{2,1,0:T(8,128)(2,1)}), bf16[4,24,768]{2,1,0:T(8,128)(2,1)S(1)}, u32[]{:S(2)}, u32[]{:S(2)}) async-start(bf16[4,24,768]{2,1,0:T(8,128)(2,1)} %get-tuple-element.11), calls=%async_computation.2 | async-start | bytes 294912 | tf_op jit(solution)/shard_map/all_to_all | solution.py:26
  86.2 12.8 %copy-start.2 = (f32[4,8,64]{2,1,0:T(8,128)S(1)}, f32[4,8,64]{2,1,0:T(8,128)}, u32[]{:S(2)}) copy-start(f32[4,8,64]{2,1,0:T(8,128)} %core_ref.1) | copy-start | bytes 24580

commit v7 on v6

--- a/solution.py
+++ b/solution.py
@@ -73,135 +73,184 @@
     return jnp.where(same((n * SUB, n), SUB, 1), 1.0, 0.0).astype(BF16)
 
 
-def first_kernel(own_ref, tex_ref, factor_ref, part_ref, tall_ref, wide_ref):
-    factor = factor_ref[...]
-    views = factor.shape[0]
+def joined(pieces):
+    return jnp.concatenate(pieces, axis=1)
+
+
+def stacked(pieces):
+    return jnp.concatenate(pieces, axis=0)
+
+
+def diagonal(x):
+    r = lax.broadcasted_iota(jnp.int32, x.shape, 0) % SUB
+    c = lax.broadcasted_iota(jnp.int32, x.shape, 1) % SUB
+    return jnp.where(r == c, x, 0.0).astype(BF16)
+
+
+def first_kernel(
+    zh_ref, own_ref, tex_ref, sent_ref, came_ref, high_ref, low_ref,
+    part_ref, tall_ref, wide_ref, seen_ref, high_out, low_out,
+):
+    nzh = SIZES[4]
+    rows = part_ref.shape[1]
+    groups = rows // SUB
     half = tex_ref.shape[1] // 2
     tex = tex_ref[:, :half]
     for g in range(part_ref.shape[0]):
-        part_ref[g] = dot(tex, jnp.concatenate(core_band(own_ref, g), axis=0))
-    spread_v, spread_b = spread(views), spread(RV)
-    tall = dot_t(dot(spread_v, factor).astype(BF16), spread_b)
-    wide = dot_t(dot_t(spread_b, factor).astype(BF16), spread_v)
-    for full, ref in ((tall, tall_ref), (wide, wide_ref)):
-        r = lax.broadcasted_iota(jnp.int32, full.shape, 0) % SUB
-        c = lax.broadcasted_iota(jnp.int32, full.shape, 1) % SUB
-        ref[...] = jnp.where(r == c, full, 0.0).astype(BF16)
+        part_ref[g] = dot(tex, stacked(core_band(own_ref, g)))
+
+    count = sent_ref.shape[0] // (rows + 1)
+    first_half = zh_ref[0] == 0
+    sent, came = sent_ref[...].astype(F32), came_ref[...].astype(F32)
+    factor, at = [], 0
+    for z in range(nzh):
+        side = jnp.where(first_half, sent if z == 0 else came, came if z == 0 else sent)
+        for lane in range(2):
+            lanes = slice(lane * RL, (lane + 1) * RL)
+            for i in range(count):
+                low = i * rows
+                seen_ref[at : at + SUB, :] = joined(
+                    [side[low + k * SUB : low + (k + 1) * SUB, lanes] for k in range(groups)]
+                )
+                at += SUB
+            factor.append(side[count * rows :, lanes])
+    factor = stacked(factor).astype(BF16)
+
+    spread_v, spread_b = spread(factor.shape[0]), spread(RV)
+    tall_ref[...] = diagonal(dot_t(dot(spread_v, factor).astype(BF16), spread_b))
+    wide_ref[...] = diagonal(dot_t(dot_t(spread_b, factor).astype(BF16), spread_v))
+
+    for ref, out in ((high_ref, high_out), (low_ref, low_out)):
+        gram = ref[...]
+        zero = jnp.zeros_like(gram)
+        out[...] = stacked(
+            [joined([gram if i == k else zero for i in range(groups)]) for k in range(groups)]
+        ).astype(BF16)
 
 
 def second_kernel(
     zh_ref, own_ref, other_ref, part_ref, tall_ref, wide_ref, tex_ref, order_ref, seen_ref,
-    high_ref, low_ref, blocks_ref, view_ref,
+    high_ref, low_ref, blocks_ref, back_ref, stack_ref,
 ):
     ny, nzh = SIZES[3], SIZES[4]
     bands, rows, width = part_ref.shape
     band = width // RL
-    views = seen_ref.shape[0]
+    groups = rows // SUB
     half = tex_ref.shape[1] // 2
     tex = tex_ref[:, half:]
-    tall, wide = tall_ref[...], wide_ref[...]
-
-    projected = [
-        part_ref[g] + dot(tex, jnp.concatenate(core_band(other_ref, g), axis=0))
-        for g in range(bands)
-    ]
-    backs, ys, stacks = [], [], []
-    for k in range(rows // SUB):
-        stack = jnp.concatenate(
+
+    pieces = []
+    for g in range(bands):
+        p = part_ref[g] + dot(tex, stacked(core_band(other_ref, g)))
+        for b in range(band):
+            pieces.append(
+                joined(
+                    [
+                        p[k * SUB : (k + 1) * SUB, b * RL : (b + 1) * RL]
+                        for k in range(groups)
+                    ]
+                )
+            )
+    stack = stacked(pieces).astype(BF16)
+    mixed = dot(tall_ref[...], stack).astype(BF16)
+    fitted = dot(mixed, high_ref[...]) + dot(mixed, low_ref[...])
+    back = (fitted - seen_ref[...]).astype(BF16)
+    y = dot(wide_ref[...], back)
+    stack_ref[...] = stack
+    back_ref[...] = back
+
+    first_half = zh_ref[0] == 0
+    tex_part, near = None, None
+    for g in range(bands):
+        y_g = stacked(
             [
-                p[k * SUB : (k + 1) * SUB, b * RL : (b + 1) * RL]
-                for p in projected
-                for b in range(band)
-            ],
-            axis=0,
-        ).astype(BF16)
-        mixed = dot(tall, stack).astype(BF16)
-        fitted = dot(mixed, high_ref[...]) + dot(mixed, low_ref[...])
-        seen = seen_ref[:, k * SUB : (k + 1) * SUB, :].reshape(views * SUB, RL)
-        back = (fitted - seen).astype(BF16)
-        stacks.append(stack)
-        backs.append(back)
-        ys.append(dot(wide, back))
-
-    tex_part = None
-    for g in range(bands):
-        y_g = jnp.concatenate(
-            [
-                jnp.concatenate(
-                    [y[(g * band + b) * SUB : (g * band + b + 1) * SUB, :] for b in range(band)],
-                    axis=1,
+                joined(
+                    [
+                        y[(g * band + b) * SUB : (g * band + b + 1) * SUB, k * RL : (k + 1) * RL]
+                        for b in range(band)
+                    ]
                 )
-                for y in ys
-            ],
-            axis=0,
-        ).astype(BF16)
-        core = jnp.concatenate(core_band(own_ref, g) + core_band(other_ref, g), axis=0)
-        part = dot_t(y_g, core)
+                for k in range(groups)
+            ]
+        )
+        if g % nzh == 0:
+            near = y_g
+        else:
+            blocks_ref[g // nzh, :, :width] = jnp.where(first_half, near, y_g).astype(BF16)
+        core = stacked(core_band(own_ref, g) + core_band(other_ref, g))
+        part = dot_t(y_g.astype(BF16), core)
         tex_part = part if tex_part is None else tex_part + part
 
-        @pl.when(zh_ref[0] == g % nzh)
-        def _():
-            blocks_ref[g // nzh, :, :width] = y_g
-
     tex_part = dot_t(tex_part.astype(BF16), order_ref[...]).astype(BF16)
-    for y in range(ny):
-        blocks_ref[y, :, width:] = tex_part
-
-    cross = None
-    for back, stack in zip(backs, stacks):
-        part = dot_t(back, stack)
-        cross = part if cross is None else cross + part
-    r = lax.broadcasted_iota(jnp.int32, cross.shape, 0) % SUB
-    c = lax.broadcasted_iota(jnp.int32, cross.shape, 1) % SUB
-    cross = jnp.where(r == c, cross, 0.0).astype(BF16)
+    for i in range(ny):
+        blocks_ref[i, :, width:] = tex_part
+
+
+def third_kernel(zh_ref, back_ref, stack_ref, view_ref):
+    height, width = view_ref.shape
+    views = back_ref.shape[0] // SUB
+    cross = diagonal(dot_t(back_ref[...], stack_ref[...]))
     cross = lax.dot_general(
         spread(views), cross, (((0,), (0,)), ((), ())), preferred_element_type=F32
     )
     view_part = dot(cross.astype(BF16), spread(RV))
-    height = view_ref.shape[0]
-    count = views // nzh
-    for z in range(nzh):
-
-        @pl.when(zh_ref[0] == z)
-        def _():
-            view_ref[...] = jnp.concatenate(
-                [
-                    view_part[z * count + v : z * count + v + height, :]
-                    for v in range(0, count, height)
-                ]
-                + [jnp.zeros((height, width - count // height * RL), F32)],
-                axis=1,
-            ).astype(BF16)
-
-
-def middle(zh, core_own, core_other, tex_rel, order, seen, factor, high, low, height):
-    rows, views = tex_rel.shape[0], factor.shape[0]
+    count = views // SIZES[4]
+    own = jnp.where(zh_ref[0] == 0, view_part[:count], view_part[count:])
+    view_ref[...] = joined(
+        [own[v : v + height, :] for v in range(0, count, height)]
+        + [jnp.zeros((height, width - count // height * RL), F32)]
+    ).astype(BF16)
+
+
+def cost(flops):
+    return pl.CostEstimate(flops=flops, bytes_accessed=flops // 500, transcendentals=0)
+
+
+def middle(zh, core_own, core_other, tex_rel, order, sent, came, high, low, height):
+    rows = tex_rel.shape[0]
     ny, nzh, width = SIZES[3], SIZES[4], core_own.shape[-1]
-    part, tall, wide = pl.pallas_call(
+    views = sent.shape[0] // (rows + 1) * 2 * nzh
+    lanes = rows // SUB * RL
+    zh = zh.reshape(1)
+    part, tall, wide, seen, high, low = pl.pallas_call(
         first_kernel,
         out_shape=(
             jax.ShapeDtypeStruct((ny * nzh, rows, width), F32),
             jax.ShapeDtypeStruct((views * SUB, RV * SUB), BF16),
             jax.ShapeDtypeStruct((RV * SUB, views * SUB), BF16),
+            jax.ShapeDtypeStruct((views * SUB, lanes), F32),
+            jax.ShapeDtypeStruct((lanes, lanes), BF16),
+            jax.ShapeDtypeStruct((lanes, lanes), BF16),
         ),
-        in_specs=[IN_VMEM] * 3,
-        out_specs=(IN_VMEM,) * 3,
+        in_specs=[IN_SMEM] + [IN_VMEM] * 6,
+        out_specs=(IN_VMEM,) * 6,
         compiler_params=PARAMS,
-        cost_estimate=pl.CostEstimate(flops=10**9, bytes_accessed=2 * 10**6, transcendentals=0),
+        cost_estimate=cost(10**9),
         name="first",
-    )(core_own, tex_rel, factor)
-    return pl.pallas_call(
+    )(zh, core_own, tex_rel, sent, came, high, low)
+    blocks, back, stack = pl.pallas_call(
         second_kernel,
         out_shape=(
             jax.ShapeDtypeStruct((ny, rows, width + RT), BF16),
-            jax.ShapeDtypeStruct((height, width), BF16),
+            jax.ShapeDtypeStruct((views * SUB, lanes), BF16),
+            jax.ShapeDtypeStruct((RV * SUB, lanes), BF16),
         ),
         in_specs=[IN_SMEM] + [IN_VMEM] * 10,
-        out_specs=(IN_VMEM, IN_VMEM),
+        out_specs=(IN_VMEM,) * 3,
         compiler_params=PARAMS,
-        cost_estimate=pl.CostEstimate(flops=10**9, bytes_accessed=3 * 10**6, transcendentals=0),
+        cost_estimate=cost(2 * 10**9),
         name="second",
-    )(zh.reshape(1), core_own, core_other, part, tall, wide, tex_rel, order, seen, high, low)
+    )(zh, core_own, core_other, part, tall, wide, tex_rel, order, seen, high, low)
+    view = pl.pallas_call(
+        third_kernel,
+        out_shape=jax.ShapeDtypeStruct((height, width), BF16),
+        in_specs=[IN_SMEM] + [IN_VMEM] * 2,
+        out_specs=IN_VMEM,
+        compiler_params=PARAMS,
+        cost_estimate=cost(10**8),
+        name="third",
+    )(zh, back, stack)
+    return blocks, view
 
 
 def last_kernel(
@@ -253,23 +302,19 @@
     )
     seen = (weights[:, None, None] * seen).astype(BF16)
     masked_bf = (weights[:, None] * view_factor).astype(BF16)
-    sent = jnp.concatenate([seen, masked_bf[:, None, :]], axis=1)
-    sent = jnp.concatenate([sent[: views // 2], sent[views // 2 :]], axis=2)
+    sent = jnp.concatenate(
+        [
+            jnp.concatenate([seen[: views // 2], seen[views // 2 :]], axis=2).reshape(-1, 2 * RL),
+            jnp.concatenate([masked_bf[: views // 2], masked_bf[views // 2 :]], axis=1),
+        ]
+    )
     came = lax.ppermute(sent, "zh", [(0, 1), (1, 0)])
-    both_halves = jnp.where(
-        zh == 0, jnp.stack([sent, came]), jnp.stack([came, sent])
-    )
-    both_halves = jnp.concatenate([both_halves[..., :RL], both_halves[..., RL:]], axis=1)
-    both_halves = both_halves.reshape(nzh * views, tex_rows + 1, RL)
-    seen_all = both_halves[:, :tex_rows].astype(F32)
-    masked_all = both_halves[:, tex_rows]
 
     gram = scaling * lax.dot_general(
         light_factor, light_factor, (((0,), (0,)), ((), ())), preferred_element_type=F32
     )
     gram_high = lax.reduce_precision(gram, 8, 7)
-    gram_low = (gram - gram_high).astype(BF16)
-    gram_high = gram_high.astype(BF16)
+    gram_low = gram - gram_high
 
     core_bf = core_tensor.astype(BF16).reshape(core_rows, width)
 
@@ -282,8 +327,7 @@
     tex_rel = lax.optimization_barrier(dot(tex_raw, order).astype(BF16))
 
     blocks, view_part = middle(
-        zh, core_own, core_other, tex_rel, order, seen_all, masked_all, gram_high, gram_low,
-        core_rows,
+        zh, core_own, core_other, tex_rel, order, sent, came, gram_high, gram_low, core_rows
     )
     blocks = sum_blocks(exchange(blocks, ("y",)))
     summed = blocks[:, :width].astype(BF16)

time: 100 us -> 97.5 us (0.975)
  Pallas kernels: 6.55 us -> 4.93 us
    pallas_call x1, Pallas kernels: 5.01 us -> 2.78 us  [middle(): pl.pallas_call(second_kernel, out_shape=(jax.ShapeDtypeStruct((ny, rows,...]
  transfers between devices with their start and end apart: 5 -> 5, of which waited for: 4 -> 4; matrix products, arithmetic and copies ran while one was open for 2% -> 1% of each run, Pallas kernels for 1% -> 1%
where the time goes in v7:
time: 97.5 us; the launch traced here: 96.8 us
  starting transfers between devices  34.9 us (36%)
  waiting for transfers between devices  26 us (27%)
  blocking collectives  24.8 us (25%)
  Pallas kernels  4.93 us (5%)
  local copies, waits for them, and re-layouts  2.65 us (3%)
  other arithmetic  1.84 us (2%)
    all_to_all x3, starting transfers between devices, exchange(): return lax.all_to_all(x, axes, 0, 0, tiled=True)  26 us
    all_to_all x3, waiting for transfers between devices, exchange(): return lax.all_to_all(x, axes, 0, 0, tiled=True)  25.6 us
    all_to_all x2, blocking collectives, exchange(): return lax.all_to_all(x, axes, 0, 0, tiled=True)  24.8 us
    ppermute x1, starting transfers between devices, per_device(): core_other = lax.ppermute(core_own, 'c', [(0, 1), (1, 0)])  5.3 us
    ppermute x1, starting transfers between devices, per_device(): came = lax.ppermute(sent, 'zh', [(0, 1), (1, 0)])  3.68 us
    pallas_call x1, Pallas kernels, middle(): pl.pallas_call(second_kernel, out_shape=(jax.ShapeDtypeStruct((ny, rows,...  2.78 us
  transfers between devices with their start and end apart: 5, of which 4 were waited for; matrix products, arithmetic and copies ran while one was open for 1% of the time, Pallas kernels for 1%

profile of v7, /device:TPU:1, one launch (start us, length us, event | category | flops | bytes accessed | tf_op | source)
XLA Modules:
  0.0 96.8 jit_solution(12940542408756733478)
XLA Ops:
  0.6 0.0 copy-start
  0.6 0.8 convert_element_type.39
  1.4 0.1 broadcast_in_dim.12
  1.5 0.7 broadcast_in_dim.13
  2.2 15.9 %all-to-all-start = ((bf16[16,4,512]{2,1,0:T(4,128)(2,1)}), bf16[16,4,512]{2,1,0:T(4,128)(2,1)S(1)}, u32[]{:S(2)}, u32[]{:S(2)}) async-start(bf16[16,4,512]{2,1,0:T(4,128)(2,1)} %broadcast_in_dim.13), calls=%async_computation | async-start | bytes 131072 | tf_op jit(solution)/shard_map/all_to_all | solution.py:26
  18.1 0.2 fusion
  18.3 11.3 %all-to-all-done = bf16[16,4,512]{2,1,0:T(4,128)(2,1)S(1)} async-done(((bf16[16,4,512]{2,1,0:T(4,128)(2,1)}), bf16[16,4,512]{2,1,0:T(4,128)(2,1)S(1)}, u32[]{:S(2)}, u32[]{:S(2)}) %all-to-all-start) | async-done | bytes 65568 | tf_op jit(solution)/shard_map/all_to_all | solution.py:26
  29.6 1.1 %broadcast_in_dim.15 = bf16[16,2,32,512]{3,2,1,0:T(8,128)(2,1)} broadcast(bf16[2,32,512]{2,1,0:T(8,128)(2,1)S(1)} %broadcast_in_dim.14), dimensions={1,2,3} | broadcast | bytes 1114112 | tf_op jit(solution)/shard_map/broadcast_in_dim | solution.py:31
  30.7 6.8 %all-to-all-start.1 = ((bf16[16,2,32,512]{3,2,1,0:T(8,128)(2,1)}), bf16[16,2,32,512]{3,2,1,0:T(8,128)(2,1)S(1)}, u32[]{:S(2)}, u32[]{:S(2)}) async-start(bf16[16,2,32,512]{3,2,1,0:T(8,128)(2,1)} %broadcast_in_dim.15), calls=%async_computation.1 | async-start | bytes 2097152 | tf_op jit(solution)/shard_map/all_to_all | solution.py:26
  37.5 0.0 copy-start.3
  37.5 0.1 pad_maximum_fusion.2
  37.6 0.6 copy-done.3
  38.2 0.1 multiply_convert_fusion
  38.3 0.1 maximum_maximum_fusion.sent_ref
  38.4 3.7 %collective-permute-start.1 = (bf16[250,128]{1,0:T(8,128)(2,1)S(1)}, bf16[250,128]{1,0:T(8,128)(2,1)S(1)}, u32[]{:S(2)}, u32[]{:S(2)}) collective-permute-start(bf16[250,128]{1,0:T(8,128)(2,1)S(1)} %maximum_maximum_fusion.sent_ref), channel_id=1, source_target_pairs={{0,1},{1,0},{2,3},{3,2},{4,5},{5,4},{6,7},{7,6},{8,9},{9,8},{10,11... | collective-permute-start | bytes 192008 | tf_op jit(solution)/shard_map/ppermute | solution.py:311
  42.1 10.1 %all-to-all-done.1 = bf16[16,2,32,512]{3,2,1,0:T(8,128)(2,1)S(1)} async-done(((bf16[16,2,32,512]{3,2,1,0:T(8,128)(2,1)}), bf16[16,2,32,512]{3,2,1,0:T(8,128)(2,1)S(1)}, u32[]{:S(2)}, u32[]{:S(2)}) %all-to-all-start.1) | async-done | bytes 1048608 | tf_op jit(solution)/shard_map/all_to_all | solution.py:26
  52.1 5.3 %collective-permute-start = (bf16[16,64,512]{2,1,0:T(8,128)(2,1)S(1)}, bf16[16,64,512]{2,1,0:T(8,128)(2,1)S(1)}, u32[]{:S(2)}, u32[]{:S(2)}) collective-permute-start(bf16[16,64,512]{2,1,0:T(8,128)(2,1)S(1)} %bitcast.15), channel_id=1, source_target_pairs={{0,8},{8,0},{1,9},{9,1},{2,10},{10,2},{3,11},{11,3},{4,12},{12,4},... | collective-permute-start | bytes 3145736 | tf_op jit(solution)/shard_map/ppermute | solution.py:323
  57.5 0.6 fusion.11.order_ref
  58.2 0.1 copy-done.1
  58.2 0.1 fusion.1.tex_ref
  58.4 0.1 reduce-precision_subtract_fusion
  58.5 0.0 collective-permute-done.1.came_ref
  58.5 0.8 first.1
  59.3 0.4 collective-permute-done.other_ref
  59.7 2.8 %second.1 = (bf16[4,24,768]{2,1,0:T(8,128)(2,1)}, bf16[320,192]{1,0:T(8,128)(2,1)S(1)}, bf16[512,192]{1,0:T(8,128)(2,1)S(1)}) custom-call(s32[1]{0:T(128)} %bitcast.1.zh_ref, bf16[16,64,512]{2,1,0:T(8,128)(2,1)S(1)} %bitcast.17, bf16[16,64,512]{2,1,0:T(8,128)(2,1)S(1)} %collective-permute-done.other_ref, f32[8,24,512]{2,1,0:T(8,128)S(1)} %get-tuple-element.12.part_ref, ...), custom_call_target="tpu_custom_call" | custom-call | flops 2000000000 | bytes 4000000 | tf_op jit(solution)/shard_map/second/pallas_call | solution.py:231
  62.5 3.3 %all-to-all-start.2 = ((bf16[4,24,768]{2,1,0:T(8,128)(2,1)}), bf16[4,24,768]{2,1,0:T(8,128)(2,1)S(1)}, u32[]{:S(2)}, u32[]{:S(2)}) async-start(bf16[4,24,768]{2,1,0:T(8,128)(2,1)} %get-tuple-element.18), calls=%async_computation.2 | async-start | bytes 294912 | tf_op jit(solution)/shard_map/all_to_all | solution.py:26
  65.9 0.6 third.1
  66.5 4.3 %all-to-all-done.2 = bf16[4,24,768]{2,1,0:T(8,128)(2,1)S(1)} async-done(((bf16[4,24,768]{2,1,0:T(8,128)(2,1)}), bf16[4,24,768]{2,1,0:T(8,128)(2,1)S(1)}, u32[]{:S(2)}, u32[]{:S(2)}) %all-to-all-start.2) | async-done | bytes 147488 | tf_op jit(solution)/shard_map/all_to_all | solution.py:26
  70.8 0.3 convolution_convert_fusion
  71.1 12.4 %all_to_all.25 = bf16[8,36,512]{2,1,0:T(8,128)(2,1)S(1)} all-to-all(bf16[8,36,512]{2,1,0:T(8,128)(2,1)S(1)} %pad_maximum_fusion), channel_id=1, replica_groups=mesh['x'=4,'zl'=8,'c'=2,'y'=4,'zh'=2] {'c','x'}, dimensions={0} | all-to-all | bytes 589824 | tf_op jit(solution)/shard_map/all_to_all | solution.py:26
  83.7 12.4 %all_to_all.26.sums_ref = bf16[8,8,512]{2,1,0:T(8,128)(2,1)S(1)} all-to-all(bf16[8,8,512]{2,1,0:T(8,128)(2,1)S(1)} %pad_maximum_fusion.1), channel_id=1, replica_groups=mesh['x'=4,'zl'=8,'c'=2,'y'=4,'zh'=2] {'zl'}, dimensions={0} | all-to-all | bytes 131072 | tf_op jit(solution)/shard_map/all_to_all | solution.py:26
  96.1 0.8 last.1
  (27 shorter events, 0.3 us)
Async XLA Ops:
  0.6 17.4 %copy-start = (bf16[24,20,151]{2,0,1:T(8,128)(2,1)S(1)}, bf16[24,20,151]{2,0,1:T(8,128)(2,1)}, u32[]{:S(2)}) copy-start(bf16[24,20,151]{2,0,1:T(8,128)(2,1)} %param.6) | copy-start | bytes 434884
  2.2 15.9 %copy-start.5 = (s32[20]{0:T(128)S(1)}, s32[20]{0:T(128)}, u32[]{:S(2)}) copy-start(s32[20]{0:T(128)} %param.7) | copy-start | bytes 244
  2.2 15.9 %copy-start.4 = (bf16[151,64]{0,1:T(8,128)(2,1)S(1)}, bf16[151,64]{0,1:T(8,128)(2,1)}, u32[]{:S(2)}) copy-start(bf16[151,64]{0,1:T(8,128)(2,1)} %param.10) | copy-start | bytes 57988
  2.2 27.4 %all-to-all-start = ((bf16[16,4,512]{2,1,0:T(4,128)(2,1)}), bf16[16,4,512]{2,1,0:T(4,128)(2,1)S(1)}, u32[]{:S(2)}, u32[]{:S(2)}) async-start(bf16[16,4,512]{2,1,0:T(4,128)(2,1)} %broadcast_in_dim.13), calls=%async_computation | async-start | bytes 131072 | tf_op jit(solution)/shard_map/all_to_all | solution.py:26
  30.7 21.4 %all-to-all-start.1 = ((bf16[16,2,32,512]{3,2,1,0:T(8,128)(2,1)}), bf16[16,2,32,512]{3,2,1,0:T(8,128)(2,1)S(1)}, u32[]{:S(2)}, u32[]{:S(2)}) async-start(bf16[16,2,32,512]{3,2,1,0:T(8,128)(2,1)} %broadcast_in_dim.15), calls=%async_computation.1 | async-start | bytes 2097152 | tf_op jit(solution)/shard_map/all_to_all | solution.py:26
  37.5 0.7 copy-start.3
  38.4 20.2 %collective-permute-start.1 = (bf16[250,128]{1,0:T(8,128)(2,1)S(1)}, bf16[250,128]{1,0:T(8,128)(2,1)S(1)}, u32[]{:S(2)}, u32[]{:S(2)}) collective-permute-start(bf16[250,128]{1,0:T(8,128)(2,1)S(1)} %maximum_maximum_fusion.sent_ref), channel_id=1, source_target_pairs={{0,1},{1,0},{2,3},{3,2},{4,5},{5,4},{6,7},{7,6},{8,9},{9,8},{10,11... | collective-permute-start | bytes 192008 | tf_op jit(solution)/shard_map/ppermute | solution.py:311
  52.1 7.6 %collective-permute-start = (bf16[16,64,512]{2,1,0:T(8,128)(2,1)S(1)}, bf16[16,64,512]{2,1,0:T(8,128)(2,1)S(1)}, u32[]{:S(2)}, u32[]{:S(2)}) collective-permute-start(bf16[16,64,512]{2,1,0:T(8,128)(2,1)S(1)} %bitcast.15), channel_id=1, source_target_pairs={{0,8},{8,0},{1,9},{9,1},{2,10},{10,2},{3,11},{11,3},{4,12},{12,4},... | collective-permute-start | bytes 3145736 | tf_op jit(solution)/shard_map/ppermute | solution.py:323
  57.5 0.7 copy-start.1
  62.5 8.2 %all-to-all-start.2 = ((bf16[4,24,768]{2,1,0:T(8,128)(2,1)}), bf16[4,24,768]{2,1,0:T(8,128)(2,1)S(1)}, u32[]{:S(2)}, u32[]{:S(2)}) async-start(bf16[4,24,768]{2,1,0:T(8,128)(2,1)} %get-tuple-element.18), calls=%async_computation.2 | async-start | bytes 294912 | tf_op jit(solution)/shard_map/all_to_all | solution.py:26
  83.6 12.4 %copy-start.2 = (f32[4,8,64]{2,1,0:T(8,128)S(1)}, f32[4,8,64]{2,1,0:T(8,128)}, u32[]{:S(2)}) copy-start(f32[4,8,64]{2,1,0:T(8,128)} %core_ref.1) | copy-start | bytes 24580

commit v8 on v7

--- a/solution.py
+++ b/solution.py
@@ -130,7 +130,7 @@
 
 def second_kernel(
     zh_ref, own_ref, other_ref, part_ref, tall_ref, wide_ref, tex_ref, order_ref, seen_ref,
-    high_ref, low_ref, blocks_ref, back_ref, stack_ref,
+    high_ref, low_ref, blocks_ref, view_ref,
 ):
     ny, nzh = SIZES[3], SIZES[4]
     bands, rows, width = part_ref.shape
@@ -156,8 +156,6 @@
     fitted = dot(mixed, high_ref[...]) + dot(mixed, low_ref[...])
     back = (fitted - seen_ref[...]).astype(BF16)
     y = dot(wide_ref[...], back)
-    stack_ref[...] = stack
-    back_ref[...] = back
 
     first_half = zh_ref[0] == 0
     tex_part, near = None, None
@@ -185,21 +183,21 @@
     for i in range(ny):
         blocks_ref[i, :, width:] = tex_part
 
-
-def third_kernel(zh_ref, back_ref, stack_ref, view_ref):
-    height, width = view_ref.shape
-    views = back_ref.shape[0] // SUB
-    cross = diagonal(dot_t(back_ref[...], stack_ref[...]))
+    height = view_ref.shape[1]
+    views = back.shape[0] // SUB
+    cross = diagonal(dot_t(back, stack))
     cross = lax.dot_general(
         spread(views), cross, (((0,), (0,)), ((), ())), preferred_element_type=F32
     )
     view_part = dot(cross.astype(BF16), spread(RV))
-    count = views // SIZES[4]
-    own = jnp.where(zh_ref[0] == 0, view_part[:count], view_part[count:])
-    view_ref[...] = joined(
+    count = views // nzh
+    own = jnp.where(first_half, view_part[:count], view_part[count:])
+    own = joined(
         [own[v : v + height, :] for v in range(0, count, height)]
         + [jnp.zeros((height, width - count // height * RL), F32)]
     ).astype(BF16)
+    for i in range(view_ref.shape[0]):
+        view_ref[i] = own
 
 
 def cost(flops):
@@ -228,29 +226,18 @@
         cost_estimate=cost(10**9),
         name="first",
     )(zh, core_own, tex_rel, sent, came, high, low)
-    blocks, back, stack = pl.pallas_call(
+    return pl.pallas_call(
         second_kernel,
         out_shape=(
             jax.ShapeDtypeStruct((ny, rows, width + RT), BF16),
-            jax.ShapeDtypeStruct((views * SUB, lanes), BF16),
-            jax.ShapeDtypeStruct((RV * SUB, lanes), BF16),
+            jax.ShapeDtypeStruct((SIZES[0] * SIZES[2], height, width), BF16),
         ),
         in_specs=[IN_SMEM] + [IN_VMEM] * 10,
-        out_specs=(IN_VMEM,) * 3,
+        out_specs=(IN_VMEM,) * 2,
         compiler_params=PARAMS,
         cost_estimate=cost(2 * 10**9),
         name="second",
     )(zh, core_own, core_other, part, tall, wide, tex_rel, order, seen, high, low)
-    view = pl.pallas_call(
-        third_kernel,
-        out_shape=jax.ShapeDtypeStruct((height, width), BF16),
-        in_specs=[IN_SMEM] + [IN_VMEM] * 2,
-        out_specs=IN_VMEM,
-        compiler_params=PARAMS,
-        cost_estimate=cost(10**8),
-        name="third",
-    )(zh, back, stack)
-    return blocks, view
 
 
 def last_kernel(
@@ -295,6 +282,9 @@
     bands = ny * nzh
     near = nzl * core_rows
     zh = lax.axis_index("zh")
+    core_bf = core_tensor.astype(BF16).reshape(core_rows, width)
+
+    core_z = gather_blocks(core_bf, ("zh", "zl")).reshape(nzh, near, width)
     weights = view_mask.astype(F32)
 
     seen = jnp.einsum(
@@ -316,34 +306,31 @@
     gram_high = lax.reduce_precision(gram, 8, 7)
     gram_low = gram - gram_high
 
-    core_bf = core_tensor.astype(BF16).reshape(core_rows, width)
-
-    core_z = gather_blocks(core_bf, ("zh", "zl")).reshape(nzh, near, width)
     core_own = gather_blocks(core_z, ("x", "y")).reshape(nx * ny, nzh * near, width)
     core_other = lax.ppermute(core_own, "c", [(0, 1), (1, 0)])
 
     tex_raw = tex_factor.astype(BF16)
     order = lax.optimization_barrier(column_order(lax.axis_index("c")))
-    tex_rel = lax.optimization_barrier(dot(tex_raw, order).astype(BF16))
-
-    blocks, view_part = middle(
-        zh, core_own, core_other, tex_rel, order, sent, came, gram_high, gram_low, core_rows
-    )
-    blocks = sum_blocks(exchange(blocks, ("y",)))
-    summed = blocks[:, :width].astype(BF16)
-
+    tex_rel = dot(tex_raw, order).astype(BF16)
     half = RT // nc
     tex_abs = jnp.where(
         lax.axis_index("c") == 0,
         tex_rel,
         jnp.concatenate([tex_rel[:, half:], tex_rel[:, :half]], axis=1),
     )
+    tex_rel, tex_abs = lax.optimization_barrier((tex_rel, tex_abs))
+
+    blocks, view_part = middle(
+        zh, core_own, core_other, tex_rel, order, sent, came, gram_high, gram_low, core_rows
+    )
+    blocks = sum_blocks(exchange(blocks, ("y",)))
+    summed = blocks[:, :width].astype(BF16)
+
     core_part = jnp.einsum("ta,tn->an", tex_abs, summed, preferred_element_type=F32)
-    core_part = core_part.astype(BF16).reshape(nx * nc, near, width)
-    view_block = jnp.broadcast_to(view_part[None], (nx * nc, core_rows, width))
-    both = exchange(jnp.concatenate([core_part, view_block], axis=1), ("c", "x"))
-    core_part = sum_blocks(both[:, :near]).astype(BF16).reshape(nzl, core_rows, width)
-    view_block = sum_blocks(both[:, near:]).astype(BF16)
+    core_part = core_part.astype(BF16).reshape(nx * nc, nzl, core_rows, width)
+    both = exchange(jnp.concatenate([core_part, view_part[:, None]], axis=1), ("c", "x"))
+    both = sum_blocks(both).astype(BF16)
+    core_part, view_block = both[:nzl], both[nzl]
     view_block = jnp.broadcast_to(view_block[None], (nzl, core_rows, width))
     both = exchange(jnp.concatenate([core_part, view_block], axis=1), ("zl",))
     rates = (scaling * rate_tex, scaling * rate_view, scaling * rate_core)

time: 97.5 us -> 96.6 us (level)
  blocking collectives: 24.8 us -> 31.9 us
  waiting for transfers between devices: 26 us -> 21.7 us
  starting transfers between devices: 34.9 us -> 31.6 us
    all_to_all x2 -> x3, blocking collectives: 24.8 us -> 31.9 us  [exchange(): return lax.all_to_all(x, axes, 0, 0, tiled=True)]
    all_to_all x3 -> x2, waiting for transfers between devices: 25.6 us -> 21.3 us  [exchange(): return lax.all_to_all(x, axes, 0, 0, tiled=True)]
    all_to_all x3 -> x2, starting transfers between devices: 26 us -> 22.6 us  [exchange(): return lax.all_to_all(x, axes, 0, 0, tiled=True)]
  transfers between devices with their start and end apart: 5 -> 4, of which waited for: 4 -> 3; matrix products, arithmetic and copies ran while one was open for 1% -> 2% of each run, Pallas kernels for 1% -> 1%
where the time goes in v8:
time: 96.6 us; the launch traced here: 95.9 us
  blocking collectives  31.9 us (33%)
  starting transfers between devices  31.6 us (33%)
  waiting for transfers between devices  21.7 us (22%)
  Pallas kernels  4.29 us (4%)
  local copies, waits for them, and re-layouts  2.7 us (3%)
  other arithmetic  2.09 us (2%)
    all_to_all x3, blocking collectives, exchange(): return lax.all_to_all(x, axes, 0, 0, tiled=True)  31.9 us
    all_to_all x2, starting transfers between devices, exchange(): return lax.all_to_all(x, axes, 0, 0, tiled=True)  22.6 us
    all_to_all x2, waiting for transfers between devices, exchange(): return lax.all_to_all(x, axes, 0, 0, tiled=True)  21.3 us
    ppermute x1, starting transfers between devices, per_device(): core_other = lax.ppermute(core_own, 'c', [(0, 1), (1, 0)])  5.3 us
    ppermute x1, starting transfers between devices, per_device(): came = lax.ppermute(sent, 'zh', [(0, 1), (1, 0)])  3.68 us
    pallas_call x1, Pallas kernels, middle(): pl.pallas_call(second_kernel, out_shape=(jax.ShapeDtypeStruct((ny, rows,...  2.76 us
  transfers between devices with their start and end apart: 4, of which 3 were waited for; matrix products, arithmetic and copies ran while one was open for 2% of the time, Pallas kernels for 1%

profile of v8, /device:TPU:1, one launch (start us, length us, event | category | flops | bytes accessed | tf_op | source)
XLA Modules:
  0.0 95.9 jit_solution(17091135134394976844)
XLA Ops:
  0.6 0.0 copy-start
  0.6 0.8 convert_element_type.37
  1.4 0.1 broadcast_in_dim.26
  1.5 0.7 broadcast_in_dim.27
  2.2 15.9 %all-to-all-start = ((bf16[16,4,512]{2,1,0:T(4,128)(2,1)}), bf16[16,4,512]{2,1,0:T(4,128)(2,1)S(1)}, u32[]{:S(2)}, u32[]{:S(2)}) async-start(bf16[16,4,512]{2,1,0:T(4,128)(2,1)} %broadcast_in_dim.27), calls=%async_computation | async-start | bytes 131072 | tf_op jit(solution)/shard_map/all_to_all | solution.py:26
  18.1 0.2 fusion
  18.3 0.0 copy-start.3
  18.3 0.1 pad_maximum_fusion.2
  18.4 0.6 copy-done.3
  19.0 0.1 multiply_convert_fusion
  19.1 10.5 %all-to-all-done = bf16[16,4,512]{2,1,0:T(4,128)(2,1)S(1)} async-done(((bf16[16,4,512]{2,1,0:T(4,128)(2,1)}), bf16[16,4,512]{2,1,0:T(4,128)(2,1)S(1)}, u32[]{:S(2)}, u32[]{:S(2)}) %all-to-all-start) | async-done | bytes 65568 | tf_op jit(solution)/shard_map/all_to_all | solution.py:26
  29.6 1.1 %broadcast_in_dim.29 = bf16[16,2,32,512]{3,2,1,0:T(8,128)(2,1)} broadcast(bf16[2,32,512]{2,1,0:T(8,128)(2,1)S(1)} %broadcast_in_dim.28), dimensions={1,2,3} | broadcast | bytes 1114112 | tf_op jit(solution)/shard_map/broadcast_in_dim | solution.py:31
  30.7 6.8 %all-to-all-start.1 = ((bf16[16,2,32,512]{3,2,1,0:T(8,128)(2,1)}), bf16[16,2,32,512]{3,2,1,0:T(8,128)(2,1)S(1)}, u32[]{:S(2)}, u32[]{:S(2)}) async-start(bf16[16,2,32,512]{3,2,1,0:T(8,128)(2,1)} %broadcast_in_dim.29), calls=%async_computation.1 | async-start | bytes 2097152 | tf_op jit(solution)/shard_map/all_to_all | solution.py:26
  37.5 0.1 maximum_maximum_fusion.sent_ref
  37.6 3.7 %collective-permute-start.1 = (bf16[250,128]{1,0:T(8,128)(2,1)S(1)}, bf16[250,128]{1,0:T(8,128)(2,1)S(1)}, u32[]{:S(2)}, u32[]{:S(2)}) collective-permute-start(bf16[250,128]{1,0:T(8,128)(2,1)S(1)} %maximum_maximum_fusion.sent_ref), channel_id=1, source_target_pairs={{0,1},{1,0},{2,3},{3,2},{4,5},{5,4},{6,7},{7,6},{8,9},{9,8},{10,11... | collective-permute-start | bytes 192008 | tf_op jit(solution)/shard_map/ppermute | solution.py:301
  41.3 10.8 %all-to-all-done.1 = bf16[16,2,32,512]{3,2,1,0:T(8,128)(2,1)S(1)} async-done(((bf16[16,2,32,512]{3,2,1,0:T(8,128)(2,1)}), bf16[16,2,32,512]{3,2,1,0:T(8,128)(2,1)S(1)}, u32[]{:S(2)}, u32[]{:S(2)}) %all-to-all-start.1) | async-done | bytes 1048608 | tf_op jit(solution)/shard_map/all_to_all | solution.py:26
  52.1 5.3 %collective-permute-start = (bf16[16,64,512]{2,1,0:T(8,128)(2,1)S(1)}, bf16[16,64,512]{2,1,0:T(8,128)(2,1)S(1)}, u32[]{:S(2)}, u32[]{:S(2)}) collective-permute-start(bf16[16,64,512]{2,1,0:T(8,128)(2,1)S(1)} %bitcast.20), channel_id=1, source_target_pairs={{0,8},{8,0},{1,9},{9,1},{2,10},{10,2},{3,11},{11,3},{4,12},{12,4},... | collective-permute-start | bytes 3145736 | tf_op jit(solution)/shard_map/ppermute | solution.py:310
  57.5 0.6 fusion.11.order_ref
  58.1 0.1 copy-done.1
  58.2 0.1 fusion.1.tex_ref
  58.3 0.1 reduce-precision_subtract_fusion
  58.5 0.8 first.1
  59.3 0.4 collective-permute-done.other_ref
  59.7 2.8 %second.1 = (bf16[4,24,768]{2,1,0:T(8,128)(2,1)S(1)}, bf16[8,4,512]{2,1,0:T(4,128)(2,1)S(1)}) custom-call(s32[1]{0:T(128)} %bitcast.1.zh_ref, bf16[16,64,512]{2,1,0:T(8,128)(2,1)S(1)} %bitcast.22, bf16[16,64,512]{2,1,0:T(8,128)(2,1)S(1)} %collective-permute-done.other_ref, f32[8,24,512]{2,1,0:T(8,128)S(1)} %get-tuple-element.15.part_ref, ...), custom_call_target="tpu_custom_call" | custom-call | flops 2000000000 | bytes 4000000 | tf_op jit(solution)/shard_map/second/pallas_call | solution.py:229
  62.5 7.3 %all_to_all.25 = bf16[4,24,768]{2,1,0:T(8,128)(2,1)S(1)} all-to-all(bf16[4,24,768]{2,1,0:T(8,128)(2,1)S(1)} %get-tuple-element.21), channel_id=1, replica_groups=mesh['x'=4,'zl'=8,'c'=2,'y'=4,'zh'=2] {'y'}, dimensions={0} | all-to-all | bytes 294912 | tf_op jit(solution)/shard_map/all_to_all | solution.py:26
  69.8 0.2 convolution_convert_fusion
  70.0 0.1 reshape.25
  70.1 0.2 pad_maximum_fusion
  70.3 12.2 %all_to_all.26 = bf16[8,9,4,512]{3,2,1,0:T(4,128)(2,1)S(1)} all-to-all(bf16[8,9,4,512]{3,2,1,0:T(4,128)(2,1)S(1)} %pad_maximum_fusion), channel_id=1, replica_groups=mesh['x'=4,'zl'=8,'c'=2,'y'=4,'zh'=2] {'c','x'}, dimensions={0} | all-to-all | bytes 589824 | tf_op jit(solution)/shard_map/all_to_all | solution.py:26
  82.5 0.1 reduce_sum.22
  82.7 12.4 %all_to_all.27.sums_ref = bf16[8,8,512]{2,1,0:T(8,128)(2,1)S(1)} all-to-all(bf16[8,8,512]{2,1,0:T(8,128)(2,1)S(1)} %pad_maximum_fusion.1), channel_id=1, replica_groups=mesh['x'=4,'zl'=8,'c'=2,'y'=4,'zh'=2] {'zl'}, dimensions={0} | all-to-all | bytes 131072 | tf_op jit(solution)/shard_map/all_to_all | solution.py:26
  95.2 0.8 last.1
  (26 shorter events, 0.2 us)
Async XLA Ops:
  0.6 17.4 %copy-start = (bf16[24,20,151]{2,0,1:T(8,128)(2,1)S(1)}, bf16[24,20,151]{2,0,1:T(8,128)(2,1)}, u32[]{:S(2)}) copy-start(bf16[24,20,151]{2,0,1:T(8,128)(2,1)} %param.6) | copy-start | bytes 434884
  2.2 15.9 %copy-start.5 = (s32[20]{0:T(128)S(1)}, s32[20]{0:T(128)}, u32[]{:S(2)}) copy-start(s32[20]{0:T(128)} %param.7) | copy-start | bytes 244
  2.2 15.9 %copy-start.4 = (bf16[151,64]{0,1:T(8,128)(2,1)S(1)}, bf16[151,64]{0,1:T(8,128)(2,1)}, u32[]{:S(2)}) copy-start(bf16[151,64]{0,1:T(8,128)(2,1)} %param.10) | copy-start | bytes 57988
  2.2 27.4 %all-to-all-start = ((bf16[16,4,512]{2,1,0:T(4,128)(2,1)}), bf16[16,4,512]{2,1,0:T(4,128)(2,1)S(1)}, u32[]{:S(2)}, u32[]{:S(2)}) async-start(bf16[16,4,512]{2,1,0:T(4,128)(2,1)} %broadcast_in_dim.27), calls=%async_computation | async-start | bytes 131072 | tf_op jit(solution)/shard_map/all_to_all | solution.py:26
  18.3 0.7 copy-start.3
  30.7 21.4 %all-to-all-start.1 = ((bf16[16,2,32,512]{3,2,1,0:T(8,128)(2,1)}), bf16[16,2,32,512]{3,2,1,0:T(8,128)(2,1)S(1)}, u32[]{:S(2)}, u32[]{:S(2)}) async-start(bf16[16,2,32,512]{3,2,1,0:T(8,128)(2,1)} %broadcast_in_dim.29), calls=%async_computation.1 | async-start | bytes 2097152 | tf_op jit(solution)/shard_map/all_to_all | solution.py:26
  37.6 20.9 %collective-permute-start.1 = (bf16[250,128]{1,0:T(8,128)(2,1)S(1)}, bf16[250,128]{1,0:T(8,128)(2,1)S(1)}, u32[]{:S(2)}, u32[]{:S(2)}) collective-permute-start(bf16[250,128]{1,0:T(8,128)(2,1)S(1)} %maximum_maximum_fusion.sent_ref), channel_id=1, source_target_pairs={{0,1},{1,0},{2,3},{3,2},{4,5},{5,4},{6,7},{7,6},{8,9},{9,8},{10,11... | collective-permute-start | bytes 192008 | tf_op jit(solution)/shard_map/ppermute | solution.py:301
  52.1 7.6 %collective-permute-start = (bf16[16,64,512]{2,1,0:T(8,128)(2,1)S(1)}, bf16[16,64,512]{2,1,0:T(8,128)(2,1)S(1)}, u32[]{:S(2)}, u32[]{:S(2)}) collective-permute-start(bf16[16,64,512]{2,1,0:T(8,128)(2,1)S(1)} %bitcast.20), channel_id=1, source_target_pairs={{0,8},{8,0},{1,9},{9,1},{2,10},{10,2},{3,11},{11,3},{4,12},{12,4},... | collective-permute-start | bytes 3145736 | tf_op jit(solution)/shard_map/ppermute | solution.py:310
  57.5 0.7 copy-start.1
  82.7 12.4 %copy-start.2 = (f32[4,8,64]{2,1,0:T(8,128)S(1)}, f32[4,8,64]{2,1,0:T(8,128)}, u32[]{:S(2)}) copy-start(f32[4,8,64]{2,1,0:T(8,128)} %core_ref.1) | copy-start | bytes 24580

commit v9 on v8

--- a/solution.py
+++ b/solution.py
@@ -128,11 +128,18 @@
         ).astype(BF16)
 
 
+def keep(x, refs):
+    refs[0][...] = x[:, :128]
+    rest = x[:, 128:]
+    refs[1][...] = joined([rest, jnp.zeros((rest.shape[0], 128 - rest.shape[1]), rest.dtype)])
+
+
 def second_kernel(
     zh_ref, own_ref, other_ref, part_ref, tall_ref, wide_ref, tex_ref, order_ref, seen_ref,
-    high_ref, low_ref, blocks_ref, view_ref,
+    high_ref, low_ref, blocks_ref, view_ref, *kept,
 ):
     ny, nzh = SIZES[3], SIZES[4]
+    back_ref, stack_ref = kept[:2], kept[2:]
     bands, rows, width = part_ref.shape
     band = width // RL
     groups = rows // SUB
@@ -151,14 +158,19 @@
                     ]
                 )
             )
-    stack = stacked(pieces).astype(BF16)
+    stack = stacked(pieces)
+    keep(stack, stack_ref)
+    stack = stack.astype(BF16)
     mixed = dot(tall_ref[...], stack).astype(BF16)
     fitted = dot(mixed, high_ref[...]) + dot(mixed, low_ref[...])
-    back = (fitted - seen_ref[...]).astype(BF16)
+    back = fitted - seen_ref[...]
+    keep(back, back_ref)
+    back = back.astype(BF16)
     y = dot(wide_ref[...], back)
 
     first_half = zh_ref[0] == 0
     tex_part, near = None, None
+    view_part, views = None, back.shape[0] // SUB
     for g in range(bands):
         y_g = stacked(
             [
@@ -179,17 +191,19 @@
         part = dot_t(y_g.astype(BF16), core)
         tex_part = part if tex_part is None else tex_part + part
 
+        for t in range(g, SUB, bands):
+            left, right = (
+                joined([part[pl.ds(t, n, stride=SUB), :] for part in ref]).astype(BF16)
+                for ref, n in ((back_ref, views), (stack_ref, RV))
+            )
+            part = dot_t(left, right)
+            view_part = part if view_part is None else view_part + part
+
     tex_part = dot_t(tex_part.astype(BF16), order_ref[...]).astype(BF16)
     for i in range(ny):
         blocks_ref[i, :, width:] = tex_part
 
     height = view_ref.shape[1]
-    views = back.shape[0] // SUB
-    cross = diagonal(dot_t(back, stack))
-    cross = lax.dot_general(
-        spread(views), cross, (((0,), (0,)), ((), ())), preferred_element_type=F32
-    )
-    view_part = dot(cross.astype(BF16), spread(RV))
     count = views // nzh
     own = jnp.where(first_half, view_part[:count], view_part[count:])
     own = joined(
@@ -234,6 +248,9 @@
         ),
         in_specs=[IN_SMEM] + [IN_VMEM] * 10,
         out_specs=(IN_VMEM,) * 2,
+        scratch_shapes=[
+            pltpu.VMEM((n * SUB, 128), F32) for n in (views, views, RV, RV)
+        ],
         compiler_params=PARAMS,
         cost_estimate=cost(2 * 10**9),
         name="second",
@@ -327,10 +344,10 @@
     summed = blocks[:, :width].astype(BF16)
 
     core_part = jnp.einsum("ta,tn->an", tex_abs, summed, preferred_element_type=F32)
-    core_part = core_part.astype(BF16).reshape(nx * nc, nzl, core_rows, width)
-    both = exchange(jnp.concatenate([core_part, view_part[:, None]], axis=1), ("c", "x"))
-    both = sum_blocks(both).astype(BF16)
-    core_part, view_block = both[:nzl], both[nzl]
+    core_part = core_part.astype(BF16).reshape(nx * nc, near, width)
+    both = exchange(jnp.concatenate([core_part, view_part], axis=1), ("c", "x"))
+    core_part = sum_blocks(both[:, :near]).astype(BF16).reshape(nzl, core_rows, width)
+    view_block = sum_blocks(both[:, near:]).astype(BF16)
     view_block = jnp.broadcast_to(view_block[None], (nzl, core_rows, width))
     both = exchange(jnp.concatenate([core_part, view_block], axis=1), ("zl",))
     rates = (scaling * rate_tex, scaling * rate_view, scaling * rate_core)

time: 96.6 us -> 95.8 us (level)
  no operation moved by 1% of the time
where the time goes in v9:
time: 95.8 us; the launch traced here: 95.2 us
  blocking collectives  32.1 us (34%)
  starting transfers between devices  31.6 us (33%)
  waiting for transfers between devices  21.7 us (23%)
  Pallas kernels  3.65 us (4%)
  local copies, waits for them, and re-layouts  2.62 us (3%)
  other arithmetic  1.86 us (2%)
    all_to_all x3, blocking collectives, exchange(): return lax.all_to_all(x, axes, 0, 0, tiled=True)  32.1 us
    all_to_all x2, starting transfers between devices, exchange(): return lax.all_to_all(x, axes, 0, 0, tiled=True)  22.6 us
    all_to_all x2, waiting for transfers between devices, exchange(): return lax.all_to_all(x, axes, 0, 0, tiled=True)  21.3 us
    ppermute x1, starting transfers between devices, per_device(): core_other = lax.ppermute(core_own, 'c', [(0, 1), (1, 0)])  5.3 us
    ppermute x1, starting transfers between devices, per_device(): came = lax.ppermute(sent, 'zh', [(0, 1), (1, 0)])  3.68 us
    pallas_call x1, Pallas kernels, middle(): pl.pallas_call(second_kernel, out_shape=(jax.ShapeDtypeStruct((ny, rows,...  2.12 us
  transfers between devices with their start and end apart: 4, of which 3 were waited for; matrix products, arithmetic and copies ran while one was open for 2% of the time, Pallas kernels for 1%

profile of v9, /device:TPU:1, one launch (start us, length us, event | category | flops | bytes accessed | tf_op | source)
XLA Modules:
  0.0 95.2 jit_solution(2165961591990717160)
XLA Ops:
  0.6 0.0 copy-start
  0.6 0.8 convert_element_type.39
  1.4 0.1 broadcast_in_dim.10
  1.5 0.6 broadcast_in_dim.11
  2.1 15.9 %all-to-all-start = ((bf16[16,4,512]{2,1,0:T(4,128)(2,1)}), bf16[16,4,512]{2,1,0:T(4,128)(2,1)S(1)}, u32[]{:S(2)}, u32[]{:S(2)}) async-start(bf16[16,4,512]{2,1,0:T(4,128)(2,1)} %broadcast_in_dim.11), calls=%async_computation | async-start | bytes 131072 | tf_op jit(solution)/shard_map/all_to_all | solution.py:26
  18.1 0.2 fusion
  18.3 0.0 copy-start.3
  18.3 0.1 pad_maximum_fusion.2
  18.4 0.6 copy-done.3
  19.0 0.1 multiply_convert_fusion
  19.1 10.5 %all-to-all-done = bf16[16,4,512]{2,1,0:T(4,128)(2,1)S(1)} async-done(((bf16[16,4,512]{2,1,0:T(4,128)(2,1)}), bf16[16,4,512]{2,1,0:T(4,128)(2,1)S(1)}, u32[]{:S(2)}, u32[]{:S(2)}) %all-to-all-start) | async-done | bytes 65568 | tf_op jit(solution)/shard_map/all_to_all | solution.py:26
  29.6 1.1 %broadcast_in_dim.25 = bf16[16,2,32,512]{3,2,1,0:T(8,128)(2,1)} broadcast(bf16[2,32,512]{2,1,0:T(8,128)(2,1)S(1)} %broadcast_in_dim.24), dimensions={1,2,3} | broadcast | bytes 1114112 | tf_op jit(solution)/shard_map/broadcast_in_dim | solution.py:31
  30.7 6.8 %all-to-all-start.1 = ((bf16[16,2,32,512]{3,2,1,0:T(8,128)(2,1)}), bf16[16,2,32,512]{3,2,1,0:T(8,128)(2,1)S(1)}, u32[]{:S(2)}, u32[]{:S(2)}) async-start(bf16[16,2,32,512]{3,2,1,0:T(8,128)(2,1)} %broadcast_in_dim.25), calls=%async_computation.1 | async-start | bytes 2097152 | tf_op jit(solution)/shard_map/all_to_all | solution.py:26
  37.5 0.1 maximum_maximum_fusion.sent_ref
  37.6 3.7 %collective-permute-start.1 = (bf16[250,128]{1,0:T(8,128)(2,1)S(1)}, bf16[250,128]{1,0:T(8,128)(2,1)S(1)}, u32[]{:S(2)}, u32[]{:S(2)}) collective-permute-start(bf16[250,128]{1,0:T(8,128)(2,1)S(1)} %maximum_maximum_fusion.sent_ref), channel_id=1, source_target_pairs={{0,1},{1,0},{2,3},{3,2},{4,5},{5,4},{6,7},{7,6},{8,9},{9,8},{10,11... | collective-permute-start | bytes 192008 | tf_op jit(solution)/shard_map/ppermute | solution.py:318
  41.3 10.8 %all-to-all-done.1 = bf16[16,2,32,512]{3,2,1,0:T(8,128)(2,1)S(1)} async-done(((bf16[16,2,32,512]{3,2,1,0:T(8,128)(2,1)}), bf16[16,2,32,512]{3,2,1,0:T(8,128)(2,1)S(1)}, u32[]{:S(2)}, u32[]{:S(2)}) %all-to-all-start.1) | async-done | bytes 1048608 | tf_op jit(solution)/shard_map/all_to_all | solution.py:26
  52.1 5.3 %collective-permute-start = (bf16[16,64,512]{2,1,0:T(8,128)(2,1)S(1)}, bf16[16,64,512]{2,1,0:T(8,128)(2,1)S(1)}, u32[]{:S(2)}, u32[]{:S(2)}) collective-permute-start(bf16[16,64,512]{2,1,0:T(8,128)(2,1)S(1)} %bitcast.16), channel_id=1, source_target_pairs={{0,8},{8,0},{1,9},{9,1},{2,10},{10,2},{3,11},{11,3},{4,12},{12,4},... | collective-permute-start | bytes 3145736 | tf_op jit(solution)/shard_map/ppermute | solution.py:327
  57.4 0.0 copy-start.1
  57.4 0.6 fusion.11.order_ref
  58.1 0.1 copy-done.1
  58.2 0.1 fusion.1.tex_ref
  58.3 0.1 reduce-precision_subtract_fusion
  58.5 0.0 collective-permute-done.1.came_ref
  58.5 0.8 first.1
  59.3 0.4 collective-permute-done.other_ref
  59.7 2.1 %second.1 = (bf16[4,24,768]{2,1,0:T(8,128)(2,1)S(1)}, bf16[8,4,512]{2,1,0:T(4,128)(2,1)S(1)}) custom-call(s32[1]{0:T(128)} %bitcast.1.zh_ref, bf16[16,64,512]{2,1,0:T(8,128)(2,1)S(1)} %bitcast.18, bf16[16,64,512]{2,1,0:T(8,128)(2,1)S(1)} %collective-permute-done.other_ref, f32[8,24,512]{2,1,0:T(8,128)S(1)} %get-tuple-element.15.part_ref, ...), custom_call_target="tpu_custom_call" | custom-call | flops 2000000000 | bytes 4000000 | tf_op jit(solution)/shard_map/second/pallas_call | solution.py:243
  61.8 7.3 %all_to_all.25 = bf16[4,24,768]{2,1,0:T(8,128)(2,1)S(1)} all-to-all(bf16[4,24,768]{2,1,0:T(8,128)(2,1)S(1)} %get-tuple-element.21), channel_id=1, replica_groups=mesh['x'=4,'zl'=8,'c'=2,'y'=4,'zh'=2] {'y'}, dimensions={0} | all-to-all | bytes 294912 | tf_op jit(solution)/shard_map/all_to_all | solution.py:26
  69.1 0.3 convolution_convert_fusion
  69.4 12.4 %all_to_all.26 = bf16[8,36,512]{2,1,0:T(8,128)(2,1)S(1)} all-to-all(bf16[8,36,512]{2,1,0:T(8,128)(2,1)S(1)} %pad_maximum_fusion), channel_id=1, replica_groups=mesh['x'=4,'zl'=8,'c'=2,'y'=4,'zh'=2] {'c','x'}, dimensions={0} | all-to-all | bytes 589824 | tf_op jit(solution)/shard_map/all_to_all | solution.py:26
  82.0 0.0 copy-start.2
  82.0 12.4 %all_to_all.27.sums_ref = bf16[8,8,512]{2,1,0:T(8,128)(2,1)S(1)} all-to-all(bf16[8,8,512]{2,1,0:T(8,128)(2,1)S(1)} %pad_maximum_fusion.1), channel_id=1, replica_groups=mesh['x'=4,'zl'=8,'c'=2,'y'=4,'zh'=2] {'zl'}, dimensions={0} | all-to-all | bytes 131072 | tf_op jit(solution)/shard_map/all_to_all | solution.py:26
  94.4 0.8 last.1
  (25 shorter events, 0.3 us)
Async XLA Ops:
  0.6 17.4 %copy-start = (bf16[24,20,151]{2,0,1:T(8,128)(2,1)S(1)}, bf16[24,20,151]{2,0,1:T(8,128)(2,1)}, u32[]{:S(2)}) copy-start(bf16[24,20,151]{2,0,1:T(8,128)(2,1)} %param.6) | copy-start | bytes 434884
  2.1 15.9 %copy-start.5 = (s32[20]{0:T(128)S(1)}, s32[20]{0:T(128)}, u32[]{:S(2)}) copy-start(s32[20]{0:T(128)} %param.7) | copy-start | bytes 244
  2.1 15.9 %copy-start.4 = (bf16[151,64]{0,1:T(8,128)(2,1)S(1)}, bf16[151,64]{0,1:T(8,128)(2,1)}, u32[]{:S(2)}) copy-start(bf16[151,64]{0,1:T(8,128)(2,1)} %param.10) | copy-start | bytes 57988
  2.1 27.4 %all-to-all-start = ((bf16[16,4,512]{2,1,0:T(4,128)(2,1)}), bf16[16,4,512]{2,1,0:T(4,128)(2,1)S(1)}, u32[]{:S(2)}, u32[]{:S(2)}) async-start(bf16[16,4,512]{2,1,0:T(4,128)(2,1)} %broadcast_in_dim.11), calls=%async_computation | async-start | bytes 131072 | tf_op jit(solution)/shard_map/all_to_all | solution.py:26
  18.3 0.7 copy-start.3
  30.7 21.4 %all-to-all-start.1 = ((bf16[16,2,32,512]{3,2,1,0:T(8,128)(2,1)}), bf16[16,2,32,512]{3,2,1,0:T(8,128)(2,1)S(1)}, u32[]{:S(2)}, u32[]{:S(2)}) async-start(bf16[16,2,32,512]{3,2,1,0:T(8,128)(2,1)} %broadcast_in_dim.25), calls=%async_computation.1 | async-start | bytes 2097152 | tf_op jit(solution)/shard_map/all_to_all | solution.py:26
  37.6 20.9 %collective-permute-start.1 = (bf16[250,128]{1,0:T(8,128)(2,1)S(1)}, bf16[250,128]{1,0:T(8,128)(2,1)S(1)}, u32[]{:S(2)}, u32[]{:S(2)}) collective-permute-start(bf16[250,128]{1,0:T(8,128)(2,1)S(1)} %maximum_maximum_fusion.sent_ref), channel_id=1, source_target_pairs={{0,1},{1,0},{2,3},{3,2},{4,5},{5,4},{6,7},{7,6},{8,9},{9,8},{10,11... | collective-permute-start | bytes 192008 | tf_op jit(solution)/shard_map/ppermute | solution.py:318
  52.1 7.6 %collective-permute-start = (bf16[16,64,512]{2,1,0:T(8,128)(2,1)S(1)}, bf16[16,64,512]{2,1,0:T(8,128)(2,1)S(1)}, u32[]{:S(2)}, u32[]{:S(2)}) collective-permute-start(bf16[16,64,512]{2,1,0:T(8,128)(2,1)S(1)} %bitcast.16), channel_id=1, source_target_pairs={{0,8},{8,0},{1,9},{9,1},{2,10},{10,2},{3,11},{11,3},{4,12},{12,4},... | collective-permute-start | bytes 3145736 | tf_op jit(solution)/shard_map/ppermute | solution.py:327
  57.4 0.7 copy-start.1
  82.0 12.4 %copy-start.2 = (f32[4,8,64]{2,1,0:T(8,128)S(1)}, f32[4,8,64]{2,1,0:T(8,128)}, u32[]{:S(2)}) copy-start(f32[4,8,64]{2,1,0:T(8,128)} %core_ref.1) | copy-start | bytes 24580

commit v10 on v9

--- a/solution.py
+++ b/solution.py
@@ -85,6 +85,31 @@
     r = lax.broadcasted_iota(jnp.int32, x.shape, 0) % SUB
     c = lax.broadcasted_iota(jnp.int32, x.shape, 1) % SUB
     return jnp.where(r == c, x, 0.0).astype(BF16)
+
+
+def copies_kernel(x_ref, out_ref, sems):
+    moves = [
+        pltpu.make_async_copy(x_ref, out_ref.at[i], sems.at[i]) for i in range(out_ref.shape[0])
+    ]
+    for move in moves:
+        move.start()
+    for move in moves:
+        move.wait()
+
+
+def copies(x, count):
+    return pl.pallas_call(
+        copies_kernel,
+        out_shape=jax.ShapeDtypeStruct((count,) + x.shape, x.dtype),
+        in_specs=[IN_VMEM],
+        out_specs=pl.BlockSpec(memory_space=pl.ANY),
+        scratch_shapes=[pltpu.SemaphoreType.DMA((count,))],
+        compiler_params=PARAMS,
+        cost_estimate=pl.CostEstimate(
+            flops=0, bytes_accessed=(count + 1) * x.size * 2, transcendentals=0
+        ),
+        name="copies",
+    )(x)
 
 
 def first_kernel(
@@ -323,7 +348,7 @@
     gram_high = lax.reduce_precision(gram, 8, 7)
     gram_low = gram - gram_high
 
-    core_own = gather_blocks(core_z, ("x", "y")).reshape(nx * ny, nzh * near, width)
+    core_own = exchange(copies(core_z, nx * ny), ("x", "y")).reshape(nx * ny, nzh * near, width)
     core_other = lax.ppermute(core_own, "c", [(0, 1), (1, 0)])
 
     tex_raw = tex_factor.astype(BF16)

time: 95.8 us -> 95.8 us (level)
  Pallas kernels: 3.65 us -> 4.77 us
  local copies, waits for them, and re-layouts: 2.62 us -> 1.51 us
    pallas_call x0 -> x1, Pallas kernels: none -> 1.12 us  [copies(): pl.pallas_call(copies_kernel, out_shape=jax.ShapeDtypeStruct((count,) + x...]
    broadcast_in_dim x4 -> x2, local copies, waits for them, and re-layouts: 1.85 us -> 0.73 us  [gather_blocks(): return exchange(jnp.broadcast_to(x[None], (count,) + x.shape), axes)]
where the time goes in v10:
time: 95.8 us; the launch traced here: 95.2 us
  blocking collectives  32.1 us (34%)
  starting transfers between devices  31.6 us (33%)
  waiting for transfers between devices  21.7 us (23%)
  Pallas kernels  4.77 us (5%)
  other arithmetic  1.86 us (2%)
  local copies, waits for them, and re-layouts  1.51 us (2%)
    all_to_all x3, blocking collectives, exchange(): return lax.all_to_all(x, axes, 0, 0, tiled=True)  32.1 us
    all_to_all x2, starting transfers between devices, exchange(): return lax.all_to_all(x, axes, 0, 0, tiled=True)  22.6 us
    all_to_all x2, waiting for transfers between devices, exchange(): return lax.all_to_all(x, axes, 0, 0, tiled=True)  21.3 us
    ppermute x1, starting transfers between devices, per_device(): core_other = lax.ppermute(core_own, 'c', [(0, 1), (1, 0)])  5.3 us
    ppermute x1, starting transfers between devices, per_device(): came = lax.ppermute(sent, 'zh', [(0, 1), (1, 0)])  3.68 us
    pallas_call x1, Pallas kernels, middle(): pl.pallas_call(second_kernel, out_shape=(jax.ShapeDtypeStruct((ny, rows,...  2.11 us
  transfers between devices with their start and end apart: 4, of which 3 were waited for; matrix products, arithmetic and copies ran while one was open for 2% of the time, Pallas kernels for 1%

profile of v10, /device:TPU:1, one launch (start us, length us, event | category | flops | bytes accessed | tf_op | source)
XLA Modules:
  0.0 95.2 jit_solution(16843411115521582368)
XLA Ops:
  0.6 0.0 copy-start
  0.6 0.8 convert_element_type.39
  1.4 0.1 broadcast_in_dim.6
  1.5 0.6 broadcast_in_dim.7
  2.1 15.9 %all-to-all-start = ((bf16[16,4,512]{2,1,0:T(4,128)(2,1)}), bf16[16,4,512]{2,1,0:T(4,128)(2,1)S(1)}, u32[]{:S(2)}, u32[]{:S(2)}) async-start(bf16[16,4,512]{2,1,0:T(4,128)(2,1)} %broadcast_in_dim.7), calls=%async_computation | async-start | bytes 131072 | tf_op jit(solution)/shard_map/all_to_all | solution.py:26
  18.1 0.2 fusion
  18.3 0.0 copy-start.3
  18.3 0.1 pad_maximum_fusion.2
  18.4 0.6 copy-done.3
  19.0 0.1 multiply_convert_fusion
  19.1 10.5 %all-to-all-done = bf16[16,4,512]{2,1,0:T(4,128)(2,1)S(1)} async-done(((bf16[16,4,512]{2,1,0:T(4,128)(2,1)}), bf16[16,4,512]{2,1,0:T(4,128)(2,1)S(1)}, u32[]{:S(2)}, u32[]{:S(2)}) %all-to-all-start) | async-done | bytes 65568 | tf_op jit(solution)/shard_map/all_to_all | solution.py:26
  29.6 1.1 %copies.1 = bf16[16,2,32,512]{3,2,1,0:T(8,128)(2,1)} custom-call(bf16[2,32,512]{2,1,0:T(8,128)(2,1)S(1)} %reshape.29.x_ref), custom_call_target="tpu_custom_call" | custom-call | bytes 1114112 | tf_op jit(solution)/shard_map/copies/pallas_call | solution.py:101
  30.7 6.8 %all-to-all-start.1 = ((bf16[16,2,32,512]{3,2,1,0:T(8,128)(2,1)}), bf16[16,2,32,512]{3,2,1,0:T(8,128)(2,1)S(1)}, u32[]{:S(2)}, u32[]{:S(2)}) async-start(bf16[16,2,32,512]{3,2,1,0:T(8,128)(2,1)} %copies.1), calls=%async_computation.1 | async-start | bytes 2097152 | tf_op jit(solution)/shard_map/all_to_all | solution.py:26
  37.5 0.1 maximum_maximum_fusion.sent_ref
  37.6 3.7 %collective-permute-start.1 = (bf16[250,128]{1,0:T(8,128)(2,1)S(1)}, bf16[250,128]{1,0:T(8,128)(2,1)S(1)}, u32[]{:S(2)}, u32[]{:S(2)}) collective-permute-start(bf16[250,128]{1,0:T(8,128)(2,1)S(1)} %maximum_maximum_fusion.sent_ref), channel_id=1, source_target_pairs={{0,1},{1,0},{2,3},{3,2},{4,5},{5,4},{6,7},{7,6},{8,9},{9,8},{10,11... | collective-permute-start | bytes 192008 | tf_op jit(solution)/shard_map/ppermute | solution.py:343
  41.4 10.8 %all-to-all-done.1 = bf16[16,2,32,512]{3,2,1,0:T(8,128)(2,1)S(1)} async-done(((bf16[16,2,32,512]{3,2,1,0:T(8,128)(2,1)}), bf16[16,2,32,512]{3,2,1,0:T(8,128)(2,1)S(1)}, u32[]{:S(2)}, u32[]{:S(2)}) %all-to-all-start.1) | async-done | bytes 1048608 | tf_op jit(solution)/shard_map/all_to_all | solution.py:26
  52.2 5.3 %collective-permute-start = (bf16[16,64,512]{2,1,0:T(8,128)(2,1)S(1)}, bf16[16,64,512]{2,1,0:T(8,128)(2,1)S(1)}, u32[]{:S(2)}, u32[]{:S(2)}) collective-permute-start(bf16[16,64,512]{2,1,0:T(8,128)(2,1)S(1)} %bitcast.16), channel_id=1, source_target_pairs={{0,8},{8,0},{1,9},{9,1},{2,10},{10,2},{3,11},{11,3},{4,12},{12,4},... | collective-permute-start | bytes 3145736 | tf_op jit(solution)/shard_map/ppermute | solution.py:352
  57.5 0.0 copy-start.1
  57.5 0.6 fusion.11.order_ref
  58.1 0.1 copy-done.1
  58.2 0.1 fusion.1.tex_ref
  58.4 0.1 reduce-precision_subtract_fusion
  58.5 0.0 collective-permute-done.1.came_ref
  58.5 0.8 first.1
  59.3 0.4 collective-permute-done.other_ref
  59.7 2.1 %second.1 = (bf16[4,24,768]{2,1,0:T(8,128)(2,1)S(1)}, bf16[8,4,512]{2,1,0:T(4,128)(2,1)S(1)}) custom-call(s32[1]{0:T(128)} %bitcast.1.zh_ref, bf16[16,64,512]{2,1,0:T(8,128)(2,1)S(1)} %bitcast.18, bf16[16,64,512]{2,1,0:T(8,128)(2,1)S(1)} %collective-permute-done.other_ref, f32[8,24,512]{2,1,0:T(8,128)S(1)} %get-tuple-element.15.part_ref, ...), custom_call_target="tpu_custom_call" | custom-call | flops 2000000000 | bytes 4000000 | tf_op jit(solution)/shard_map/second/pallas_call | solution.py:268
  61.9 7.3 %all_to_all.25 = bf16[4,24,768]{2,1,0:T(8,128)(2,1)S(1)} all-to-all(bf16[4,24,768]{2,1,0:T(8,128)(2,1)S(1)} %get-tuple-element.21), channel_id=1, replica_groups=mesh['x'=4,'zl'=8,'c'=2,'y'=4,'zh'=2] {'y'}, dimensions={0} | all-to-all | bytes 294912 | tf_op jit(solution)/shard_map/all_to_all | solution.py:26
  69.2 0.3 convolution_convert_fusion
  69.4 12.4 %all_to_all.26 = bf16[8,36,512]{2,1,0:T(8,128)(2,1)S(1)} all-to-all(bf16[8,36,512]{2,1,0:T(8,128)(2,1)S(1)} %pad_maximum_fusion), channel_id=1, replica_groups=mesh['x'=4,'zl'=8,'c'=2,'y'=4,'zh'=2] {'c','x'}, dimensions={0} | all-to-all | bytes 589824 | tf_op jit(solution)/shard_map/all_to_all | solution.py:26
  82.0 0.0 copy-start.2
  82.0 12.4 %all_to_all.27.sums_ref = bf16[8,8,512]{2,1,0:T(8,128)(2,1)S(1)} all-to-all(bf16[8,8,512]{2,1,0:T(8,128)(2,1)S(1)} %pad_maximum_fusion.1), channel_id=1, replica_groups=mesh['x'=4,'zl'=8,'c'=2,'y'=4,'zh'=2] {'zl'}, dimensions={0} | all-to-all | bytes 131072 | tf_op jit(solution)/shard_map/all_to_all | solution.py:26
  94.4 0.8 last.1
  (25 shorter events, 0.3 us)
Async XLA Ops:
  0.6 17.4 %copy-start = (bf16[24,20,151]{2,0,1:T(8,128)(2,1)S(1)}, bf16[24,20,151]{2,0,1:T(8,128)(2,1)}, u32[]{:S(2)}) copy-start(bf16[24,20,151]{2,0,1:T(8,128)(2,1)} %param.6) | copy-start | bytes 434884
  2.1 15.9 %copy-start.5 = (s32[20]{0:T(128)S(1)}, s32[20]{0:T(128)}, u32[]{:S(2)}) copy-start(s32[20]{0:T(128)} %param.7) | copy-start | bytes 244
  2.1 15.9 %copy-start.4 = (bf16[151,64]{0,1:T(8,128)(2,1)S(1)}, bf16[151,64]{0,1:T(8,128)(2,1)}, u32[]{:S(2)}) copy-start(bf16[151,64]{0,1:T(8,128)(2,1)} %param.10) | copy-start | bytes 57988
  2.1 27.4 %all-to-all-start = ((bf16[16,4,512]{2,1,0:T(4,128)(2,1)}), bf16[16,4,512]{2,1,0:T(4,128)(2,1)S(1)}, u32[]{:S(2)}, u32[]{:S(2)}) async-start(bf16[16,4,512]{2,1,0:T(4,128)(2,1)} %broadcast_in_dim.7), calls=%async_computation | async-start | bytes 131072 | tf_op jit(solution)/shard_map/all_to_all | solution.py:26
  18.3 0.7 copy-start.3
  30.7 21.4 %all-to-all-start.1 = ((bf16[16,2,32,512]{3,2,1,0:T(8,128)(2,1)}), bf16[16,2,32,512]{3,2,1,0:T(8,128)(2,1)S(1)}, u32[]{:S(2)}, u32[]{:S(2)}) async-start(bf16[16,2,32,512]{3,2,1,0:T(8,128)(2,1)} %copies.1), calls=%async_computation.1 | async-start | bytes 2097152 | tf_op jit(solution)/shard_map/all_to_all | solution.py:26
  37.6 20.9 %collective-permute-start.1 = (bf16[250,128]{1,0:T(8,128)(2,1)S(1)}, bf16[250,128]{1,0:T(8,128)(2,1)S(1)}, u32[]{:S(2)}, u32[]{:S(2)}) collective-permute-start(bf16[250,128]{1,0:T(8,128)(2,1)S(1)} %maximum_maximum_fusion.sent_ref), channel_id=1, source_target_pairs={{0,1},{1,0},{2,3},{3,2},{4,5},{5,4},{6,7},{7,6},{8,9},{9,8},{10,11... | collective-permute-start | bytes 192008 | tf_op jit(solution)/shard_map/ppermute | solution.py:343
  52.2 7.6 %collective-permute-start = (bf16[16,64,512]{2,1,0:T(8,128)(2,1)S(1)}, bf16[16,64,512]{2,1,0:T(8,128)(2,1)S(1)}, u32[]{:S(2)}, u32[]{:S(2)}) collective-permute-start(bf16[16,64,512]{2,1,0:T(8,128)(2,1)S(1)} %bitcast.16), channel_id=1, source_target_pairs={{0,8},{8,0},{1,9},{9,1},{2,10},{10,2},{3,11},{11,3},{4,12},{12,4},... | collective-permute-start | bytes 3145736 | tf_op jit(solution)/shard_map/ppermute | solution.py:352
  57.5 0.7 copy-start.1
  82.0 12.4 %copy-start.2 = (f32[4,8,64]{2,1,0:T(8,128)S(1)}, f32[4,8,64]{2,1,0:T(8,128)}, u32[]{:S(2)}) copy-start(f32[4,8,64]{2,1,0:T(8,128)} %core_ref.1) | copy-start | bytes 24580

commit v11 on v9

--- a/solution.py
+++ b/solution.py
@@ -344,8 +344,9 @@
     summed = blocks[:, :width].astype(BF16)
 
     core_part = jnp.einsum("ta,tn->an", tex_abs, summed, preferred_element_type=F32)
-    core_part = core_part.astype(BF16).reshape(nx * nc, near, width)
-    both = exchange(jnp.concatenate([core_part, view_part], axis=1), ("c", "x"))
+    core_part = core_part.astype(BF16).reshape(nc, nx, near, width)
+    core_part = jnp.transpose(core_part, (1, 0, 2, 3)).reshape(nx * nc, near, width)
+    both = exchange(jnp.concatenate([core_part, view_part], axis=1), ("x", "c"))
     core_part = sum_blocks(both[:, :near]).astype(BF16).reshape(nzl, core_rows, width)
     view_block = sum_blocks(both[:, near:]).astype(BF16)
     view_block = jnp.broadcast_to(view_block[None], (nzl, core_rows, width))

time: 95.8 us -> 95.7 us (level)
  no operation moved by 1% of the time
where the time goes in v11:
time: 95.7 us; the launch traced here: 95.1 us
  blocking collectives  32 us (33%)
  starting transfers between devices  31.6 us (33%)
  waiting for transfers between devices  21.7 us (23%)
  Pallas kernels  3.65 us (4%)
  local copies, waits for them, and re-layouts  2.64 us (3%)
  other arithmetic  1.86 us (2%)
    all_to_all x3, blocking collectives, exchange(): return lax.all_to_all(x, axes, 0, 0, tiled=True)  32 us
    all_to_all x2, starting transfers between devices, exchange(): return lax.all_to_all(x, axes, 0, 0, tiled=True)  22.6 us
    all_to_all x2, waiting for transfers between devices, exchange(): return lax.all_to_all(x, axes, 0, 0, tiled=True)  21.3 us
    ppermute x1, starting transfers between devices, per_device(): core_other = lax.ppermute(core_own, 'c', [(0, 1), (1, 0)])  5.3 us
    ppermute x1, starting transfers between devices, per_device(): came = lax.ppermute(sent, 'zh', [(0, 1), (1, 0)])  3.68 us
    pallas_call x1, Pallas kernels, middle(): pl.pallas_call(second_kernel, out_shape=(jax.ShapeDtypeStruct((ny, rows,...  2.12 us
  transfers between devices with their start and end apart: 4, of which 3 were waited for; matrix products, arithmetic and copies ran while one was open for 2% of the time, Pallas kernels for 1%

profile of v11, /device:TPU:1, one launch (start us, length us, event | category | flops | bytes accessed | tf_op | source)
XLA Modules:
  0.0 95.1 jit_solution(18069306414493630862)
XLA Ops:
  0.6 0.0 copy-start
  0.6 0.8 convert_element_type.39
  1.4 0.1 broadcast_in_dim.10
  1.5 0.6 broadcast_in_dim.11
  2.1 15.9 %all-to-all-start = ((bf16[16,4,512]{2,1,0:T(4,128)(2,1)}), bf16[16,4,512]{2,1,0:T(4,128)(2,1)S(1)}, u32[]{:S(2)}, u32[]{:S(2)}) async-start(bf16[16,4,512]{2,1,0:T(4,128)(2,1)} %broadcast_in_dim.11), calls=%async_computation | async-start | bytes 131072 | tf_op jit(solution)/shard_map/all_to_all | solution.py:26
  18.1 0.2 fusion
  18.3 0.0 copy-start.3
  18.3 0.1 pad_maximum_fusion.2
  18.4 0.6 copy-done.3
  19.0 0.1 multiply_convert_fusion
  19.1 10.5 %all-to-all-done = bf16[16,4,512]{2,1,0:T(4,128)(2,1)S(1)} async-done(((bf16[16,4,512]{2,1,0:T(4,128)(2,1)}), bf16[16,4,512]{2,1,0:T(4,128)(2,1)S(1)}, u32[]{:S(2)}, u32[]{:S(2)}) %all-to-all-start) | async-done | bytes 65568 | tf_op jit(solution)/shard_map/all_to_all | solution.py:26
  29.6 1.1 %broadcast_in_dim.25 = bf16[16,2,32,512]{3,2,1,0:T(8,128)(2,1)} broadcast(bf16[2,32,512]{2,1,0:T(8,128)(2,1)S(1)} %broadcast_in_dim.24), dimensions={1,2,3} | broadcast | bytes 1114112 | tf_op jit(solution)/shard_map/broadcast_in_dim | solution.py:31
  30.7 6.8 %all-to-all-start.1 = ((bf16[16,2,32,512]{3,2,1,0:T(8,128)(2,1)}), bf16[16,2,32,512]{3,2,1,0:T(8,128)(2,1)S(1)}, u32[]{:S(2)}, u32[]{:S(2)}) async-start(bf16[16,2,32,512]{3,2,1,0:T(8,128)(2,1)} %broadcast_in_dim.25), calls=%async_computation.1 | async-start | bytes 2097152 | tf_op jit(solution)/shard_map/all_to_all | solution.py:26
  37.5 0.1 maximum_maximum_fusion.sent_ref
  37.6 3.7 %collective-permute-start.1 = (bf16[250,128]{1,0:T(8,128)(2,1)S(1)}, bf16[250,128]{1,0:T(8,128)(2,1)S(1)}, u32[]{:S(2)}, u32[]{:S(2)}) collective-permute-start(bf16[250,128]{1,0:T(8,128)(2,1)S(1)} %maximum_maximum_fusion.sent_ref), channel_id=1, source_target_pairs={{0,1},{1,0},{2,3},{3,2},{4,5},{5,4},{6,7},{7,6},{8,9},{9,8},{10,11... | collective-permute-start | bytes 192008 | tf_op jit(solution)/shard_map/ppermute | solution.py:318
  41.3 10.8 %all-to-all-done.1 = bf16[16,2,32,512]{3,2,1,0:T(8,128)(2,1)S(1)} async-done(((bf16[16,2,32,512]{3,2,1,0:T(8,128)(2,1)}), bf16[16,2,32,512]{3,2,1,0:T(8,128)(2,1)S(1)}, u32[]{:S(2)}, u32[]{:S(2)}) %all-to-all-start.1) | async-done | bytes 1048608 | tf_op jit(solution)/shard_map/all_to_all | solution.py:26
  52.1 5.3 %collective-permute-start = (bf16[16,64,512]{2,1,0:T(8,128)(2,1)S(1)}, bf16[16,64,512]{2,1,0:T(8,128)(2,1)S(1)}, u32[]{:S(2)}, u32[]{:S(2)}) collective-permute-start(bf16[16,64,512]{2,1,0:T(8,128)(2,1)S(1)} %bitcast.19), channel_id=1, source_target_pairs={{0,8},{8,0},{1,9},{9,1},{2,10},{10,2},{3,11},{11,3},{4,12},{12,4},... | collective-permute-start | bytes 3145736 | tf_op jit(solution)/shard_map/ppermute | solution.py:327
  57.4 0.0 copy-start.1
  57.4 0.6 fusion.11.order_ref
  58.1 0.1 copy-done.1
  58.2 0.1 fusion.1.tex_ref
  58.3 0.1 reduce-precision_subtract_fusion
  58.5 0.0 collective-permute-done.1.came_ref
  58.5 0.8 first.1
  59.3 0.4 collective-permute-done.other_ref
  59.7 2.1 %second.1 = (bf16[4,24,768]{2,1,0:T(8,128)(2,1)S(1)}, bf16[8,4,512]{2,1,0:T(4,128)(2,1)S(1)}) custom-call(s32[1]{0:T(128)} %bitcast.1.zh_ref, bf16[16,64,512]{2,1,0:T(8,128)(2,1)S(1)} %bitcast.21, bf16[16,64,512]{2,1,0:T(8,128)(2,1)S(1)} %collective-permute-done.other_ref, f32[8,24,512]{2,1,0:T(8,128)S(1)} %get-tuple-element.15.part_ref, ...), custom_call_target="tpu_custom_call" | custom-call | flops 2000000000 | bytes 4000000 | tf_op jit(solution)/shard_map/second/pallas_call | solution.py:243
  61.8 7.3 %all_to_all.25 = bf16[4,24,768]{2,1,0:T(8,128)(2,1)S(1)} all-to-all(bf16[4,24,768]{2,1,0:T(8,128)(2,1)S(1)} %get-tuple-element.21), channel_id=1, replica_groups=mesh['x'=4,'zl'=8,'c'=2,'y'=4,'zh'=2] {'y'}, dimensions={0} | all-to-all | bytes 294912 | tf_op jit(solution)/shard_map/all_to_all | solution.py:26
  69.1 0.3 convolution_convert_fusion
  69.4 12.3 %all_to_all.26 = bf16[8,36,512]{2,1,0:T(8,128)(2,1)S(1)} all-to-all(bf16[8,36,512]{2,1,0:T(8,128)(2,1)S(1)} %pad_maximum_fusion), channel_id=1, replica_groups=mesh['x'=4,'zl'=8,'c'=2,'y'=4,'zh'=2] {'x','c'}, dimensions={0} | all-to-all | bytes 589824 | tf_op jit(solution)/shard_map/all_to_all | solution.py:26
  81.9 0.0 copy-start.2
  81.9 12.4 %all_to_all.27.sums_ref = bf16[8,8,512]{2,1,0:T(8,128)(2,1)S(1)} all-to-all(bf16[8,8,512]{2,1,0:T(8,128)(2,1)S(1)} %pad_maximum_fusion.1), channel_id=1, replica_groups=mesh['x'=4,'zl'=8,'c'=2,'y'=4,'zh'=2] {'zl'}, dimensions={0} | all-to-all | bytes 131072 | tf_op jit(solution)/shard_map/all_to_all | solution.py:26
  94.3 0.8 last.1
  (26 shorter events, 0.3 us)
Async XLA Ops:
  0.6 17.4 %copy-start = (bf16[24,20,151]{2,0,1:T(8,128)(2,1)S(1)}, bf16[24,20,151]{2,0,1:T(8,128)(2,1)}, u32[]{:S(2)}) copy-start(bf16[24,20,151]{2,0,1:T(8,128)(2,1)} %param.6) | copy-start | bytes 434884
  2.1 15.9 %copy-start.5 = (s32[20]{0:T(128)S(1)}, s32[20]{0:T(128)}, u32[]{:S(2)}) copy-start(s32[20]{0:T(128)} %param.7) | copy-start | bytes 244
  2.1 15.9 %copy-start.4 = (bf16[151,64]{0,1:T(8,128)(2,1)S(1)}, bf16[151,64]{0,1:T(8,128)(2,1)}, u32[]{:S(2)}) copy-start(bf16[151,64]{0,1:T(8,128)(2,1)} %param.10) | copy-start | bytes 57988
  2.1 27.4 %all-to-all-start = ((bf16[16,4,512]{2,1,0:T(4,128)(2,1)}), bf16[16,4,512]{2,1,0:T(4,128)(2,1)S(1)}, u32[]{:S(2)}, u32[]{:S(2)}) async-start(bf16[16,4,512]{2,1,0:T(4,128)(2,1)} %broadcast_in_dim.11), calls=%async_computation | async-start | bytes 131072 | tf_op jit(solution)/shard_map/all_to_all | solution.py:26
  18.3 0.7 copy-start.3
  30.7 21.4 %all-to-all-start.1 = ((bf16[16,2,32,512]{3,2,1,0:T(8,128)(2,1)}), bf16[16,2,32,512]{3,2,1,0:T(8,128)(2,1)S(1)}, u32[]{:S(2)}, u32[]{:S(2)}) async-start(bf16[16,2,32,512]{3,2,1,0:T(8,128)(2,1)} %broadcast_in_dim.25), calls=%async_computation.1 | async-start | bytes 2097152 | tf_op jit(solution)/shard_map/all_to_all | solution.py:26
  37.6 20.9 %collective-permute-start.1 = (bf16[250,128]{1,0:T(8,128)(2,1)S(1)}, bf16[250,128]{1,0:T(8,128)(2,1)S(1)}, u32[]{:S(2)}, u32[]{:S(2)}) collective-permute-start(bf16[250,128]{1,0:T(8,128)(2,1)S(1)} %maximum_maximum_fusion.sent_ref), channel_id=1, source_target_pairs={{0,1},{1,0},{2,3},{3,2},{4,5},{5,4},{6,7},{7,6},{8,9},{9,8},{10,11... | collective-permute-start | bytes 192008 | tf_op jit(solution)/shard_map/ppermute | solution.py:318
  52.1 7.6 %collective-permute-start = (bf16[16,64,512]{2,1,0:T(8,128)(2,1)S(1)}, bf16[16,64,512]{2,1,0:T(8,128)(2,1)S(1)}, u32[]{:S(2)}, u32[]{:S(2)}) collective-permute-start(bf16[16,64,512]{2,1,0:T(8,128)(2,1)S(1)} %bitcast.19), channel_id=1, source_target_pairs={{0,8},{8,0},{1,9},{9,1},{2,10},{10,2},{3,11},{11,3},{4,12},{12,4},... | collective-permute-start | bytes 3145736 | tf_op jit(solution)/shard_map/ppermute | solution.py:327
  57.4 0.7 copy-start.1
  81.9 12.4 %copy-start.2 = (f32[4,8,64]{2,1,0:T(8,128)S(1)}, f32[4,8,64]{2,1,0:T(8,128)}, u32[]{:S(2)}) copy-start(f32[4,8,64]{2,1,0:T(8,128)} %core_ref.1) | copy-start | bytes 24580

commit v12 on v11

--- a/solution.py
+++ b/solution.py
@@ -63,10 +63,10 @@
 
 
 def core_band(ref, g):
-    nx, ny, nzh = SIZES[0], SIZES[3], SIZES[4]
+    nx, nzh = SIZES[0], SIZES[4]
     near = ref.shape[1] // nzh
     y, z = g // nzh, g % nzh
-    return [ref[x * ny + y, z * near : (z + 1) * near, :] for x in range(nx)]
+    return [ref[y * nx + x, z * near : (z + 1) * near, :] for x in range(nx)]
 
 
 def spread(n):
@@ -323,7 +323,7 @@
     gram_high = lax.reduce_precision(gram, 8, 7)
     gram_low = gram - gram_high
 
-    core_own = gather_blocks(core_z, ("x", "y")).reshape(nx * ny, nzh * near, width)
+    core_own = gather_blocks(core_z, ("y", "x")).reshape(nx * ny, nzh * near, width)
     core_other = lax.ppermute(core_own, "c", [(0, 1), (1, 0)])
 
     tex_raw = tex_factor.astype(BF16)

time: 95.7 us -> 95.7 us (level)
  no operation moved by 1% of the time
where the time goes in v12:
time: 95.7 us; the launch traced here: 95.1 us
  starting transfers between devices  31.7 us (33%)
  blocking collectives  31.5 us (33%)
  waiting for transfers between devices  22.1 us (23%)
  Pallas kernels  3.65 us (4%)
  local copies, waits for them, and re-layouts  2.64 us (3%)
  other arithmetic  1.86 us (2%)
    all_to_all x3, blocking collectives, exchange(): return lax.all_to_all(x, axes, 0, 0, tiled=True)  31.5 us
    all_to_all x2, starting transfers between devices, exchange(): return lax.all_to_all(x, axes, 0, 0, tiled=True)  22.6 us
    all_to_all x2, waiting for transfers between devices, exchange(): return lax.all_to_all(x, axes, 0, 0, tiled=True)  21.6 us
    ppermute x1, starting transfers between devices, per_device(): core_other = lax.ppermute(core_own, 'c', [(0, 1), (1, 0)])  5.43 us
    ppermute x1, starting transfers between devices, per_device(): came = lax.ppermute(sent, 'zh', [(0, 1), (1, 0)])  3.68 us
    pallas_call x1, Pallas kernels, middle(): pl.pallas_call(second_kernel, out_shape=(jax.ShapeDtypeStruct((ny, rows,...  2.12 us
  transfers between devices with their start and end apart: 4, of which 3 were waited for; matrix products, arithmetic and copies ran while one was open for 2% of the time, Pallas kernels for 1%

profile of v12, /device:TPU:1, one launch (start us, length us, event | category | flops | bytes accessed | tf_op | source)
XLA Modules:
  0.0 95.1 jit_solution(7849965120242562554)
XLA Ops:
  0.6 0.0 copy-start
  0.6 0.8 convert_element_type.39
  1.4 0.1 broadcast_in_dim.10
  1.5 0.6 broadcast_in_dim.11
  2.1 15.9 %all-to-all-start = ((bf16[16,4,512]{2,1,0:T(4,128)(2,1)}), bf16[16,4,512]{2,1,0:T(4,128)(2,1)S(1)}, u32[]{:S(2)}, u32[]{:S(2)}) async-start(bf16[16,4,512]{2,1,0:T(4,128)(2,1)} %broadcast_in_dim.11), calls=%async_computation | async-start | bytes 131072 | tf_op jit(solution)/shard_map/all_to_all | solution.py:26
  18.1 0.2 fusion
  18.3 0.0 copy-start.3
  18.3 0.1 pad_maximum_fusion.2
  18.4 0.6 copy-done.3
  19.0 0.1 multiply_convert_fusion
  19.1 10.5 %all-to-all-done = bf16[16,4,512]{2,1,0:T(4,128)(2,1)S(1)} async-done(((bf16[16,4,512]{2,1,0:T(4,128)(2,1)}), bf16[16,4,512]{2,1,0:T(4,128)(2,1)S(1)}, u32[]{:S(2)}, u32[]{:S(2)}) %all-to-all-start) | async-done | bytes 65568 | tf_op jit(solution)/shard_map/all_to_all | solution.py:26
  29.6 1.1 %broadcast_in_dim.25 = bf16[16,2,32,512]{3,2,1,0:T(8,128)(2,1)} broadcast(bf16[2,32,512]{2,1,0:T(8,128)(2,1)S(1)} %broadcast_in_dim.24), dimensions={1,2,3} | broadcast | bytes 1114112 | tf_op jit(solution)/shard_map/broadcast_in_dim | solution.py:31
  30.7 6.8 %all-to-all-start.1 = ((bf16[16,2,32,512]{3,2,1,0:T(8,128)(2,1)}), bf16[16,2,32,512]{3,2,1,0:T(8,128)(2,1)S(1)}, u32[]{:S(2)}, u32[]{:S(2)}) async-start(bf16[16,2,32,512]{3,2,1,0:T(8,128)(2,1)} %broadcast_in_dim.25), calls=%async_computation.1 | async-start | bytes 2097152 | tf_op jit(solution)/shard_map/all_to_all | solution.py:26
  37.5 0.1 maximum_maximum_fusion.sent_ref
  37.6 3.7 %collective-permute-start.1 = (bf16[250,128]{1,0:T(8,128)(2,1)S(1)}, bf16[250,128]{1,0:T(8,128)(2,1)S(1)}, u32[]{:S(2)}, u32[]{:S(2)}) collective-permute-start(bf16[250,128]{1,0:T(8,128)(2,1)S(1)} %maximum_maximum_fusion.sent_ref), channel_id=1, source_target_pairs={{0,1},{1,0},{2,3},{3,2},{4,5},{5,4},{6,7},{7,6},{8,9},{9,8},{10,11... | collective-permute-start | bytes 192008 | tf_op jit(solution)/shard_map/ppermute | solution.py:318
  41.3 11.1 %all-to-all-done.1 = bf16[16,2,32,512]{3,2,1,0:T(8,128)(2,1)S(1)} async-done(((bf16[16,2,32,512]{3,2,1,0:T(8,128)(2,1)}), bf16[16,2,32,512]{3,2,1,0:T(8,128)(2,1)S(1)}, u32[]{:S(2)}, u32[]{:S(2)}) %all-to-all-start.1) | async-done | bytes 1048608 | tf_op jit(solution)/shard_map/all_to_all | solution.py:26
  52.4 5.4 %collective-permute-start = (bf16[16,64,512]{2,1,0:T(8,128)(2,1)S(1)}, bf16[16,64,512]{2,1,0:T(8,128)(2,1)S(1)}, u32[]{:S(2)}, u32[]{:S(2)}) collective-permute-start(bf16[16,64,512]{2,1,0:T(8,128)(2,1)S(1)} %bitcast.19), channel_id=1, source_target_pairs={{0,8},{8,0},{1,9},{9,1},{2,10},{10,2},{3,11},{11,3},{4,12},{12,4},... | collective-permute-start | bytes 3145736 | tf_op jit(solution)/shard_map/ppermute | solution.py:327
  57.9 0.0 copy-start.1
  57.9 0.6 fusion.11.order_ref
  58.5 0.1 copy-done.1
  58.6 0.1 fusion.1.tex_ref
  58.8 0.1 reduce-precision_subtract_fusion
  58.9 0.0 collective-permute-done.1.came_ref
  58.9 0.8 first.1
  59.7 0.4 collective-permute-done.other_ref
  60.1 2.1 %second.1 = (bf16[4,24,768]{2,1,0:T(8,128)(2,1)S(1)}, bf16[8,4,512]{2,1,0:T(4,128)(2,1)S(1)}) custom-call(s32[1]{0:T(128)} %bitcast.1.zh_ref, bf16[16,64,512]{2,1,0:T(8,128)(2,1)S(1)} %bitcast.21, bf16[16,64,512]{2,1,0:T(8,128)(2,1)S(1)} %collective-permute-done.other_ref, f32[8,24,512]{2,1,0:T(8,128)S(1)} %get-tuple-element.15.part_ref, ...), custom_call_target="tpu_custom_call" | custom-call | flops 2000000000 | bytes 4000000 | tf_op jit(solution)/shard_map/second/pallas_call | solution.py:243
  62.3 7.3 %all_to_all.25 = bf16[4,24,768]{2,1,0:T(8,128)(2,1)S(1)} all-to-all(bf16[4,24,768]{2,1,0:T(8,128)(2,1)S(1)} %get-tuple-element.21), channel_id=1, replica_groups=mesh['x'=4,'zl'=8,'c'=2,'y'=4,'zh'=2] {'y'}, dimensions={0} | all-to-all | bytes 294912 | tf_op jit(solution)/shard_map/all_to_all | solution.py:26
  69.6 0.3 convolution_convert_fusion
  69.9 11.9 %all_to_all.26 = bf16[8,36,512]{2,1,0:T(8,128)(2,1)S(1)} all-to-all(bf16[8,36,512]{2,1,0:T(8,128)(2,1)S(1)} %pad_maximum_fusion), channel_id=1, replica_groups=mesh['x'=4,'zl'=8,'c'=2,'y'=4,'zh'=2] {'x','c'}, dimensions={0} | all-to-all | bytes 589824 | tf_op jit(solution)/shard_map/all_to_all | solution.py:26
  81.9 0.0 copy-start.2
  81.9 12.4 %all_to_all.27.sums_ref = bf16[8,8,512]{2,1,0:T(8,128)(2,1)S(1)} all-to-all(bf16[8,8,512]{2,1,0:T(8,128)(2,1)S(1)} %pad_maximum_fusion.1), channel_id=1, replica_groups=mesh['x'=4,'zl'=8,'c'=2,'y'=4,'zh'=2] {'zl'}, dimensions={0} | all-to-all | bytes 131072 | tf_op jit(solution)/shard_map/all_to_all | solution.py:26
  94.3 0.8 last.1
  (26 shorter events, 0.3 us)
Async XLA Ops:
  0.6 17.4 %copy-start = (bf16[24,20,151]{2,0,1:T(8,128)(2,1)S(1)}, bf16[24,20,151]{2,0,1:T(8,128)(2,1)}, u32[]{:S(2)}) copy-start(bf16[24,20,151]{2,0,1:T(8,128)(2,1)} %param.6) | copy-start | bytes 434884
  2.1 15.9 %copy-start.5 = (s32[20]{0:T(128)S(1)}, s32[20]{0:T(128)}, u32[]{:S(2)}) copy-start(s32[20]{0:T(128)} %param.7) | copy-start | bytes 244
  2.1 15.9 %copy-start.4 = (bf16[151,64]{0,1:T(8,128)(2,1)S(1)}, bf16[151,64]{0,1:T(8,128)(2,1)}, u32[]{:S(2)}) copy-start(bf16[151,64]{0,1:T(8,128)(2,1)} %param.10) | copy-start | bytes 57988
  2.1 27.4 %all-to-all-start = ((bf16[16,4,512]{2,1,0:T(4,128)(2,1)}), bf16[16,4,512]{2,1,0:T(4,128)(2,1)S(1)}, u32[]{:S(2)}, u32[]{:S(2)}) async-start(bf16[16,4,512]{2,1,0:T(4,128)(2,1)} %broadcast_in_dim.11), calls=%async_computation | async-start | bytes 131072 | tf_op jit(solution)/shard_map/all_to_all | solution.py:26
  18.3 0.7 copy-start.3
  30.7 21.7 %all-to-all-start.1 = ((bf16[16,2,32,512]{3,2,1,0:T(8,128)(2,1)}), bf16[16,2,32,512]{3,2,1,0:T(8,128)(2,1)S(1)}, u32[]{:S(2)}, u32[]{:S(2)}) async-start(bf16[16,2,32,512]{3,2,1,0:T(8,128)(2,1)} %broadcast_in_dim.25), calls=%async_computation.1 | async-start | bytes 2097152 | tf_op jit(solution)/shard_map/all_to_all | solution.py:26
  37.6 21.4 %collective-permute-start.1 = (bf16[250,128]{1,0:T(8,128)(2,1)S(1)}, bf16[250,128]{1,0:T(8,128)(2,1)S(1)}, u32[]{:S(2)}, u32[]{:S(2)}) collective-permute-start(bf16[250,128]{1,0:T(8,128)(2,1)S(1)} %maximum_maximum_fusion.sent_ref), channel_id=1, source_target_pairs={{0,1},{1,0},{2,3},{3,2},{4,5},{5,4},{6,7},{7,6},{8,9},{9,8},{10,11... | collective-permute-start | bytes 192008 | tf_op jit(solution)/shard_map/ppermute | solution.py:318
  52.4 7.7 %collective-permute-start = (bf16[16,64,512]{2,1,0:T(8,128)(2,1)S(1)}, bf16[16,64,512]{2,1,0:T(8,128)(2,1)S(1)}, u32[]{:S(2)}, u32[]{:S(2)}) collective-permute-start(bf16[16,64,512]{2,1,0:T(8,128)(2,1)S(1)} %bitcast.19), channel_id=1, source_target_pairs={{0,8},{8,0},{1,9},{9,1},{2,10},{10,2},{3,11},{11,3},{4,12},{12,4},... | collective-permute-start | bytes 3145736 | tf_op jit(solution)/shard_map/ppermute | solution.py:327
  57.9 0.7 copy-start.1
  81.9 12.4 %copy-start.2 = (f32[4,8,64]{2,1,0:T(8,128)S(1)}, f32[4,8,64]{2,1,0:T(8,128)}, u32[]{:S(2)}) copy-start(f32[4,8,64]{2,1,0:T(8,128)} %core_ref.1) | copy-start | bytes 24580

commit v13 on v11

--- a/solution.py
+++ b/solution.py
@@ -324,7 +324,6 @@
     gram_low = gram - gram_high
 
     core_own = gather_blocks(core_z, ("x", "y")).reshape(nx * ny, nzh * near, width)
-    core_other = lax.ppermute(core_own, "c", [(0, 1), (1, 0)])
 
     tex_raw = tex_factor.astype(BF16)
     order = lax.optimization_barrier(column_order(lax.axis_index("c")))
@@ -335,7 +334,10 @@
         tex_rel,
         jnp.concatenate([tex_rel[:, half:], tex_rel[:, :half]], axis=1),
     )
-    tex_rel, tex_abs = lax.optimization_barrier((tex_rel, tex_abs))
+    core_own, order, tex_rel, tex_abs, gram_high, gram_low = lax.optimization_barrier(
+        (core_own, order, tex_rel, tex_abs, gram_high, gram_low)
+    )
+    core_other = lax.ppermute(core_own, "c", [(0, 1), (1, 0)])
 
     blocks, view_part = middle(
         zh, core_own, core_other, tex_rel, order, sent, came, gram_high, gram_low, core_rows

time: 95.7 us -> 113 us (1.18)
  waiting for transfers between devices: 21.7 us -> 35.1 us
  blocking collectives: 32 us -> 35 us
  local copies, waits for them, and re-layouts: 2.64 us -> 3.97 us
    ppermute x1, waiting for transfers between devices: 0.01 us -> 11.5 us  [per_device(): came = lax.ppermute(sent, 'zh', [(0, 1), (1, 0)])]
    all_to_all x3, blocking collectives: 32 us -> 35 us  [exchange(): return lax.all_to_all(x, axes, 0, 0, tiled=True)]
    all_to_all x2, waiting for transfers between devices: 21.3 us -> 23.6 us  [exchange(): return lax.all_to_all(x, axes, 0, 0, tiled=True)]
    unnamed x12, local copies, waits for them, and re-layouts: 0.71 us -> 2.05 us
  transfers between devices with their start and end apart: 4 -> 4, of which waited for: 3 -> 3; matrix products, arithmetic and copies ran while one was open for 2% -> 1% of each run, Pallas kernels for 1% -> 1%
where the time goes in v13:
time: 113 us
  waiting for transfers between devices  35.1 us (31%)
  blocking collectives  35 us (31%)
  starting transfers between devices  31.6 us (28%)
  local copies, waits for them, and re-layouts  3.97 us (4%)
  Pallas kernels  3.65 us (3%)
  other arithmetic  1.85 us (2%)
    all_to_all x3, blocking collectives, exchange(): return lax.all_to_all(x, axes, 0, 0, tiled=True)  35 us
    all_to_all x2, waiting for transfers between devices, exchange(): return lax.all_to_all(x, axes, 0, 0, tiled=True)  23.6 us
    all_to_all x2, starting transfers between devices, exchange(): return lax.all_to_all(x, axes, 0, 0, tiled=True)  22.6 us
    ppermute x1, waiting for transfers between devices, per_device(): came = lax.ppermute(sent, 'zh', [(0, 1), (1, 0)])  11.5 us
    ppermute x1, starting transfers between devices, per_device(): core_other = lax.ppermute(core_own, 'c', [(0, 1), (1, 0)])  5.3 us
    ppermute x1, starting transfers between devices, per_device(): came = lax.ppermute(sent, 'zh', [(0, 1), (1, 0)])  3.69 us
  transfers between devices with their start and end apart: 4, of which 3 were waited for; matrix products, arithmetic and copies ran while one was open for 1% of the time, Pallas kernels for 1%

profile of v13, /device:TPU:1, one launch (start us, length us, event | category | flops | bytes accessed | tf_op | source)
XLA Modules:
  0.0 112.8 jit_solution(9803453906724109400)
XLA Ops:
  0.6 0.0 copy-start
  0.6 0.8 convert_element_type.35
  1.4 0.1 broadcast_in_dim.10
  1.5 0.6 broadcast_in_dim.11
  2.1 15.7 %all-to-all-start = ((bf16[16,4,512]{2,1,0:T(4,128)(2,1)}), bf16[16,4,512]{2,1,0:T(4,128)(2,1)S(1)}, u32[]{:S(2)}, u32[]{:S(2)}) async-start(bf16[16,4,512]{2,1,0:T(4,128)(2,1)} %broadcast_in_dim.11), calls=%async_computation | async-start | bytes 131072 | tf_op jit(solution)/shard_map/all_to_all | solution.py:26
  18.0 0.6 fusion.11.order_ref
  18.6 10.8 %all-to-all-done = bf16[16,4,512]{2,1,0:T(4,128)(2,1)S(1)} async-done(((bf16[16,4,512]{2,1,0:T(4,128)(2,1)}), bf16[16,4,512]{2,1,0:T(4,128)(2,1)S(1)}, u32[]{:S(2)}, u32[]{:S(2)}) %all-to-all-start) | async-done | bytes 65568 | tf_op jit(solution)/shard_map/all_to_all | solution.py:26
  29.5 1.1 broadcast_in_dim.25
  30.6 6.9 %all-to-all-start.1 = ((bf16[16,2,32,512]{3,2,1,0:T(8,128)(2,1)}), bf16[16,2,32,512]{3,2,1,0:T(8,128)(2,1)S(1)}, u32[]{:S(2)}, u32[]{:S(2)}) async-start(bf16[16,2,32,512]{3,2,1,0:T(8,128)(2,1)} %broadcast_in_dim.25), calls=%async_computation.1 | async-start | bytes 2097152 | tf_op jit(solution)/shard_map/all_to_all | solution.py:26
  37.5 0.1 fusion.1.tex_ref
  37.6 0.7 copy-done.5
  38.3 0.7 copy-done.4
  39.0 0.1 reduce-precision_subtract_fusion
  39.2 0.0 copy-done
  39.2 0.2 fusion
  39.4 12.7 %all-to-all-done.1 = bf16[16,2,32,512]{3,2,1,0:T(8,128)(2,1)S(1)} async-done(((bf16[16,2,32,512]{3,2,1,0:T(8,128)(2,1)}), bf16[16,2,32,512]{3,2,1,0:T(8,128)(2,1)S(1)}, u32[]{:S(2)}, u32[]{:S(2)}) %all-to-all-start.1) | async-done | bytes 1048608 | tf_op jit(solution)/shard_map/all_to_all | solution.py:26
  52.1 5.3 %collective-permute-start = (bf16[16,64,512]{2,1,0:T(8,128)(2,1)S(1)}, bf16[16,64,512]{2,1,0:T(8,128)(2,1)S(1)}, u32[]{:S(2)}, u32[]{:S(2)}) collective-permute-start(bf16[16,64,512]{2,1,0:T(8,128)(2,1)S(1)} %bitcast.19), channel_id=1, source_target_pairs={{0,8},{8,0},{1,9},{9,1},{2,10},{10,2},{3,11},{11,3},{4,12},{12,4},... | collective-permute-start | bytes 3145736 | tf_op jit(solution)/shard_map/ppermute | solution.py:340
  57.5 0.0 copy-start.3
  57.5 0.1 pad_maximum_fusion.2
  57.6 0.6 copy-done.3
  58.2 0.1 multiply_convert_fusion
  58.2 0.1 maximum_maximum_fusion.sent_ref
  58.3 3.7 %collective-permute-start.1 = (bf16[250,128]{1,0:T(8,128)(2,1)S(1)}, bf16[250,128]{1,0:T(8,128)(2,1)S(1)}, u32[]{:S(2)}, u32[]{:S(2)}) collective-permute-start(bf16[250,128]{1,0:T(8,128)(2,1)S(1)} %maximum_maximum_fusion.sent_ref), channel_id=1, source_target_pairs={{0,1},{1,0},{2,3},{3,2},{4,5},{5,4},{6,7},{7,6},{8,9},{9,8},{10,11... | collective-permute-start | bytes 192008 | tf_op jit(solution)/shard_map/ppermute | solution.py:318
  62.0 11.5 %collective-permute-done.1.came_ref = bf16[250,128]{1,0:T(8,128)(2,1)S(1)} collective-permute-done((bf16[250,128]{1,0:T(8,128)(2,1)S(1)}, bf16[250,128]{1,0:T(8,128)(2,1)S(1)}, u32[]{:S(2)}, u32[]{:S(2)}) %collective-permute-start.1) | collective-permute-done | bytes 64032 | tf_op jit(solution)/shard_map/ppermute | solution.py:318
  73.6 0.8 first.1
  74.3 2.1 %second.1 = (bf16[4,24,768]{2,1,0:T(8,128)(2,1)S(1)}, bf16[8,4,512]{2,1,0:T(4,128)(2,1)S(1)}) custom-call(s32[1]{0:T(128)} %bitcast.2.zh_ref, bf16[16,64,512]{2,1,0:T(8,128)(2,1)S(1)} %bitcast.21, bf16[16,64,512]{2,1,0:T(8,128)(2,1)S(1)} %collective-permute-done.other_ref, f32[8,24,512]{2,1,0:T(8,128)S(1)} %get-tuple-element.22.part_ref, ...), custom_call_target="tpu_custom_call" | custom-call | flops 2000000000 | bytes 4000000 | tf_op jit(solution)/shard_map/second/pallas_call | solution.py:243
  76.5 7.3 %all_to_all.25 = bf16[4,24,768]{2,1,0:T(8,128)(2,1)S(1)} all-to-all(bf16[4,24,768]{2,1,0:T(8,128)(2,1)S(1)} %get-tuple-element.29), channel_id=1, replica_groups=mesh['x'=4,'zl'=8,'c'=2,'y'=4,'zh'=2] {'y'}, dimensions={0} | all-to-all | bytes 294912 | tf_op jit(solution)/shard_map/all_to_all | solution.py:26
  83.7 0.3 convolution_convert_fusion
  84.1 12.1 %all_to_all.26 = bf16[8,36,512]{2,1,0:T(8,128)(2,1)S(1)} all-to-all(bf16[8,36,512]{2,1,0:T(8,128)(2,1)S(1)} %pad_maximum_fusion), channel_id=1, replica_groups=mesh['x'=4,'zl'=8,'c'=2,'y'=4,'zh'=2] {'x','c'}, dimensions={0} | all-to-all | bytes 589824 | tf_op jit(solution)/shard_map/all_to_all | solution.py:26
  96.3 0.0 copy-start.2
  96.3 15.7 %all_to_all.27.sums_ref = bf16[8,8,512]{2,1,0:T(8,128)(2,1)S(1)} all-to-all(bf16[8,8,512]{2,1,0:T(8,128)(2,1)S(1)} %pad_maximum_fusion.1), channel_id=1, replica_groups=mesh['x'=4,'zl'=8,'c'=2,'y'=4,'zh'=2] {'zl'}, dimensions={0} | all-to-all | bytes 131072 | tf_op jit(solution)/shard_map/all_to_all | solution.py:26
  112.0 0.8 last.1
  (26 shorter events, 0.3 us)
Async XLA Ops:
  0.6 38.6 %copy-start = (bf16[24,20,151]{2,0,1:T(8,128)(2,1)S(1)}, bf16[24,20,151]{2,0,1:T(8,128)(2,1)}, u32[]{:S(2)}) copy-start(bf16[24,20,151]{2,0,1:T(8,128)(2,1)} %param.6) | copy-start | bytes 434884
  2.1 27.3 %all-to-all-start = ((bf16[16,4,512]{2,1,0:T(4,128)(2,1)}), bf16[16,4,512]{2,1,0:T(4,128)(2,1)S(1)}, u32[]{:S(2)}, u32[]{:S(2)}) async-start(bf16[16,4,512]{2,1,0:T(4,128)(2,1)} %broadcast_in_dim.11), calls=%async_computation | async-start | bytes 131072 | tf_op jit(solution)/shard_map/all_to_all | solution.py:26
  30.6 6.9 %copy-start.1 = (f32[24,256]{1,0:T(8,128)S(1)}, f32[24,256]{1,0:T(8,128)}, u32[]{:S(2)}) copy-start(f32[24,256]{1,0:T(8,128)} %tex_ref.1) | copy-start | bytes 73732
  30.6 21.6 %all-to-all-start.1 = ((bf16[16,2,32,512]{3,2,1,0:T(8,128)(2,1)}), bf16[16,2,32,512]{3,2,1,0:T(8,128)(2,1)S(1)}, u32[]{:S(2)}, u32[]{:S(2)}) async-start(bf16[16,2,32,512]{3,2,1,0:T(8,128)(2,1)} %broadcast_in_dim.25), calls=%async_computation.1 | async-start | bytes 2097152 | tf_op jit(solution)/shard_map/all_to_all | solution.py:26
  37.6 0.7 copy-start.5
  38.3 0.8 copy-start.4
  52.1 22.2 %collective-permute-start = (bf16[16,64,512]{2,1,0:T(8,128)(2,1)S(1)}, bf16[16,64,512]{2,1,0:T(8,128)(2,1)S(1)}, u32[]{:S(2)}, u32[]{:S(2)}) collective-permute-start(bf16[16,64,512]{2,1,0:T(8,128)(2,1)S(1)} %bitcast.19), channel_id=1, source_target_pairs={{0,8},{8,0},{1,9},{9,1},{2,10},{10,2},{3,11},{11,3},{4,12},{12,4},... | collective-permute-start | bytes 3145736 | tf_op jit(solution)/shard_map/ppermute | solution.py:340
  57.5 0.7 copy-start.3
  58.3 15.2 %collective-permute-start.1 = (bf16[250,128]{1,0:T(8,128)(2,1)S(1)}, bf16[250,128]{1,0:T(8,128)(2,1)S(1)}, u32[]{:S(2)}, u32[]{:S(2)}) collective-permute-start(bf16[250,128]{1,0:T(8,128)(2,1)S(1)} %maximum_maximum_fusion.sent_ref), channel_id=1, source_target_pairs={{0,1},{1,0},{2,3},{3,2},{4,5},{5,4},{6,7},{7,6},{8,9},{9,8},{10,11... | collective-permute-start | bytes 192008 | tf_op jit(solution)/shard_map/ppermute | solution.py:318
  96.3 15.7 %copy-start.2 = (f32[4,8,64]{2,1,0:T(8,128)S(1)}, f32[4,8,64]{2,1,0:T(8,128)}, u32[]{:S(2)}) copy-start(f32[4,8,64]{2,1,0:T(8,128)} %core_ref.1) | copy-start | bytes 24580
